TPU v7x, 32 devices: a whole 2x2x4 slice. The times are simulated.
32 devices in a mesh: dp: 8 (over y, x, core), tensor: 4 (over z).
Axes of the slice: x: 2, y: 2, z: 4, core: 2. Of those that a mesh axis runs over, the one named last changes fastest.
Arguments:
- hidden_in: bfloat16 [8, 512, 2048], P(None, 'dp'), may hold values from -6 to 6
- layer_inputs: bfloat16 [8, 512, 256], P(None, 'dp'), may hold values from -6 to 6
- out_grad: bfloat16 [8, 512, 2048], P(None, 'dp'), may hold values from -6 to 6
- lengths: int32 [3], replicated, may hold values from 1024 to 2048, as said below
- order: int32 [3], replicated, may hold values from 0 to 2, each once
- w_query: bfloat16 [2048, 2048], P('dp', 'tensor'), may hold values from -0.125 to 0.125
- w_keyval: bfloat16 [2, 2048, 512], P(None, 'dp'), may hold values from -0.125 to 0.125
- w_out: bfloat16 [2048, 2048], P('tensor', 'dp'), may hold values from -0.125 to 0.125
- w_left: bfloat16 [2048, 64], P('dp'), may hold values from -0.125 to 0.125
- w_right: bfloat16 [64, 2048], P(None, 'dp'), may hold values from -0.75 to 0.75
- w_gateup: bfloat16 [2, 2048, 8192], P(None, 'dp', 'tensor'), may hold values from -0.125 to 0.125
- w_down: bfloat16 [8192, 2048], P('tensor', 'dp'), may hold values from -0.0625 to 0.0625
- w_pergate: bfloat16 [2048, 256], P('dp'), may hold values from -0.125 to 0.125
- w_perproj: bfloat16 [256, 2048], P(None, 'dp'), may hold values from -0.375 to 0.375
- gains: float32 [6, 2048], P(None, 'dp'), may hold values from 0.5 to 1.5
- head_gains: float32 [2, 256], replicated, may hold values from 0.25 to 0.45
Outputs:
- output: bfloat16 [8, 512, 2048], P(None, 'dp')
- input_grad: bfloat16 [8, 512, 2048], P(None, 'dp')
- layer_grad: bfloat16 [8, 512, 256], P(None, 'dp')
- grad_query: float32 [2048, 2048], P('dp', 'tensor')
- grad_keyval: float32 [2, 2048, 512], P(None, 'dp')
- grad_out: float32 [2048, 2048], P('tensor', 'dp')
- grad_left: float32 [2048, 64], P('dp')
- grad_right: float32 [64, 2048], P(None, 'dp')
- grad_gateup: float32 [2, 2048, 8192], P(None, 'dp', 'tensor')
- grad_down: float32 [8192, 2048], P('tensor', 'dp')
- grad_pergate: float32 [2048, 256], P('dp')
- grad_perproj: float32 [256, 2048], P(None, 'dp')
- grad_gains: float32 [6, 2048], P(None, 'dp')
- grad_head_gains: float32 [2, 256], replicated
Inputs may be any that keep to these rules, and one draw needn't show every extreme that they name: 3 lengths of 1024 to 2048 tokens that sum to 4096; one is 2048. `order`: each of 0 to 2 once.
All inputs are finite; a program needn't handle non-finite values.
Results may differ from a plain program's by a relative error of at most 0.04.
Values may be sent and summed in bfloat16 or wider, within the bound.
No kernel may reach another device: no remote copies, remote signals or barrier semaphores. Data moves between devices by JAX's collectives and lax.ppermute only.
A program may use at most 256 MiB of HBM per device.

v0:
```python
import jax
import jax.numpy as jnp
from jax import lax
from jax.sharding import PartitionSpec as P

KVH = 2
HD = 256
WIN = 512
LMIN = 1024


half_root = 0.7071067811865476
masked_value = -1e30


def passed_along(shard, axis, by):
    length = lax.axis_size(axis)
    pairs = [(i, i + by) for i in range(length) if 0 <= i + by < length]
    return lax.ppermute(shard, axis, pairs)


def shortened(shard):

    def short(part):
        return part.astype(jnp.bfloat16) if part.dtype == jnp.float32 else part

    return jax.tree.map(short, shard)


def normed(values_in, gain_vec):
    norm_scale = lax.rsqrt(jnp.mean(values_in * values_in, axis=-1, keepdims=True) + 1e-06)
    return values_in * norm_scale * gain_vec


def rotate(values_in, angles):
    half_dim = values_in.shape[-1] // 2
    first_half = values_in[..., :half_dim]
    second_half = values_in[..., half_dim:]
    cosine = jnp.cos(angles)
    sine_part = jnp.sin(angles)
    return jnp.concatenate(
        [
            first_half * cosine - second_half * sine_part,
            second_half * cosine + first_half * sine_part,
        ],
        axis=-1,
    )


def gelu_tanh(values_in):
    return jax.nn.gelu(values_in, approximate=True)


def glu_pair(gate_raw, upward):
    return gelu_tanh(gate_raw) * upward


def value_map(raw_value):
    return normed(raw_value, 1.0)


def product(left_mat, right_mat):
    return jnp.dot(left_mat, right_mat, preferred_element_type=jnp.float32)


def against(left_mat, right_mat):
    return lax.dot_general(
        left_mat, right_mat, (((1,), (1,)), ((), ())), preferred_element_type=jnp.float32
    )


def across(left_mat, right_mat):
    return lax.dot_general(
        left_mat, right_mat, (((0,), (0,)), ((), ())), preferred_element_type=jnp.float32
    )


def frequencies():
    half_dim = HD // 2
    return jnp.power(10000.0, -2.0 * jnp.arange(half_dim, dtype=jnp.float32) / HD)


def layout(lengths, order, my_index, devices, tok_dev):
    block_rows = tok_dev // devices
    capacity = (tok_dev // LMIN + 2) * block_rows
    seq_count = lengths.shape[0]
    given_len = jnp.take(lengths, order)
    given_start = jnp.cumsum(given_len) - given_len
    dealt_start = jnp.cumsum(lengths) - lengths
    local_rows = jnp.arange(tok_dev, dtype=jnp.int32)
    stream = local_rows // block_rows * tok_dev + my_index * block_rows + local_rows % block_rows
    arrival = jnp.sum((stream[:, None] >= given_start[None, 1:]).astype(jnp.int32), axis=1)
    dealt_pos = (
        jnp.take(dealt_start, jnp.take(order, arrival)) + stream - jnp.take(given_start, arrival)
    )
    target = dealt_pos // tok_dev
    before_mask = (local_rows[None, :] < local_rows[:, None]) & (target[None, :] == target[:, None])
    send_slot = target * capacity + jnp.sum(before_mask.astype(jnp.int32), axis=1)
    place_rows = my_index * tok_dev - WIN + jnp.arange(tok_dev + WIN, dtype=jnp.int32)
    dealt_seq = jnp.sum((place_rows[:, None] >= dealt_start[None, 1:]).astype(jnp.int32), axis=1)
    ext_pos = place_rows - jnp.take(dealt_start, dealt_seq)
    ext_seg = jnp.where(place_rows >= 0, dealt_seq, -1)
    own_seq = dealt_seq[WIN:]
    seq_ids = jnp.arange(seq_count, dtype=jnp.int32)
    arrived = jnp.sum(jnp.where(order[None, :] == own_seq[:, None], seq_ids[None, :], 0), axis=1)
    anchor = jnp.take(given_start, arrived) + place_rows[WIN:] - jnp.take(dealt_start, own_seq)
    source = anchor % tok_dev // block_rows
    prior_mask = (anchor[None, :] < anchor[:, None]) & (source[None, :] == source[:, None])
    recv_slot = source * capacity + jnp.sum(prior_mask.astype(jnp.int32), axis=1)
    return (send_slot, recv_slot, ext_seg, ext_pos, devices * capacity)


def pack(rows_in, slots, total_rows):
    row_count = rows_in.shape[0]
    index = (
        jnp.full((total_rows,), row_count, jnp.int32)
        .at[slots]
        .set(jnp.arange(row_count, dtype=jnp.int32))
    )
    return jnp.take(rows_in, index, axis=0, mode="fill", fill_value=0)


def attention_scores(queries, ext_keys, ext_seg, ext_pos, offset):
    query_block = lax.dynamic_slice_in_dim(queries, offset, WIN, 0)
    key_block = lax.dynamic_slice_in_dim(ext_keys, offset, 2 * WIN, 0)
    seg_query = lax.dynamic_slice_in_dim(ext_seg, offset + WIN, WIN, 0)
    pos_query = lax.dynamic_slice_in_dim(ext_pos, offset + WIN, WIN, 0)
    scores = jnp.einsum("qhd,kd->hqk", query_block, key_block, preferred_element_type=jnp.float32)
    gap = pos_query[:, None] - ext_pos[None, :]
    allowed = (seg_query[:, None] == ext_seg[None, :]) & (gap >= 0) & (gap < WIN)
    return (jnp.where(allowed[None], scores, masked_value), query_block, key_block)


def attend_forward(queries, ext_keys, ext_vals, ext_seg, ext_pos):
    row_count = queries.shape[0]
    blocks = row_count // WIN

    def one_block(block_id):
        offset = block_id * WIN
        masked, query_block, key_block = attention_scores(
            queries, ext_keys, ext_seg, ext_pos, offset
        )
        top_score = jnp.max(masked, axis=-1, keepdims=True)
        exp_scores = jnp.exp(masked - top_score)
        denom_sum = jnp.sum(exp_scores, axis=-1, keepdims=True)
        probs = (exp_scores / denom_sum).astype(jnp.bfloat16)
        result = jnp.einsum("hqk,kd->qhd", probs, ext_vals, preferred_element_type=jnp.float32)
        return (result, top_score + jnp.log(denom_sum))

    results, summary = lax.map(one_block, jnp.arange(blocks, dtype=jnp.int32))
    return (results.reshape(row_count, -1), summary)


def attend_backward(queries, ext_keys, ext_vals, ext_seg, ext_pos, summary, grad_out):
    row_count = queries.shape[0]
    blocks = row_count // WIN
    zero_grad = jnp.zeros((row_count + WIN, HD), jnp.float32)

    def one_block(carry, block_id):
        key_grad, value_grad = carry
        offset = block_id * WIN
        masked, query_block, key_block = attention_scores(
            queries, ext_keys, ext_seg, ext_pos, offset
        )
        value_block = lax.dynamic_slice_in_dim(ext_vals, offset, 2 * WIN, 0)
        probs = jnp.exp(masked - summary[block_id])
        low_probs = probs.astype(jnp.bfloat16)
        value_part = jnp.einsum(
            "hqk,qhd->kd", low_probs, grad_out, preferred_element_type=jnp.float32
        )
        prob_grad = jnp.einsum(
            "qhd,kd->hqk", grad_out, value_block, preferred_element_type=jnp.float32
        )
        centre = jnp.sum(probs * prob_grad, axis=-1, keepdims=True)
        score_grad = (probs * (prob_grad - centre)).astype(jnp.bfloat16)
        query_grad = jnp.einsum(
            "hqk,kd->qhd", score_grad, key_block, preferred_element_type=jnp.float32
        )
        key_part = jnp.einsum(
            "hqk,qhd->kd", score_grad, query_block, preferred_element_type=jnp.float32
        )
        key_grad = lax.dynamic_update_slice_in_dim(
            key_grad, lax.dynamic_slice_in_dim(key_grad, offset, 2 * WIN, 0) + key_part, offset, 0
        )
        value_grad = lax.dynamic_update_slice_in_dim(
            value_grad,
            lax.dynamic_slice_in_dim(value_grad, offset, 2 * WIN, 0) + value_part,
            offset,
            0,
        )
        return ((key_grad, value_grad), query_grad)

    (key_grad, value_grad), query_grads = lax.scan(
        one_block, (zero_grad, zero_grad), jnp.arange(blocks, dtype=jnp.int32)
    )
    return (key_grad, value_grad, query_grads.reshape(row_count, -1, HD))


def forward(inputs, layer_in, gathered, head_gains, ext_seg, ext_pos, angles, key_cols):
    w_query, w_keyval, w_out, w_left, w_right, w_gateup, w_down, w_pergate, w_perproj, gains = (
        gathered
    )
    row_count = inputs.shape[0]
    w_key = lax.dynamic_slice_in_dim(w_keyval[0], key_cols, HD, 1)
    w_value = lax.dynamic_slice_in_dim(w_keyval[1], key_cols, HD, 1)
    normal_in = normed(inputs, gains[0])
    low_in = normal_in.astype(jnp.bfloat16)
    query_raw = product(low_in, w_query).reshape(row_count, -1, HD)
    key_raw = product(low_in, w_key)
    value_raw = product(low_in, w_value)
    queries = rotate(normed(query_raw, head_gains[0]), angles[:, None, :]).astype(jnp.bfloat16)
    keys = rotate(normed(key_raw, head_gains[1]), angles).astype(jnp.bfloat16)
    values = value_map(value_raw).astype(jnp.bfloat16)
    tail_keys, tail_values = passed_along((keys, values), "dp", 1)
    ext_keys = jnp.concatenate([tail_keys, keys], axis=0)
    ext_vals = jnp.concatenate([tail_values, values], axis=0)
    attended, summary = attend_forward(queries, ext_keys, ext_vals, ext_seg, ext_pos)
    low_att = attended.astype(jnp.bfloat16)
    branch = lax.psum(product(low_att, w_out), "tensor")
    low_rank = product(low_in, w_left).astype(jnp.bfloat16)
    laurel_raw = product(low_rank, w_right)
    first_sum = (
        inputs + normed(branch, gains[1]) + normal_in + normed(laurel_raw, gains[2])
    ) * half_root
    low_mid = normed(first_sum, gains[3]).astype(jnp.bfloat16)
    gate_raw = product(low_mid, w_gateup[0])
    upward = product(low_mid, w_gateup[1])
    low_hidden = glu_pair(gate_raw, upward).astype(jnp.bfloat16)
    feed_raw = lax.psum(product(low_hidden, w_down), "tensor")
    second_sum = first_sum + normed(feed_raw, gains[4])
    low_second = second_sum.astype(jnp.bfloat16)
    pre_gate = product(low_second, w_pergate)
    low_gated = (gelu_tanh(pre_gate) * layer_in).astype(jnp.bfloat16)
    per_raw = product(low_gated, w_perproj)
    result = second_sum + normed(per_raw, gains[5])
    return dict(
        w_key=w_key,
        w_value=w_value,
        normal_in=normal_in,
        low_in=low_in,
        query_raw=query_raw,
        key_raw=key_raw,
        value_raw=value_raw,
        queries=queries,
        ext_keys=ext_keys,
        ext_vals=ext_vals,
        summary=summary,
        low_att=low_att,
        branch=branch,
        low_rank=low_rank,
        laurel_raw=laurel_raw,
        first_sum=first_sum,
        low_mid=low_mid,
        gate_raw=gate_raw,
        upward=upward,
        low_hidden=low_hidden,
        feed_raw=feed_raw,
        low_second=low_second,
        pre_gate=pre_gate,
        low_gated=low_gated,
        per_raw=per_raw,
        result=result,
    )


def body(
    hidden_in,
    layer_inputs,
    out_grad,
    lengths,
    order,
    w_query,
    w_keyval,
    w_out,
    w_left,
    w_right,
    w_gateup,
    w_down,
    w_pergate,
    w_perproj,
    gains,
    head_gains,
):
    devices = lax.axis_size("dp")
    my_index = lax.axis_index("dp")
    tok_dev = hidden_in.shape[0] * hidden_in.shape[1]
    width = hidden_in.shape[2]
    per_width = layer_inputs.shape[2]
    send_slot, recv_slot, ext_seg, ext_pos, total_rows = layout(
        lengths, order, my_index, devices, tok_dev
    )
    flat_in = hidden_in.reshape(tok_dev, width)
    flat_layer = layer_inputs.reshape(tok_dev, per_width)
    flat_cot = out_grad.reshape(tok_dev, width)
    arrived = (
        lax.all_to_all(
            pack(flat_in, send_slot, total_rows), "dp", split_axis=0, concat_axis=0, tiled=True
        ),
        lax.all_to_all(
            pack(flat_layer, send_slot, total_rows), "dp", split_axis=0, concat_axis=0, tiled=True
        ),
        lax.all_to_all(
            pack(flat_cot, send_slot, total_rows), "dp", split_axis=0, concat_axis=0, tiled=True
        ),
    )
    inputs = jnp.take(arrived[0], recv_slot, axis=0).astype(jnp.float32)
    layer_in = jnp.take(arrived[1], recv_slot, axis=0).astype(jnp.float32)
    cotangent = jnp.take(arrived[2], recv_slot, axis=0).astype(jnp.float32)
    gathered = (
        lax.all_gather(w_query, "dp", axis=0, tiled=True),
        lax.all_gather(w_keyval, "dp", axis=1, tiled=True),
        lax.all_gather(w_out, "dp", axis=1, tiled=True),
        lax.all_gather(w_left, "dp", axis=0, tiled=True),
        lax.all_gather(w_right, "dp", axis=1, tiled=True),
        lax.all_gather(w_gateup, "dp", axis=1, tiled=True),
        lax.all_gather(w_down, "dp", axis=1, tiled=True),
        lax.all_gather(w_pergate, "dp", axis=0, tiled=True),
        lax.all_gather(w_perproj, "dp", axis=1, tiled=True),
        lax.all_gather(gains.astype(jnp.bfloat16), "dp", axis=1, tiled=True).astype(gains.dtype),
    )
    (
        w_query_f,
        w_keyval_f,
        w_out_f,
        w_left_f,
        w_right_f,
        w_gateup_f,
        w_down_f,
        w_pergate_f,
        w_perproj_f,
        gains_f,
    ) = gathered
    parts = lax.axis_size("tensor")
    kv_index = lax.axis_index("tensor") // (parts // KVH)
    key_cols = kv_index * HD
    angles = ext_pos[WIN:].astype(jnp.float32)[:, None] * frequencies()
    first_pass = forward(inputs, layer_in, gathered, head_gains, ext_seg, ext_pos, angles, key_cols)
    saved = forward(inputs, layer_in, gathered, head_gains, ext_seg, ext_pos, angles, key_cols)
    _, back_per = jax.vjp(normed, saved["per_raw"], gains_f[5])
    per_grad, grad_g5 = back_per(cotangent)
    low_per = per_grad.astype(jnp.bfloat16)
    gated_grad = against(low_per, w_perproj_f)
    grad_perproj = across(saved["low_gated"], low_per)
    _, back_gelu = jax.vjp(gelu_tanh, saved["pre_gate"])
    pre_grad = back_gelu(gated_grad * layer_in)[0]
    layer_grad = gated_grad * gelu_tanh(saved["pre_gate"])
    low_pre = pre_grad.astype(jnp.bfloat16)
    grad_pergate = across(saved["low_second"], low_pre)
    second_grad = cotangent + against(low_pre, w_pergate_f)
    _, back_feed = jax.vjp(normed, saved["feed_raw"], gains_f[4])
    feed_grad, grad_g4 = back_feed(second_grad)
    low_feed = feed_grad.astype(jnp.bfloat16)
    hidden_grad = against(low_feed, w_down_f)
    grad_down = across(saved["low_hidden"], low_feed)
    _, back_glu = jax.vjp(glu_pair, saved["gate_raw"], saved["upward"])
    gate_grad, up_grad = back_glu(hidden_grad)
    low_gate = gate_grad.astype(jnp.bfloat16)
    low_up = up_grad.astype(jnp.bfloat16)
    grad_gateup = jnp.stack([across(saved["low_mid"], low_gate), across(saved["low_mid"], low_up)])
    mid_grad = lax.psum(against(low_gate, w_gateup_f[0]) + against(low_up, w_gateup_f[1]), "tensor")
    _, back_mid = jax.vjp(normed, saved["first_sum"], gains_f[3])
    first_part, grad_g3 = back_mid(mid_grad)
    first_grad = second_grad + first_part
    shared = first_grad * half_root
    _, back_laurel = jax.vjp(normed, saved["laurel_raw"], gains_f[2])
    laurel_grad, grad_g2 = back_laurel(shared)
    low_laurel = laurel_grad.astype(jnp.bfloat16)
    rank_grad = against(low_laurel, w_right_f)
    grad_right = across(saved["low_rank"], low_laurel)
    low_rank_grad = rank_grad.astype(jnp.bfloat16)
    grad_left = across(saved["low_in"], low_rank_grad)
    _, back_branch = jax.vjp(normed, saved["branch"], gains_f[1])
    branch_grad, grad_g1 = back_branch(shared)
    low_branch = branch_grad.astype(jnp.bfloat16)
    attended_grad = against(low_branch, w_out_f)
    grad_out = across(saved["low_att"], low_branch)
    low_att_grad = attended_grad.astype(jnp.bfloat16).reshape(tok_dev, -1, HD)
    key_grad, value_grad, query_grad = attend_backward(
        saved["queries"],
        saved["ext_keys"],
        saved["ext_vals"],
        ext_seg,
        ext_pos,
        saved["summary"],
        low_att_grad,
    )
    from_next = passed_along((key_grad[:WIN], value_grad[:WIN]), "dp", -1)
    pad_rows = jnp.zeros((tok_dev - WIN, HD), jnp.float32)
    key_total = key_grad[WIN:] + jnp.concatenate([pad_rows, from_next[0]], axis=0)
    value_total = value_grad[WIN:] + jnp.concatenate([pad_rows, from_next[1]], axis=0)

    def query_map(raw_value, gain_vec):
        return rotate(normed(raw_value, gain_vec), angles[:, None, :])

    def key_map(raw_value, gain_vec):
        return rotate(normed(raw_value, gain_vec), angles)

    _, back_query = jax.vjp(query_map, saved["query_raw"], head_gains[0])
    query_raw_grad, grad_hq = back_query(query_grad)
    _, back_key = jax.vjp(key_map, saved["key_raw"], head_gains[1])
    key_raw_grad, grad_hk = back_key(key_total)
    _, back_value = jax.vjp(value_map, saved["value_raw"])
    value_raw_grad = back_value(value_total)[0]
    low_q = query_raw_grad.reshape(tok_dev, -1).astype(jnp.bfloat16)
    low_k = key_raw_grad.astype(jnp.bfloat16)
    low_v = value_raw_grad.astype(jnp.bfloat16)
    attn_part = (
        against(low_q, w_query_f)
        + against(low_k, saved["w_key"])
        + against(low_v, saved["w_value"])
    )
    in_attn = lax.psum(attn_part, "tensor")
    grad_query = across(saved["low_in"], low_q)
    kv_head = jnp.stack([across(saved["low_in"], low_k), across(saved["low_in"], low_v)])
    zero_index = key_cols * 0
    grad_keyval = lax.dynamic_update_slice(
        jnp.zeros(w_keyval_f.shape, jnp.float32), kv_head, (zero_index, zero_index, key_cols)
    )
    normal_grad = in_attn + against(low_rank_grad, w_left_f) + shared
    _, back_in = jax.vjp(normed, inputs, gains_f[0])
    in_part, grad_g0 = back_in(normal_grad)
    input_grad = shared + in_part
    grad_gains = jnp.stack([grad_g0, grad_g1, grad_g2, grad_g3, grad_g4, grad_g5])
    grad_heads = jnp.stack([grad_hq, grad_hk])
    shards = (
        lax.psum_scatter(grad_query, "dp", scatter_dimension=0, tiled=True),
        lax.psum_scatter(grad_keyval, "dp", scatter_dimension=1, tiled=True),
        lax.psum_scatter(grad_out, "dp", scatter_dimension=1, tiled=True),
        lax.psum_scatter(grad_left, "dp", scatter_dimension=0, tiled=True),
        lax.psum_scatter(grad_right, "dp", scatter_dimension=1, tiled=True),
        lax.psum_scatter(grad_gateup, "dp", scatter_dimension=1, tiled=True),
        lax.psum_scatter(grad_down, "dp", scatter_dimension=1, tiled=True),
        lax.psum_scatter(grad_pergate, "dp", scatter_dimension=0, tiled=True),
        lax.psum_scatter(grad_perproj, "dp", scatter_dimension=1, tiled=True),
        lax.psum_scatter(grad_gains, "dp", scatter_dimension=1, tiled=True),
    )
    (
        shard_query,
        shard_keyval,
        shard_out,
        shard_left,
        shard_right,
        shard_gateup,
        shard_down,
        shard_pergate,
        shard_perproj,
        shard_gains,
    ) = shards
    shard_keyval = lax.psum(shard_keyval, "tensor")
    head_total = lax.psum(grad_heads, ("dp", "tensor"))
    back_home = (
        lax.all_to_all(
            shortened(pack(first_pass["result"].astype(jnp.bfloat16), recv_slot, total_rows)),
            "dp",
            split_axis=0,
            concat_axis=0,
            tiled=True,
        ),
        lax.all_to_all(
            pack(input_grad.astype(jnp.bfloat16), recv_slot, total_rows),
            "dp",
            split_axis=0,
            concat_axis=0,
            tiled=True,
        ),
        lax.all_to_all(
            pack(layer_grad.astype(jnp.bfloat16), recv_slot, total_rows),
            "dp",
            split_axis=0,
            concat_axis=0,
            tiled=True,
        ),
    )
    shape_lead = (hidden_in.shape[0], hidden_in.shape[1])
    output = jnp.take(back_home[0], send_slot, axis=0).reshape(shape_lead + (width,))
    grad_input = jnp.take(back_home[1], send_slot, axis=0).reshape(shape_lead + (width,))
    grad_layer = jnp.take(back_home[2], send_slot, axis=0).reshape(shape_lead + (per_width,))
    return (
        output,
        grad_input,
        grad_layer,
        shard_query,
        shard_keyval,
        shard_out,
        shard_left,
        shard_right,
        shard_gateup,
        shard_down,
        shard_pergate,
        shard_perproj,
        shard_gains,
        head_total,
    )


def solution(mesh):
    placed = (
        P(None, "dp", None),
        P(None, "dp", None),
        P(None, "dp", None),
        P(),
        P(),
        P("dp", "tensor"),
        P(None, "dp", None),
        P("tensor", "dp"),
        P("dp", None),
        P(None, "dp"),
        P(None, "dp", "tensor"),
        P("tensor", "dp"),
        P("dp", None),
        P(None, "dp"),
        P(None, "dp"),
        P(),
    )
    return jax.shard_map(
        body,
        mesh=mesh,
        in_specs=placed,
        out_specs=(
            P(None, "dp", None),
            P(None, "dp", None),
            P(None, "dp", None),
            P("dp", "tensor"),
            P(None, "dp", None),
            P("tensor", "dp"),
            P("dp", None),
            P(None, "dp"),
            P(None, "dp", "tensor"),
            P("tensor", "dp"),
            P("dp", None),
            P(None, "dp"),
            P(None, "dp"),
            P(),
        ),
        check_vma=False,
    )
```

profile of v0, /device:TPU:0, one launch (start us, length us, event | category | flops | bytes accessed | tf_op | source)
XLA Modules:
  0.0 1864.3 jit_solution(323387511991338859)
XLA Ops:
  17.3 5.8 add_select_fusion
  27.0 6.0 gather_fusion.7
  32.9 10.7 gather_fusion.1
  43.6 6.2 broadcast_select_fusion.2
  49.8 5.3 all-to-all-start
  57.9 61.1 %all_gather.30 = bf16[6,2048]{1,0:T(8,128)(2,1)S(1)} all-gather(bf16[6,256]{1,0:T(8,128)(2,1)S(1)} %convert_element_type.139), channel_id=1, replica_groups=mesh['dp'=8,'tensor'=4] {'dp'}, dimensions={1}, use_global_device_ids=true | all-gather | bytes 27648 | tf_op jit(solution)/shard_map/all_gather | solution.py:319
  122.8 7.1 gather_fusion.2
  161.5 5.0 fusion.146
  167.8 11.8 all_gather.34
  179.6 8.6 all_gather.35
  191.7 132.6 %all-reduce.10.cloned.1.call-done = f32[512,2048]{1,0:T(8,128)} async-done(((f32[512,2048]{1,0:T(8,128)}), f32[512,2048]{1,0:T(8,128)}) %all-reduce.10.cloned.1.call-update) | async-done | bytes 4194320 | tf_op jit(solution)/shard_map/psum | solution.py:219
  335.8 79.4 %all-gather.14.cloned.1.call-done = bf16[2,2048,2048]{2,1,0:T(8,128)(2,1)} async-done(((bf16[2,256,2048]{2,1,0:T(8,128)(2,1)}), bf16[2,2048,2048]{2,1,0:T(8,128)(2,1)}) %all-gather.14.cloned.1.call-update) | async-done | bytes 16777232 | tf_op jit(solution)/shard_map/all_gather | solution.py:315
  415.2 8.6 fusion.1
  425.7 7.0 multiply_convert_fusion.1
  432.7 40.4 %all-gather.16.cloned.1.call-done = bf16[2048,2048]{1,0:T(8,128)(2,1)} async-done(((bf16[2048,256]{1,0:T(8,128)(2,1)}), bf16[2048,2048]{1,0:T(8,128)(2,1)}) %all-gather.16.cloned.1.call-update) | async-done | bytes 8388624 | tf_op jit(solution)/shard_map/all_gather | solution.py:316
  473.1 10.6 fusion.147
  490.9 12.3 all_to_all.72
  512.2 44.8 %all-to-all-done.3 = bf16[8,128,2048]{2,1,0:T(8,128)(2,1)} async-done(((bf16[8,128,2048]{2,1,0:T(8,128)(2,1)}), bf16[8,128,2048]{2,1,0:T(8,128)(2,1)}, u32[]{:S(2)}, u32[]{:S(2)}) %all-to-all-start.3) | async-done | bytes 4194336 | tf_op jit(solution)/shard_map/all_to_all | solution.py:302
  557.1 7.9 gather_fusion.8
  565.0 73.8 %all-reduce.12.cloned.1.call-done = f32[512,2048]{1,0:T(8,128)} async-done(((f32[512,2048]{1,0:T(8,128)}), f32[512,2048]{1,0:T(8,128)}) %all-reduce.12.cloned.1.call-update) | async-done | bytes 4194320 | tf_op jit(solution)/shard_map/psum | solution.py:229
  647.2 16.0 all-gather.18.cloned.1.call-done
  667.3 21.4 %all-gather.20.cloned.1.call-done = bf16[256,2048]{1,0:T(8,128)(2,1)} async-done(((bf16[256,256]{1,0:T(8,128)(2,1)}), bf16[256,2048]{1,0:T(8,128)(2,1)}) %all-gather.20.cloned.1.call-update) | async-done | bytes 1048592 | tf_op jit(solution)/shard_map/all_gather | solution.py:318
  704.4 15.1 multiply_convert_fusion
  719.5 7.7 fusion
  727.2 8.4 fusion.35
  736.3 154.5 %all-reduce.14.cloned.1.call-done = f32[512,2048]{1,0:T(8,128)} async-done(((f32[512,2048]{1,0:T(8,128)}), f32[512,2048]{1,0:T(8,128)}) %all-reduce.14.cloned.1.call-update) | async-done | bytes 4194320 | tf_op jit(solution)/shard_map/psum | solution.py:360
  890.7 5.3 multiply_reduce_fusion.1
  896.7 8.4 multiply_reduce_fusion.2
  947.5 61.7 %reduce-scatter.13.cloned.1.call-done = f32[2,256,512]{2,1,0:T(8,128)} async-done(((f32[2,2048,512]{2,1,0:T(8,128)}), f32[2,256,512]{2,1,0:T(8,128)}) %reduce-scatter.13.cloned.1.call-update) | async-done | bytes 1048592 | tf_op jit(solution)/shard_map/reduce_scatter | solution.py:427
  1028.7 5.0 fusion.149
  1033.8 167.0 %all-reduce.16.cloned.1.call-done = (f32[512,2048]{1,0:T(8,128)}, f32[2,256,512]{2,1,0:T(8,128)}) async-done(((f32[512,2048]{1,0:T(8,128)}, f32[2,256,512]{2,1,0:T(8,128)}), (f32[512,2048]{1,0:T(8,128)}, f32[2,256,512]{2,1,0:T(8,128)})) %all-reduce.16.cloned.1.call-update) | async-done | bytes 5242896 | tf_op jit(solution)/shard_map/psum | solution.py:412
  1200.9 6.0 fusion.11
  1207.7 12.8 fusion.151
  1222.0 6.4 convolution_bitcast_fusion
  1228.5 8.1 convolution_bitcast_fusion.1
  1236.6 18.5 pad_maximum_fusion
  1266.7 6.0 gather_fusion.5
  1277.7 6.0 gather_fusion.9
  1283.7 6.2 broadcast_select_fusion
  1289.9 55.7 %all_to_all.73 = bf16[8,128,2048]{2,1,0:T(8,128)(2,1)} all-to-all(bf16[8,128,2048]{2,1,0:T(8,128)(2,1)} %bitcast.225), channel_id=1, replica_groups=mesh['dp'=8,'tensor'=4] {'dp'}, dimensions={0} | all-to-all | bytes 8388608 | tf_op jit(solution)/shard_map/all_to_all | solution.py:452
  1353.3 80.0 %psum.53 = f32[2,256]{1,0:T(2,128)} all-reduce(f32[2,256]{1,0:T(2,128)S(1)} %pad_maximum_fusion.5), channel_id=1, replica_groups=mesh['dp'=8,'tensor'=4] {'dp','tensor'}, use_global_device_ids=true, to_apply=%region_53.59 | all-reduce | flops 512 | bytes 4096 | tf_op jit(solution)/shard_map/psum | solution.py:450
  1433.3 8.0 gather_fusion.6
  1441.3 8.4 gather_fusion.10
  1449.7 5.0 broadcast_select_fusion.4
  1454.8 34.5 %reduce-scatter.15.cloned.1.call-done = f32[512,256]{1,0:T(8,128)} async-done(((f32[512,2048]{1,0:T(8,128)}), f32[512,256]{1,0:T(8,128)}) %reduce-scatter.15.cloned.1.call-update) | async-done | bytes 524304 | tf_op jit(solution)/shard_map/reduce_scatter | solution.py:428
  1489.3 36.8 %reduce-scatter.29.cloned.1.call-done = f32[6,256]{1,0:T(8,128)} async-done(((f32[6,2048]{1,0:T(8,128)}), f32[6,256]{1,0:T(8,128)}) %reduce-scatter.29.cloned.1.call-update) | async-done | bytes 6160 | tf_op jit(solution)/shard_map/reduce_scatter | solution.py:435
  1526.1 120.4 %reduce-scatter.23.cloned.1.call-done = f32[2048,256]{1,0:T(8,128)} async-done(((f32[2048,2048]{1,0:T(8,128)}), f32[2048,256]{1,0:T(8,128)}) %reduce-scatter.23.cloned.1.call-update) | async-done | bytes 2097168 | tf_op jit(solution)/shard_map/reduce_scatter | solution.py:432
  1646.5 209.8 %reduce-scatter.21.cloned.1.call-done = f32[2,256,2048]{2,1,0:T(8,128)} async-done(((f32[2,2048,2048]{2,1,0:T(8,128)}), f32[2,256,2048]{2,1,0:T(8,128)}) %reduce-scatter.21.cloned.1.call-update) | async-done | bytes 4194320 | tf_op jit(solution)/shard_map/reduce_scatter | solution.py:431
  (466 shorter events, 203.7 us)
Async XLA Ops:
  7.2 19.8 %copy-start = (bf16[8,64,2048]{2,1,0:T(8,128)(2,1)S(1)}, bf16[8,64,2048]{2,1,0:T(8,128)(2,1)}, u32[]{:S(2)}) copy-start(bf16[8,64,2048]{2,1,0:T(8,128)(2,1)} %param.28) | copy-start | bytes 6291460
  7.2 126.5 %all-gather.10.cloned.1.call-start = ((), (), s32[]{:S(2)}) async-start(), calls=%async_computation.17 | async-start | bytes 2359296 | tf_op jit(solution)/shard_map/all_gather | solution.py:310
  7.9 132.6 %all-gather.8.cloned.1.call-start = ((), (), s32[]{:S(2)}) async-start(), calls=%async_computation.16 | async-start | bytes 4718592 | tf_op jit(solution)/shard_map/all_gather | solution.py:311
  49.7 70.2 %copy-start.123 = (f32[2,256]{1,0:T(2,128)S(1)}, f32[2,256]{1,0:T(2,128)}, u32[]{:S(2)}) copy-start(f32[2,256]{1,0:T(2,128)} %param.41) | copy-start | bytes 6148
  49.8 73.1 %all-to-all-start = ((bf16[8,128,2048]{2,1,0:T(8,128)(2,1)}), bf16[8,128,2048]{2,1,0:T(8,128)(2,1)}, u32[]{:S(2)}, u32[]{:S(2)}) async-start(bf16[8,128,2048]{2,1,0:T(8,128)(2,1)} %bitcast.223), calls=%async_computation | async-start | bytes 8388608 | tf_op jit(solution)/shard_map/all_to_all | solution.py:296
  55.1 106.4 %all-gather.12.cloned.1.call-start = ((), (), s32[]{:S(2)}) async-start(), calls=%async_computation.18 | async-start | bytes 2359296 | tf_op jit(solution)/shard_map/all_gather | solution.py:312
  55.8 268.5 %all-reduce.10.cloned.1.call-start = ((), (), s32[]{:S(2)}) async-start(), calls=%async_computation.19 | async-start | bytes 8388608 | tf_op jit(solution)/shard_map/psum | solution.py:219
  120.0 25.2 %copy-start.108 = (f32[1,256]{1,0:T(1,128)}, f32[1,256]{1,0:T(1,128)S(1)}, u32[]{:S(2)}) copy-start(f32[1,256]{1,0:T(1,128)S(1)} %get-tuple-element.158) | copy-start | bytes 3076
  122.8 204.2 %copy-start.69 = (f32[1,2048]{1,0:T(1,128)}, f32[1,2048]{1,0:T(1,128)S(1)}, u32[]{:S(2)}) copy-start(f32[1,2048]{1,0:T(1,128)S(1)} %get-tuple-element.149) | copy-start | bytes 24580
  149.1 6.9 collective-permute-start.1
  153.5 4.6 collective-permute-start
  166.5 248.7 %all-gather.14.cloned.1.call-start = ((), (), s32[]{:S(2)}) async-start(), calls=%async_computation.20 | async-start | bytes 18874368 | tf_op jit(solution)/shard_map/all_gather | solution.py:315
  167.1 305.9 %all-gather.16.cloned.1.call-start = ((), (), s32[]{:S(2)}) async-start(), calls=%async_computation.21 | async-start | bytes 9437184 | tf_op jit(solution)/shard_map/all_gather | solution.py:316
  167.7 471.1 %all-reduce.12.cloned.1.call-start = ((), (), s32[]{:S(2)}) async-start(), calls=%async_computation.22 | async-start | bytes 8388608 | tf_op jit(solution)/shard_map/psum | solution.py:229
  189.0 138.0 %copy-start.73 = (f32[1,2048]{1,0:T(1,128)S(1)}, f32[1,2048]{1,0:T(1,128)}, u32[]{:S(2)}) copy-start(f32[1,2048]{1,0:T(1,128)} %get-tuple-element.147) | copy-start | bytes 24580
  189.0 138.0 %copy-start.74 = (f32[1,2048]{1,0:T(1,128)S(1)}, f32[1,2048]{1,0:T(1,128)}, u32[]{:S(2)}) copy-start(f32[1,2048]{1,0:T(1,128)} %get-tuple-element.148) | copy-start | bytes 24580
  189.0 138.0 %copy-start.80 = (pred[512]{0:T(512)(128)(4,1)S(1)}, pred[512]{0:T(512)(128)(4,1)}, u32[]{:S(2)}) copy-start(pred[512]{0:T(512)(128)(4,1)} %copy-done.79) | copy-start | bytes 1540
  189.0 138.0 %copy-start.83 = (f32[512]{0:T(512)S(1)}, f32[512]{0:T(512)}, u32[]{:S(2)}) copy-start(f32[512]{0:T(512)} %copy-done.82) | copy-start | bytes 6148
  503.2 53.8 %all-to-all-start.3 = ((bf16[8,128,2048]{2,1,0:T(8,128)(2,1)}), bf16[8,128,2048]{2,1,0:T(8,128)(2,1)}, u32[]{:S(2)}, u32[]{:S(2)}) async-start(bf16[8,128,2048]{2,1,0:T(8,128)(2,1)} %bitcast.222), calls=%async_computation.3 | async-start | bytes 8388608 | tf_op jit(solution)/shard_map/all_to_all | solution.py:302
  507.9 155.3 %all-gather.18.cloned.1.call-start = ((), (), s32[]{:S(2)}) async-start(), calls=%async_computation.23 | async-start | bytes 1179648 | tf_op jit(solution)/shard_map/all_gather | solution.py:317
  508.7 180.0 %all-gather.20.cloned.1.call-start = ((), (), s32[]{:S(2)}) async-start(), calls=%async_computation.24 | async-start | bytes 1179648 | tf_op jit(solution)/shard_map/all_gather | solution.py:318
  509.4 381.3 %all-reduce.14.cloned.1.call-start = ((), (), s32[]{:S(2)}) async-start(), calls=%async_computation.25 | async-start | bytes 8388608 | tf_op jit(solution)/shard_map/psum | solution.py:360
  565.0 76.5 %copy-start.71 = (f32[1,2048]{1,0:T(1,128)S(1)}, f32[1,2048]{1,0:T(1,128)}, u32[]{:S(2)}) copy-start(f32[1,2048]{1,0:T(1,128)} %get-tuple-element.145) | copy-start | bytes 24580
  642.3 21.0 %copy-start.60 = (bf16[512,256]{1,0:T(8,128)(2,1)S(1)}, bf16[512,256]{1,0:T(8,128)(2,1)}, u32[]{:S(2)}) copy-start(bf16[512,256]{1,0:T(8,128)(2,1)} %gather_fusion.4) | copy-start | bytes 786436
  667.3 23.6 %copy-start.72 = (f32[1,2048]{1,0:T(1,128)S(1)}, f32[1,2048]{1,0:T(1,128)}, u32[]{:S(2)}) copy-start(f32[1,2048]{1,0:T(1,128)} %get-tuple-element.144) | copy-start | bytes 24580
  735.6 273.6 %reduce-scatter.13.cloned.1.call-start = ((), (), s32[]{:S(2)}) async-start(), calls=%async_computation.27 | async-start | bytes 9437184 | tf_op jit(solution)/shard_map/reduce_scatter | solution.py:427
  912.4 6.2 collective-permute-start.3
  917.3 4.4 collective-permute-start.2
  931.9 268.8 %all-reduce.16.cloned.1.call-start = ((), (), s32[]{:S(2)}) async-start(), calls=%async_computation.36 | async-start | bytes 10485760 | tf_op jit(solution)/shard_map/psum | solution.py:412
  947.5 61.8 %copy-start.57 = (bf16[512,256]{1,0:T(8,128)(2,1)S(1)}, bf16[512,256]{1,0:T(8,128)(2,1)}, u32[]{:S(2)}) copy-start(bf16[512,256]{1,0:T(8,128)(2,1)} %copy-done.56) | copy-start | bytes 786436
  1009.2 445.5 %reduce-scatter.25.cloned.1.call-start = ((), (), s32[]{:S(2)}) async-start(), calls=%async_computation.33 | async-start | bytes 2359296 | tf_op jit(solution)/shard_map/reduce_scatter | solution.py:433
  1013.6 441.1 %reduce-scatter.27.cloned.1.call-start = ((), (), s32[]{:S(2)}) async-start(), calls=%async_computation.34 | async-start | bytes 2359296 | tf_op jit(solution)/shard_map/reduce_scatter | solution.py:434
  1017.4 437.3 %reduce-scatter.19.cloned.1.call-start = ((), (), s32[]{:S(2)}) async-start(), calls=%async_computation.30 | async-start | bytes 589824 | tf_op jit(solution)/shard_map/reduce_scatter | solution.py:430
  1020.6 434.1 %reduce-scatter.17.cloned.1.call-start = ((), (), s32[]{:S(2)}) async-start(), calls=%async_computation.29 | async-start | bytes 589824 | tf_op jit(solution)/shard_map/reduce_scatter | solution.py:429
  1024.3 430.5 %reduce-scatter.11.cloned.1.call-start = ((), (), s32[]{:S(2)}) async-start(), calls=%async_computation.26 | async-start | bytes 4718592 | tf_op jit(solution)/shard_map/reduce_scatter | solution.py:426
  1027.7 173.1 %copy-start.8 = (bf16[512,2048]{1,0:T(8,128)(2,1)S(1)}, bf16[512,2048]{1,0:T(8,128)(2,1)}, u32[]{:S(2)}) copy-start(bf16[512,2048]{1,0:T(8,128)(2,1)} %copy-done.6) | copy-start | bytes 6291460
  1027.7 173.1 %copy-start.38 = (bf16[2048,64]{0,1:T(8,128)(2,1)S(1)}, bf16[2048,64]{0,1:T(8,128)(2,1)}, u32[]{:S(2)}) copy-start(bf16[2048,64]{0,1:T(8,128)(2,1)} %copy-done.37) | copy-start | bytes 786436
  1027.7 173.1 %copy-start.70 = (f32[1,2048]{1,0:T(1,128)S(1)}, f32[1,2048]{1,0:T(1,128)}, u32[]{:S(2)}) copy-start(f32[1,2048]{1,0:T(1,128)} %copy-done.69) | copy-start | bytes 24580
  1027.7 173.1 %copy-start.81 = (pred[512]{0:T(512)(128)(4,1)S(1)}, pred[512]{0:T(512)(128)(4,1)}, u32[]{:S(2)}) copy-start(pred[512]{0:T(512)(128)(4,1)} %copy-done.79) | copy-start | bytes 1540
  1027.7 173.1 %copy-start.84 = (f32[512]{0:T(512)S(1)}, f32[512]{0:T(512)}, u32[]{:S(2)}) copy-start(f32[512]{0:T(512)} %copy-done.82) | copy-start | bytes 6148
  1027.7 461.6 %reduce-scatter.15.cloned.1.call-start = ((), (), s32[]{:S(2)}) async-start(), calls=%async_computation.28 | async-start | bytes 4718592 | tf_op jit(solution)/shard_map/reduce_scatter | solution.py:428
  1033.7 492.3 %reduce-scatter.29.cloned.1.call-start = ((), (), s32[]{:S(2)}) async-start(), calls=%async_computation.35 | async-start | bytes 73728 | tf_op jit(solution)/shard_map/reduce_scatter | solution.py:435
  1207.6 438.9 %reduce-scatter.23.cloned.1.call-start = ((), (), s32[]{:S(2)}) async-start(), calls=%async_computation.32 | async-start | bytes 18874368 | tf_op jit(solution)/shard_map/reduce_scatter | solution.py:432
  1220.5 635.9 %reduce-scatter.21.cloned.1.call-start = ((), (), s32[]{:S(2)}) async-start(), calls=%async_computation.31 | async-start | bytes 37748736 | tf_op jit(solution)/shard_map/reduce_scatter | solution.py:431
  1262.9 26.9 %all-to-all-start.5 = ((bf16[8,128,256]{2,1,0:T(8,128)(2,1)}), bf16[8,128,256]{2,1,0:T(8,128)(2,1)S(1)}, u32[]{:S(2)}, u32[]{:S(2)}) async-start(bf16[8,128,256]{2,1,0:T(8,128)(2,1)} %bitcast.67), calls=%async_computation.5 | async-start | bytes 1048576 | tf_op jit(solution)/shard_map/all_to_all | solution.py:466
  1345.6 95.7 %all-to-all-start.4 = ((bf16[8,128,2048]{2,1,0:T(8,128)(2,1)}), bf16[8,128,2048]{2,1,0:T(8,128)(2,1)}, u32[]{:S(2)}, u32[]{:S(2)}) async-start(bf16[8,128,2048]{2,1,0:T(8,128)(2,1)} %bitcast.224), calls=%async_computation.4 | async-start | bytes 8388608 | tf_op jit(solution)/shard_map/all_to_all | solution.py:459
  1441.3 416.0 %copy-start.1 = (bf16[8,64,2048]{2,1,0:T(8,128)(2,1)S(1)}, bf16[8,64,2048]{2,1,0:T(8,128)(2,1)}, u32[]{:S(2)}) copy-start(bf16[8,64,2048]{2,1,0:T(8,128)(2,1)} %param.28) | copy-start | bytes 6291460
  1449.7 406.7 %copy-start.58 = (f32[2,256,512]{2,1,0:T(8,128)S(1)}, f32[2,256,512]{2,1,0:T(8,128)}, u32[]{:S(2)}) copy-start(f32[2,256,512]{2,1,0:T(8,128)} %get-tuple-element.202) | copy-start | bytes 3145732
  (113 other events, 561.6 us)
Sparse Core Ops, SparseCore 0:
  9.9 30.5 all-gather.9
  42.5 63.0 all-gather.7
  107.4 33.5 all-gather.11
  166.6 157.6 all-reduce.9
  326.2 88.9 all-gather.13
  417.1 55.9 all-gather.15
  483.8 154.9 all-reduce.11
  640.7 22.4 all-gather.17
  665.1 23.5 all-gather.19
  735.7 154.9 all-reduce.13
  932.0 77.1 reduce-scatter.12
  1011.5 189.2 all-reduce.15
  1204.6 40.1 reduce-scatter.24
  1248.9 42.7 reduce-scatter.26
  1295.2 38.1 reduce-scatter.18
  1337.2 43.7 reduce-scatter.16
  1384.7 48.9 reduce-scatter.10
  1437.9 51.3 reduce-scatter.14
  1492.8 33.1 reduce-scatter.28
  1530.5 115.9 reduce-scatter.22
  1651.1 205.2 reduce-scatter.20
where the time goes:
time: 1880 us; the launch traced here: 1860 us
  waiting for transfers between devices  1200 us (64%)
  blocking collectives  230 us (12%)
  matrix products  157 us (8%)
  other arithmetic  117 us (6%)
  local copies, waits for them, and re-layouts  116 us (6%)
  starting transfers between devices  27.4 us (1%)
    reduce_scatter x1, waiting for transfers between devices, body(): lax.psum_scatter(grad_gateup, 'dp', scatter_dimension=1, tiled=True)  210 us
    psum x1, waiting for transfers between devices, body(): in_attn = lax.psum(attn_part, 'tensor')  167 us
    psum x1, waiting for transfers between devices, body(): lax.psum(against(low_gate, w_gateup_f[0]) + against(low_up, w_gateup_f[1]...  154 us
    psum x1, waiting for transfers between devices, forward(): branch = lax.psum(product(low_att, w_out), 'tensor')  133 us
    reduce_scatter x1, waiting for transfers between devices, body(): lax.psum_scatter(grad_down, 'dp', scatter_dimension=1, tiled=True)  120 us
    psum x1, blocking collectives, body(): head_total = lax.psum(grad_heads, ('dp', 'tensor'))  80 us
    all_gather x1, waiting for transfers between devices, body(): lax.all_gather(w_gateup, 'dp', axis=1, tiled=True)  79.4 us
    psum x1, waiting for transfers between devices, forward(): feed_raw = lax.psum(product(low_hidden, w_down), 'tensor')  73.8 us
  transfers between devices with their start and end apart: 29, of which 15 were waited for; matrix products, arithmetic and copies ran while one was open for 15% of the time, Pallas kernels for 0%

commit v1 on v0

v1 whole, which is shorter than its diff:
```python
import jax
import jax.numpy as jnp
from jax import lax
from jax.sharding import PartitionSpec as P

KVH = 2
HD = 256
WIN = 512
LMIN = 1024
LANES = 128

half_root = 0.7071067811865476
masked_value = -1e30
bf16 = jnp.bfloat16
f32 = jnp.float32


def normed(values_in, gain_vec):
    norm_scale = lax.rsqrt(jnp.mean(values_in * values_in, axis=-1, keepdims=True) + 1e-06)
    return values_in * norm_scale * gain_vec


def rotate(values_in, angles):
    half_dim = values_in.shape[-1] // 2
    first_half = values_in[..., :half_dim]
    second_half = values_in[..., half_dim:]
    cosine = jnp.cos(angles)
    sine_part = jnp.sin(angles)
    return jnp.concatenate(
        [
            first_half * cosine - second_half * sine_part,
            second_half * cosine + first_half * sine_part,
        ],
        axis=-1,
    )


def gelu_tanh(values_in):
    return jax.nn.gelu(values_in, approximate=True)


def glu_pair(gate_raw, upward):
    return gelu_tanh(gate_raw) * upward


def value_map(raw_value):
    return normed(raw_value, 1.0)


def product(left_mat, right_mat, kind=f32):
    return jnp.dot(left_mat, right_mat, preferred_element_type=f32).astype(kind)


def against(left_mat, right_mat, kind=f32):
    return lax.dot_general(
        left_mat, right_mat, (((1,), (1,)), ((), ())), preferred_element_type=f32
    ).astype(kind)


def across(left_mat, right_mat, kind=f32):
    return lax.dot_general(
        left_mat, right_mat, (((0,), (0,)), ((), ())), preferred_element_type=f32
    ).astype(kind)


def frequencies():
    half_dim = HD // 2
    return jnp.power(10000.0, -2.0 * jnp.arange(half_dim, dtype=f32) / HD)


def shifted(piece, axis, by):
    length = lax.axis_size(axis)
    return lax.ppermute(piece, axis, [(i, (i + by) % length) for i in range(length)])


def crossed(piece, axis, bit):
    length = lax.axis_size(axis)
    return lax.ppermute(piece, axis, [(i, i ^ bit) for i in range(length)])


def spread(piece, axis):
    length = lax.axis_size(axis)
    return jnp.concatenate([piece] + [shifted(piece, axis, s) for s in range(1, length)], axis=0)


def folded(parts, axis):
    length = lax.axis_size(axis)
    rows = parts.shape[0] // length
    total = parts[:rows].astype(f32)
    for s in range(1, length):
        total = total + shifted(parts[s * rows : (s + 1) * rows], axis, -s).astype(f32)
    return total


def butterfly(piece, axis):
    length = lax.axis_size(axis)
    bit = 1
    while bit < length:
        piece = piece + crossed(piece, axis, bit)
        bit *= 2
    return piece


def passed_along(shard, axis, by):
    length = lax.axis_size(axis)
    pairs = [(i, i + by) for i in range(length) if 0 <= i + by < length]
    return lax.ppermute(shard, axis, pairs)


def blocks_of(mat, order_of):
    width = mat.shape[1] // lax.axis_size("dp")
    return jnp.concatenate(
        [lax.dynamic_slice_in_dim(mat, o * width, width, 1) for o in order_of], axis=1
    )


def rank_among(keys_own):
    count = keys_own.shape[0]
    place = jnp.arange(count, dtype=jnp.int32)
    same = (keys_own[None, :] == keys_own[:, None]) & (place[None, :] < place[:, None])
    return jnp.sum(same.astype(jnp.int32), axis=1)


def plan(lengths, order, micro, block_rows):
    devices = lax.axis_size("dp")
    parts = lax.axis_size("tensor")
    me = lax.axis_index("dp")
    part = lax.axis_index("tensor")
    tok = micro * block_rows
    own = tok // parts
    stretch = devices * block_rows
    seqs = lengths.shape[0]
    given_len = jnp.take(lengths, order)
    given_start = jnp.cumsum(given_len) - given_len
    dealt_start = jnp.cumsum(lengths) - lengths
    seq_ids = jnp.arange(seqs, dtype=jnp.int32)
    shift_given = jnp.take(dealt_start, order) - given_start
    pieces = tok // LMIN + 2
    runs = tok // stretch + 1
    per_piece = block_rows * (-(-tok // stretch)) + (parts - 1) * runs
    capacity = -(-(pieces * (per_piece // parts)) // 8) * 8
    kept = -(-(tok // parts + seqs) // 8) * 8

    def pick(table, index):
        return jnp.sum(jnp.where(index[:, None] == seq_ids[None, :], table[None, :], 0), axis=1)

    local = jnp.arange(tok, dtype=jnp.int32)
    stream = local // block_rows * stretch + me * block_rows + local % block_rows
    arrival = jnp.sum((stream[:, None] >= given_start[None, 1:]).astype(jnp.int32), axis=1)
    dealt = stream + pick(shift_given, arrival)
    target = dealt // tok
    quarter = dealt % parts
    send_slot = target * capacity + rank_among(target * parts + quarter)
    send_slot = jnp.where(quarter == part, send_slot, -1)
    keep_rank = rank_among(quarter)
    keep_slot = (part - quarter) % parts * kept + keep_rank

    place = me * tok + jnp.arange(own, dtype=jnp.int32) * parts + part
    own_seq = jnp.sum((place[:, None] >= dealt_start[None, 1:]).astype(jnp.int32), axis=1)
    shift_dealt = jnp.sum(
        jnp.where(order[None, :] == seq_ids[:, None], -shift_given[None, :], 0), axis=1
    )
    anchor = place + pick(shift_dealt, own_seq)
    source = anchor % stretch // block_rows
    prior = (anchor[None, :] < anchor[:, None]) & (source[None, :] == source[:, None])
    recv_slot = source * capacity + jnp.sum(prior.astype(jnp.int32), axis=1)

    total = devices * capacity
    slots = jnp.arange(total, dtype=jnp.int32)
    sender = (slots[:, None] == send_slot[None, :]).astype(bf16)
    receiver = (recv_slot[:, None] == slots[None, :]).astype(bf16)
    mine = jnp.where(quarter == part, keep_rank, -1)
    chosen = (jnp.arange(kept, dtype=jnp.int32)[:, None] == mine[None, :]).astype(bf16)
    compact = against(chosen, sender, bf16)
    homing = (
        keep_slot[:, None] == jnp.arange(parts * kept, dtype=jnp.int32)[None, :]
    ).astype(bf16)

    held = (part - jnp.arange(parts, dtype=jnp.int32)) % parts
    rows = (jnp.arange(own, dtype=jnp.int32)[None, :] * parts + held[:, None]).reshape(tok)
    both = me * tok + jnp.concatenate([rows - tok, rows])
    ext_seq = jnp.sum((both[:, None] >= dealt_start[None, 1:]).astype(jnp.int32), axis=1)
    ext_pos = both - pick(dealt_start, ext_seq)
    ext_seg = jnp.where(both >= 0, ext_seq, -1)
    return sender, receiver, compact, homing, ext_seg, ext_pos


def body(
    hidden_in,
    layer_inputs,
    out_grad,
    lengths,
    order,
    w_query,
    w_keyval,
    w_out,
    w_left,
    w_right,
    w_gateup,
    w_down,
    w_pergate,
    w_perproj,
    gains,
    head_gains,
):
    devices = lax.axis_size("dp")
    me = lax.axis_index("dp")
    parts = lax.axis_size("tensor")
    part = lax.axis_index("tensor")
    micro, block_rows, width = hidden_in.shape
    per_width = layer_inputs.shape[2]
    tok = micro * block_rows
    assert tok == WIN
    sender, receiver, compact, homing, ext_seg, ext_pos = plan(lengths, order, micro, block_rows)

    kv_cols = part // (parts // KVH) * HD
    kv_own = lax.dynamic_slice_in_dim(w_keyval, kv_cols, HD, 2)
    gains_high = lax.reduce_precision(gains, 8, 7)
    gains_low = (gains - gains_high).astype(bf16)
    gain_cols = jnp.concatenate([gains_high.astype(bf16), gains_low], axis=0)
    gain_cols = jnp.pad(gain_cols, ((0, LANES - gain_cols.shape[0]), (0, 0))).T
    q_width = w_query.shape[1]
    rank = w_left.shape[1]
    bundle = [
        w_query,
        kv_own[0],
        kv_own[1],
        w_out.T,
        w_left,
        w_right.T,
        w_pergate,
        w_perproj.T,
        gain_cols,
    ]
    marks = [0]
    for piece in bundle:
        marks.append(marks[-1] + piece.shape[1])
    bundle_f = lax.all_gather(jnp.concatenate(bundle, axis=1), "dp", axis=0, tiled=True)
    gathered = [bundle_f[:, a:b] for a, b in zip(marks[:-1], marks[1:])]
    wq, wk, wv, wo_t, wl, wr_t, wg, wp_t, gain_f = gathered
    gu_in, _ = lax.optimization_barrier((w_gateup, bundle_f[:8, :LANES]))
    w_gu = lax.all_gather(gu_in, "dp", axis=1, tiled=True)
    dn_in, _ = lax.optimization_barrier((w_down, w_gu[0, :8, :LANES]))
    w_dn = lax.all_gather(dn_in, "dp", axis=1, tiled=True)
    gain_rows = gain_f.T
    gains_f = gain_rows[:6].astype(f32) + gain_rows[6:12].astype(f32)

    flat = jnp.concatenate(
        [
            hidden_in.reshape(tok, width),
            layer_inputs.reshape(tok, per_width),
            out_grad.reshape(tok, width),
        ],
        axis=1,
    )
    packed = product(sender, flat, bf16)
    first_cols = width + per_width
    come_in = lax.all_to_all(packed[:, :width], "dp", 0, 0, tiled=True)
    come_rest = lax.all_to_all(packed[:, width:], "dp", 0, 0, tiled=True)
    inputs = product(receiver, come_in, bf16).astype(f32)
    rest = product(receiver, come_rest, bf16)
    layer_in = rest[:, :per_width].astype(f32)
    cotangent = rest[:, per_width:].astype(f32)

    angles = ext_pos[tok:].astype(f32)[:, None] * frequencies()

    normal_in = normed(inputs, gains_f[0])
    low_in = normal_in.astype(bf16)
    all_in = spread(low_in, "tensor")
    query_raw = product(all_in, wq).reshape(tok, -1, HD)
    key_raw = product(all_in, wk)
    value_raw = product(all_in, wv)

    def query_map(raw_value, gain_vec):
        return rotate(normed(raw_value, gain_vec), angles[:, None, :])

    def key_map(raw_value, gain_vec):
        return rotate(normed(raw_value, gain_vec), angles)

    queries = query_map(query_raw, head_gains[0]).astype(bf16)
    keys = key_map(key_raw, head_gains[1]).astype(bf16)
    values = value_map(value_raw).astype(bf16)
    tails = passed_along(jnp.concatenate([keys, values], axis=1), "dp", 1)
    ext_keys = jnp.concatenate([tails[:, :HD], keys], axis=0)
    ext_vals = jnp.concatenate([tails[:, HD:], values], axis=0)
    gap = ext_pos[tok:, None] - ext_pos[None, :]
    allowed = (ext_seg[tok:, None] == ext_seg[None, :]) & (gap >= 0) & (gap < WIN)
    scores = jnp.einsum("qhd,kd->hqk", queries, ext_keys, preferred_element_type=f32)
    masked = jnp.where(allowed[None], scores, masked_value)
    top_score = jnp.max(masked, axis=-1, keepdims=True)
    exp_scores = jnp.exp(masked - top_score)
    probs = exp_scores / jnp.sum(exp_scores, axis=-1, keepdims=True)
    low_probs = probs.astype(bf16)
    attended = jnp.einsum("hqk,kd->qhd", low_probs, ext_vals, preferred_element_type=f32)
    low_att = attended.astype(bf16).reshape(tok, -1)
    branch = folded(against(low_att, wo_t, bf16), "tensor")

    low_rank = product(low_in, wl, bf16)
    laurel_raw = against(low_rank, wr_t)
    first_sum = (
        inputs + normed(branch, gains_f[1]) + normal_in + normed(laurel_raw, gains_f[2])
    ) * half_root
    low_mid = normed(first_sum, gains_f[3]).astype(bf16)

    all_mid = spread(low_mid, "tensor")
    gate_raw = product(all_mid, w_gu[0])
    upward = product(all_mid, w_gu[1])
    low_hidden = glu_pair(gate_raw, upward).astype(bf16)
    feed_raw = folded(product(low_hidden, w_dn, bf16), "tensor")

    second_sum = first_sum + normed(feed_raw, gains_f[4])
    low_second = second_sum.astype(bf16)
    pre_gate = product(low_second, wg)
    low_gated = (gelu_tanh(pre_gate) * layer_in).astype(bf16)
    per_raw = against(low_gated, wp_t)
    result = second_sum + normed(per_raw, gains_f[5])

    _, back_per = jax.vjp(normed, per_raw, gains_f[5])
    per_grad, grad_g5 = back_per(cotangent)
    low_per = per_grad.astype(bf16)
    gated_grad = product(low_per, wp_t)
    grad_perproj = across(low_per, low_gated, bf16)
    gelu_out, back_gelu = jax.vjp(gelu_tanh, pre_gate)
    low_pre = back_gelu(gated_grad * layer_in)[0].astype(bf16)
    layer_grad = gated_grad * gelu_out
    grad_pergate = across(low_second, low_pre, bf16)
    second_grad = cotangent + against(low_pre, wg)
    _, back_feed = jax.vjp(normed, feed_raw, gains_f[4])
    feed_grad, grad_g4 = back_feed(second_grad)
    low_feed = feed_grad.astype(bf16)

    all_feed = spread(low_feed, "tensor")
    hidden_grad = against(all_feed, w_dn)
    _, back_glu = jax.vjp(glu_pair, gate_raw, upward)
    gate_grad, up_grad = back_glu(hidden_grad)
    low_gate = gate_grad.astype(bf16)
    low_up = up_grad.astype(bf16)
    mid_part = against(low_gate, w_gu[0]) + against(low_up, w_gu[1])
    mid_grad = folded(mid_part.astype(bf16), "tensor")

    _, back_mid = jax.vjp(normed, first_sum, gains_f[3])
    first_part, grad_g3 = back_mid(mid_grad)
    shared = (second_grad + first_part) * half_root
    _, back_laurel = jax.vjp(normed, laurel_raw, gains_f[2])
    laurel_grad, grad_g2 = back_laurel(shared)
    low_laurel = laurel_grad.astype(bf16)
    low_rank_grad = product(low_laurel, wr_t, bf16)
    grad_right = across(low_laurel, low_rank, bf16)
    grad_left = across(low_in, low_rank_grad, bf16)
    _, back_branch = jax.vjp(normed, branch, gains_f[1])
    branch_grad, grad_g1 = back_branch(shared)
    low_branch = branch_grad.astype(bf16)

    all_branch = spread(low_branch, "tensor")
    low_att_grad = product(all_branch, wo_t, bf16).reshape(tok, -1, HD)
    value_grad = jnp.einsum("hqk,qhd->kd", low_probs, low_att_grad, preferred_element_type=f32)
    prob_grad = jnp.einsum("qhd,kd->hqk", low_att_grad, ext_vals, preferred_element_type=f32)
    centre = jnp.sum(probs * prob_grad, axis=-1, keepdims=True)
    score_grad = (probs * (prob_grad - centre)).astype(bf16)
    query_grad = jnp.einsum("hqk,kd->qhd", score_grad, ext_keys, preferred_element_type=f32)
    key_grad = jnp.einsum("hqk,qhd->kd", score_grad, queries, preferred_element_type=f32)
    both_grad = jnp.concatenate([key_grad, value_grad], axis=1)
    from_next = passed_along(both_grad[:tok].astype(bf16), "dp", -1)
    both_total = both_grad[tok:] + from_next.astype(f32)
    _, back_query = jax.vjp(query_map, query_raw, head_gains[0])
    query_raw_grad, grad_hq = back_query(query_grad)
    _, back_key = jax.vjp(key_map, key_raw, head_gains[1])
    key_raw_grad, grad_hk = back_key(both_total[:, :HD])
    _, back_value = jax.vjp(value_map, value_raw)
    value_raw_grad = back_value(both_total[:, HD:])[0]
    low_q = query_raw_grad.reshape(tok, -1).astype(bf16)
    low_k = key_raw_grad.astype(bf16)
    low_v = value_raw_grad.astype(bf16)
    attn_part = against(low_q, wq) + against(low_k, wk) + against(low_v, wv)
    in_attn = folded(attn_part.astype(bf16), "tensor")
    normal_grad = in_attn + against(low_rank_grad, wl) + shared
    _, back_in = jax.vjp(normed, inputs, gains_f[0])
    in_part, grad_g0 = back_in(normal_grad)
    input_grad = shared + in_part

    s_gateup = lax.psum_scatter(
        jnp.stack([across(all_mid, low_gate, bf16), across(all_mid, low_up, bf16)]),
        "dp",
        scatter_dimension=1,
        tiled=True,
    )
    s_down = lax.psum_scatter(
        across(low_hidden, all_feed, bf16), "dp", scatter_dimension=1, tiled=True
    )
    gain_part = jnp.stack([grad_g1, grad_g2, grad_g3, grad_g4, grad_g5]).astype(bf16)
    gain_part = jnp.pad(gain_part, ((0, LANES - 5), (0, 0))).T
    small = jnp.concatenate(
        [grad_left, grad_right, grad_pergate, grad_perproj, gain_part], axis=1
    )
    s_small = lax.psum_scatter(small, "dp", scatter_dimension=0, tiled=True)
    attn_grads = jnp.concatenate(
        [
            across(all_in, low_q, bf16),
            across(all_in, low_k, bf16),
            across(all_in, low_v, bf16),
            across(all_branch, low_att, bf16),
        ],
        axis=1,
    )
    s_attn = lax.psum_scatter(attn_grads, "dp", scatter_dimension=0, tiled=True)

    shard_gateup = s_gateup.astype(f32)
    shard_down = s_down.astype(f32)
    small_sum = butterfly(s_small.astype(f32), "tensor")
    o_left, o_right, o_gate, o_proj = (
        rank,
        2 * rank,
        2 * rank + per_width,
        2 * rank + 2 * per_width,
    )
    shard_left = small_sum[:, :o_left]
    shard_right = small_sum[:, o_left:o_right].T
    shard_pergate = small_sum[:, o_right:o_gate]
    shard_perproj = small_sum[:, o_gate:o_proj].T
    gains_rest = small_sum[:, o_proj : o_proj + 5].T
    g0_sum = butterfly(grad_g0, "tensor")
    g0_own = lax.psum_scatter(g0_sum.reshape(1, -1), "dp", scatter_dimension=1, tiled=True)
    shard_gains = jnp.concatenate([g0_own, gains_rest], axis=0)
    shard_query = s_attn[:, :q_width].astype(f32)
    kv_part = s_attn[:, q_width : q_width + 2 * HD]
    shard_out = s_attn[:, q_width + 2 * HD :].T.astype(f32)
    group = parts // KVH
    bit = 1
    kv_sum = kv_part
    while bit < group:
        kv_sum = (kv_sum.astype(f32) + crossed(kv_sum, "tensor", bit).astype(f32)).astype(bf16)
        bit *= 2
    kv_other = crossed(kv_sum, "tensor", group)
    upper = part // group == 1
    low_head = jnp.where(upper, kv_other, kv_sum).astype(f32)
    high_head = jnp.where(upper, kv_sum, kv_other).astype(f32)
    shard_keyval = jnp.stack(
        [
            jnp.concatenate([low_head[:, :HD], high_head[:, :HD]], axis=1),
            jnp.concatenate([low_head[:, HD:], high_head[:, HD:]], axis=1),
        ]
    )
    head_total = butterfly(butterfly(jnp.stack([grad_hq, grad_hk]), "tensor"), "dp")

    def home(rows_own):
        arrived = lax.all_to_all(across(receiver, rows_own, bf16), "dp", 0, 0, tiled=True)
        shared_rows = spread(product(compact, arrived, bf16), "tensor")
        return product(homing, shared_rows, bf16)

    back_one = home(jnp.concatenate([result.astype(bf16), layer_grad.astype(bf16)], axis=1))
    back_two = home(input_grad.astype(bf16))
    return (
        back_one[:, :width].reshape(micro, block_rows, width),
        back_two.reshape(micro, block_rows, width),
        back_one[:, width:].reshape(micro, block_rows, per_width),
        shard_query,
        shard_keyval,
        shard_out,
        shard_left,
        shard_right,
        shard_gateup,
        shard_down,
        shard_pergate,
        shard_perproj,
        shard_gains,
        head_total,
    )


def solution(mesh):
    placed = (
        P(None, "dp", None),
        P(None, "dp", None),
        P(None, "dp", None),
        P(),
        P(),
        P("dp", "tensor"),
        P(None, "dp", None),
        P("tensor", "dp"),
        P("dp", None),
        P(None, "dp"),
        P(None, "dp", "tensor"),
        P("tensor", "dp"),
        P("dp", None),
        P(None, "dp"),
        P(None, "dp"),
        P(),
    )
    return jax.shard_map(
        body,
        mesh=mesh,
        in_specs=placed,
        out_specs=(
            P(None, "dp", None),
            P(None, "dp", None),
            P(None, "dp", None),
            P("dp", "tensor"),
            P(None, "dp", None),
            P("tensor", "dp"),
            P("dp", None),
            P(None, "dp"),
            P(None, "dp", "tensor"),
            P("tensor", "dp"),
            P("dp", None),
            P(None, "dp"),
            P(None, "dp"),
            P(),
        ),
        check_vma=False,
    )
```

time: 1880 us -> 974 us (0.52)
  waiting for transfers between devices: 1200 us -> 471 us
  blocking collectives: 230 us -> 0 us
  starting transfers between devices: 27.4 us -> 217 us
  local copies, waits for them, and re-layouts: 116 us -> 45.2 us
  other arithmetic: 117 us -> 54.8 us
    psum x4 -> x0, waiting for transfers between devices: 528 us -> none  [the longest x1 167 us: body(): in_attn = lax.psum(attn_part, 'tensor')]
    reduce_scatter x10 -> x4, waiting for transfers between devices: 463 us -> 68.5 us  [the longest x1 68.5 us: body(): lax.psum_scatter(jnp.stack([across(all_mid, low_gate, bf16), across(all_m...]
    ppermute x0 -> x41, waiting for transfers between devices: none -> 323 us  [the longest x30 260 us: shifted(): lax.ppermute(piece, axis, [(i, (i + by) % length) for i in range(length)])]
    ppermute x0 -> x41, starting transfers between devices: none -> 144 us  [the longest x30 100 us: shifted(): lax.ppermute(piece, axis, [(i, (i + by) % length) for i in range(length)])]
    all_gather x7 -> x3, waiting for transfers between devices: 157 us -> 35.3 us  [the longest x1 35.3 us: body(): lax.all_gather(jnp.concatenate(bundle, axis=1), 'dp', axis=0, tiled=True)]
    all_gather x3 -> x0, blocking collectives: 81.5 us -> none  [the longest x1 61.1 us: body(): lax.all_gather(gains.astype(jnp.bfloat16), 'dp', axis=1, tiled=True)]
    psum x1 -> x0, blocking collectives: 80 us -> none  [body(): head_total = lax.psum(grad_heads, ('dp', 'tensor'))]
    gather x16 -> x2, local copies, waits for them, and re-layouts: 77.3 us -> 1.28 us  [the longest x1 0.64 us: plan(): shift_given = jnp.take(dealt_start, order) - given_start]
  transfers between devices with their start and end apart: 29 -> 55, of which waited for: 15 -> 28; matrix products, arithmetic and copies ran while one was open for 15% -> 20% of each run, Pallas kernels for 0% -> 0%
where the time goes in v1:
time: 974 us; the launch traced here: 966 us
  waiting for transfers between devices  471 us (48%)
  starting transfers between devices  217 us (22%)
  matrix products  162 us (17%)
  other arithmetic  54.8 us (6%)
  local copies, waits for them, and re-layouts  45.2 us (5%)
  between operations  16.6 us (2%)
    ppermute x30, waiting for transfers between devices, shifted(): lax.ppermute(piece, axis, [(i, (i + by) % length) for i in range(length)])  260 us
    ppermute x30, starting transfers between devices, shifted(): lax.ppermute(piece, axis, [(i, (i + by) % length) for i in range(length)])  100 us
    reduce_scatter x1, waiting for transfers between devices, body(): lax.psum_scatter(jnp.stack([across(all_mid, low_gate, bf16), across(all_m...  68.5 us
    dot_general x18, matrix products, product(): return jnp.dot(left_mat, right_mat, preferred_element_type=f32).astype(kind)  67 us
    ppermute x11, waiting for transfers between devices, crossed(): return lax.ppermute(piece, axis, [(i, i ^ bit) for i in range(length)])  63.2 us
    dot_general x12, matrix products, against(): lax.dot_general(left_mat, right_mat, (((1,), (1,)), ((), ())), preferred_...  48.6 us
    ppermute x11, starting transfers between devices, crossed(): return lax.ppermute(piece, axis, [(i, i ^ bit) for i in range(length)])  44.3 us
    dot_general x13, matrix products, across(): lax.dot_general(left_mat, right_mat, (((0,), (0,)), ((), ())), preferred_...  41.5 us
  transfers between devices with their start and end apart: 55, of which 28 were waited for; matrix products, arithmetic and copies ran while one was open for 20% of the time, Pallas kernels for 0%

profile of v1, /device:TPU:0, one launch (start us, length us, event | category | flops | bytes accessed | tf_op | source)
XLA Modules:
  0.0 965.7 jit_solution(14672695069873735812)
XLA Ops:
  26.3 5.2 all-to-all-start
  33.7 23.2 %all-to-all-done = bf16[8,40,2048]{2,1,0:T(8,128)(2,1)S(1)} async-done(((bf16[8,40,2048]{2,1,0:T(8,128)(2,1)}), bf16[8,40,2048]{2,1,0:T(8,128)(2,1)S(1)}, u32[]{:S(2)}, u32[]{:S(2)}) %all-to-all-start) | async-done | bytes 1310752 | tf_op jit(solution)/shard_map/all_to_all | solution.py:258
  58.0 35.3 %all-gather.4.cloned.1.call-done = bf16[2048,2304]{0,1:T(8,128)(2,1)} async-done(((bf16[256,2304]{0,1:T(8,128)(2,1)}), bf16[2048,2304]{0,1:T(8,128)(2,1)}) %all-gather.4.cloned.1.call-update) | async-done | bytes 9437200 | tf_op jit(solution)/shard_map/all_gather | solution.py:238
  102.4 9.7 %collective-permute-done = bf16[128,2048]{1,0:T(8,128)(2,1)S(1)} collective-permute-done((bf16[128,2048]{1,0:T(8,128)(2,1)S(1)}, bf16[128,2048]{1,0:T(8,128)(2,1)S(1)}, u32[]{:S(2)}, u32[]{:S(2)}) %collective-permute-start) | collective-permute-done | bytes 524320 | tf_op jit(solution)/shard_map/ppermute | solution.py:73
  112.0 21.8 %collective-permute-done.1 = bf16[128,2048]{1,0:T(8,128)(2,1)S(1)} collective-permute-done((bf16[128,2048]{1,0:T(8,128)(2,1)S(1)}, bf16[128,2048]{1,0:T(8,128)(2,1)S(1)}, u32[]{:S(2)}, u32[]{:S(2)}) %collective-permute-start.1) | collective-permute-done | bytes 524320 | tf_op jit(solution)/shard_map/ppermute | solution.py:73
  133.9 4.3 multiply_reduce_fusion.17
  162.5 12.9 %collective-permute-start.4 = (bf16[128,2048]{1,0:T(8,128)(2,1)S(1)}, bf16[128,2048]{1,0:T(8,128)(2,1)S(1)}, u32[]{:S(2)}, u32[]{:S(2)}) collective-permute-start(bf16[128,2048]{1,0:T(8,128)(2,1)S(1)} %get-tuple-element.116), channel_id=1, source_target_pairs={{0,3},{1,0},{2,1},{3,2},{4,7},{5,4},{6,5},{7,6},{8,11},{9,8},{10,9... | collective-permute-start | bytes 1572872 | tf_op jit(solution)/shard_map/ppermute | solution.py:73
  182.2 34.2 %collective-permute-done.5 = bf16[128,2048]{1,0:T(8,128)(2,1)S(1)} collective-permute-done((bf16[128,2048]{1,0:T(8,128)(2,1)S(1)}, bf16[128,2048]{1,0:T(8,128)(2,1)S(1)}, u32[]{:S(2)}, u32[]{:S(2)}) %collective-permute-start.5) | collective-permute-done | bytes 524320 | tf_op jit(solution)/shard_map/ppermute | solution.py:73
  225.7 23.3 %all-to-all-start.1 = ((bf16[8,40,2304]{2,1,0:T(8,128)(2,1)}), bf16[8,40,2304]{2,1,0:T(8,128)(2,1)}, u32[]{:S(2)}, u32[]{:S(2)}) async-start(bf16[8,40,2304]{2,1,0:T(8,128)(2,1)} %bitcast.169), calls=%async_computation.1 | async-start | bytes 2949120 | tf_op jit(solution)/shard_map/all_to_all | solution.py:259
  249.5 8.1 collective-permute-done.8
  257.7 10.7 %fusion.2 = f32[512,2048]{1,0:T(8,128)} fusion(bf16[2,2048,2048]{2,1,0:T(8,128)(2,1)} %all-gather.6.cloned.1.call-done, bf16[128,2048]{1,0:T(8,128)(2,1)} %collective-permute-done.9, bf16[128,2048]{1,0:T(8,128)(2,1)} %collective-permute-done.8, bf16[128,2048]{1,0:T(8,128)(2,1)} %collective-permute-done.7, bf16[128,2048]{1,0:T(8,128)(2,1)} %multiply_convert_fusion.2), kind=kOutput, calls=%fused_computation.10 | convolution fusion | flops 4303355904 | bytes 14680064 | tf_op jit(solution)/shard_map/dot_general | solution.py:51
  268.3 10.8 %multiply_convert_fusion.1 = (bf16[512,2048]{1,0:T(8,128)(2,1)}, f32[512,2048]{1,0:T(8,128)}) fusion(f32[512,2048]{1,0:T(8,128)} %fusion.2, bf16[2,2048,2048]{2,1,0:T(8,128)(2,1)S(1)} %copy-done.111, bf16[128,2048]{1,0:T(8,128)(2,1)} %collective-permute-done.9, bf16[128,2048]{1,0:T(8,128)(2,1)} %collective-permute-done.8, ...), kind=kOutput, calls=%fused_computation.39 | convolution fusion | flops 4313841664 | bytes 20971520 | tf_op jit(solution)/shard_map/dot_general | solution.py:51
  279.1 8.5 convolution_convert_fusion.9
  290.1 9.6 collective-permute-start.10
  305.3 9.3 collective-permute-done.10
  314.6 34.9 %collective-permute-done.11 = bf16[128,2048]{1,0:T(8,128)(2,1)} collective-permute-done((bf16[128,2048]{1,0:T(8,128)(2,1)}, bf16[128,2048]{1,0:T(8,128)(2,1)}, u32[]{:S(2)}, u32[]{:S(2)}) %collective-permute-start.11) | collective-permute-done | bytes 524320 | tf_op jit(solution)/shard_map/ppermute | solution.py:73
  361.6 3.9 collective-permute-start.18
  365.5 12.8 %collective-permute-done.16 = bf16[128,2048]{1,0:T(8,128)(2,1)S(1)} collective-permute-done((bf16[128,2048]{1,0:T(8,128)(2,1)S(1)}, bf16[128,2048]{1,0:T(8,128)(2,1)S(1)}, u32[]{:S(2)}, u32[]{:S(2)}) %collective-permute-start.16) | collective-permute-done | bytes 524320 | tf_op jit(solution)/shard_map/ppermute | solution.py:73
  378.2 21.1 %collective-permute-done.17 = bf16[128,2048]{1,0:T(8,128)(2,1)S(1)} collective-permute-done((bf16[128,2048]{1,0:T(8,128)(2,1)S(1)}, bf16[128,2048]{1,0:T(8,128)(2,1)S(1)}, u32[]{:S(2)}, u32[]{:S(2)}) %collective-permute-start.17) | collective-permute-done | bytes 524320 | tf_op jit(solution)/shard_map/ppermute | solution.py:73
  399.3 15.2 %multiply_convert_fusion = (bf16[512,2048]{1,0:T(8,128)(2,1)}, bf16[512,2048]{1,0:T(8,128)(2,1)}) fusion(f32[512,2048]{1,0:T(8,128)} %fusion.2, f32[512,2048]{1,0:T(8,128)} %get-tuple-element.184, bf16[2048,2048]{1,0:T(8,128)(2,1)} %all-gather.8.cloned.1.call-done, bf16[128,2048]{1,0:T(8,128)(2,1)S(1)} %collective-permute-done.18, ...), kind=kOutput, calls=%fused_computation.38 | convolution fusion | flops 4328521728 | bytes 23068672 | tf_op jit(solution)/shard_map/dot_general | solution.py:55
  414.5 7.8 fusion.1
  422.3 8.5 add_convert_fusion.1
  431.0 10.7 %collective-permute-start.19 = (bf16[128,2048]{1,0:T(8,128)(2,1)S(1)}, bf16[128,2048]{1,0:T(8,128)(2,1)S(1)}, u32[]{:S(2)}, u32[]{:S(2)}) collective-permute-start(bf16[128,2048]{1,0:T(8,128)(2,1)S(1)} %get-tuple-element.110), channel_id=1, source_target_pairs={{0,3},{1,0},{2,1},{3,2},{4,7},{5,4},{6,5},{7,6},{8,11},{9,8},{10,9... | collective-permute-start | bytes 1572872 | tf_op jit(solution)/shard_map/ppermute | solution.py:73
  443.8 10.4 %collective-permute-done.19 = bf16[128,2048]{1,0:T(8,128)(2,1)S(1)} collective-permute-done((bf16[128,2048]{1,0:T(8,128)(2,1)S(1)}, bf16[128,2048]{1,0:T(8,128)(2,1)S(1)}, u32[]{:S(2)}, u32[]{:S(2)}) %collective-permute-start.19) | collective-permute-done | bytes 524320 | tf_op jit(solution)/shard_map/ppermute | solution.py:73
  454.1 33.7 %collective-permute-done.20 = bf16[128,2048]{1,0:T(8,128)(2,1)S(1)} collective-permute-done((bf16[128,2048]{1,0:T(8,128)(2,1)S(1)}, bf16[128,2048]{1,0:T(8,128)(2,1)S(1)}, u32[]{:S(2)}, u32[]{:S(2)}) %collective-permute-start.20) | collective-permute-done | bytes 524320 | tf_op jit(solution)/shard_map/ppermute | solution.py:73
  507.4 19.8 %collective-permute-done.23 = bf16[128,2048]{1,0:T(8,128)(2,1)} collective-permute-done((bf16[128,2048]{1,0:T(8,128)(2,1)S(1)}, bf16[128,2048]{1,0:T(8,128)(2,1)}, u32[]{:S(2)}, u32[]{:S(2)}) %collective-permute-start.23) | collective-permute-done | bytes 524320 | tf_op jit(solution)/shard_map/ppermute | solution.py:73
  554.5 12.0 %collective-permute-start.26 = (bf16[128,2048]{1,0:T(8,128)(2,1)S(1)}, bf16[128,2048]{1,0:T(8,128)(2,1)S(1)}, u32[]{:S(2)}, u32[]{:S(2)}) collective-permute-start(bf16[128,2048]{1,0:T(8,128)(2,1)S(1)} %get-tuple-element.107), channel_id=1, source_target_pairs={{0,3},{1,0},{2,1},{3,2},{4,7},{5,4},{6,5},{7,6},{8,11},{9,8},{10,9... | collective-permute-start | bytes 1572872 | tf_op jit(solution)/shard_map/ppermute | solution.py:73
  570.2 4.1 convolution_convert_fusion.6
  574.3 17.3 %collective-permute-done.27 = bf16[128,2048]{1,0:T(8,128)(2,1)S(1)} collective-permute-done((bf16[128,2048]{1,0:T(8,128)(2,1)S(1)}, bf16[128,2048]{1,0:T(8,128)(2,1)S(1)}, u32[]{:S(2)}, u32[]{:S(2)}) %collective-permute-start.27) | collective-permute-done | bytes 524320 | tf_op jit(solution)/shard_map/ppermute | solution.py:73
  593.3 11.0 %collective-permute-start.36 = (f32[2048]{0:T(1024)S(1)}, f32[2048]{0:T(1024)S(1)}, u32[]{:S(2)}, u32[]{:S(2)}) collective-permute-start(f32[2048]{0:T(1024)S(1)} %get-tuple-element.75), channel_id=1, source_target_pairs={{0,1},{1,0},{2,3},{3,2},{4,5},{5,4},{6,7},{7,6},{8,9},{9,8},{10,11... | collective-permute-start | bytes 24584 | tf_op jit(solution)/shard_map/ppermute | solution.py:78
  613.3 5.9 pad_maximum_fusion.1
  619.3 10.1 %convolution_convert_fusion = bf16[2048,2048]{1,0:T(8,128)(2,1)} fusion(bf16[512,2048]{1,0:T(8,128)(2,1)} %get-tuple-element.183, bf16[128,2048]{1,0:T(8,128)(2,1)} %copy-done.120, bf16[128,2048]{1,0:T(8,128)(2,1)} %copy-done.119, bf16[128,2048]{1,0:T(8,128)(2,1)} %copy-done.118, bf16[128,2048]{1,0:T(8,128)(2,1)} %copy-done.42), kind=kOutput, calls=%fused_computation.8 | convolution fusion | flops 4307550208 | bytes 12582912 | tf_op jit(solution)/shard_map/dot_general | solution.py:61
  629.6 6.8 convert_bitcast_fusion.1
  636.5 6.8 convert_bitcast_fusion
  643.3 6.7 pad_maximum_fusion
  653.7 35.5 %all-to-all-start.2 = ((bf16[8,40,2304]{2,1,0:T(8,128)(2,1)}), bf16[8,40,2304]{2,1,0:T(8,128)(2,1)}, u32[]{:S(2)}, u32[]{:S(2)}) async-start(bf16[8,40,2304]{2,1,0:T(8,128)(2,1)} %bitcast.170), calls=%async_computation.2 | async-start | bytes 2949120 | tf_op jit(solution)/shard_map/all_to_all | solution.py:446
  691.0 18.3 %all-to-all-done.2 = bf16[8,40,2304]{2,1,0:T(8,128)(2,1)} async-done(((bf16[8,40,2304]{2,1,0:T(8,128)(2,1)}), bf16[8,40,2304]{2,1,0:T(8,128)(2,1)}, u32[]{:S(2)}, u32[]{:S(2)}) %all-to-all-start.2) | async-done | bytes 1474592 | tf_op jit(solution)/shard_map/all_to_all | solution.py:446
  725.4 22.5 %collective-permute-done.39 = f32[2,256]{1,0:T(2,128)S(1)} collective-permute-done((f32[2,256]{1,0:T(2,128)S(1)}, f32[2,256]{1,0:T(2,128)S(1)}, u32[]{:S(2)}, u32[]{:S(2)}) %collective-permute-start.39) | collective-permute-done | bytes 2080 | tf_op jit(solution)/shard_map/ppermute | solution.py:78
  756.4 7.3 collective-permute-start.30
  763.7 14.2 %collective-permute-start.31 = (bf16[136,2048]{1,0:T(8,128)(2,1)}, bf16[136,2048]{1,0:T(8,128)(2,1)}, u32[]{:S(2)}, u32[]{:S(2)}) collective-permute-start(bf16[136,2048]{1,0:T(8,128)(2,1)} %convolution_convert_fusion.16), channel_id=1, source_target_pairs={{0,3},{1,0},{2,1},{3,2},{4,7},{5,4},{6,5},{7,6},{8,11},{9,8},{10,9... | collective-permute-start | bytes 1671176 | tf_op jit(solution)/shard_map/ppermute | solution.py:73
  781.2 20.9 %collective-permute-start.35 = (f32[256,768]{0,1:T(8,128)S(1)}, f32[256,768]{0,1:T(8,128)S(1)}, u32[]{:S(2)}, u32[]{:S(2)}) collective-permute-start(f32[256,768]{0,1:T(8,128)S(1)} %convert_add_fusion.3), channel_id=1, source_target_pairs={{0,2},{1,3},{2,0},{3,1},{4,6},{5,7},{6,4},{7,5},{8,10},{9,11},{10,... | collective-permute-start | bytes 2359304 | tf_op jit(solution)/shard_map/ppermute | solution.py:78
  809.5 21.9 %collective-permute-done.30 = bf16[136,2048]{1,0:T(8,128)(2,1)} collective-permute-done((bf16[136,2048]{1,0:T(8,128)(2,1)}, bf16[136,2048]{1,0:T(8,128)(2,1)}, u32[]{:S(2)}, u32[]{:S(2)}) %collective-permute-start.30) | collective-permute-done | bytes 557088 | tf_op jit(solution)/shard_map/ppermute | solution.py:73
  831.4 4.8 convolution_convert_fusion.8
  836.2 22.4 %collective-permute-done.35 = f32[256,768]{0,1:T(8,128)S(1)} collective-permute-done((f32[256,768]{0,1:T(8,128)S(1)}, f32[256,768]{0,1:T(8,128)S(1)}, u32[]{:S(2)}, u32[]{:S(2)}) %collective-permute-start.35) | collective-permute-done | bytes 786464 | tf_op jit(solution)/shard_map/ppermute | solution.py:78
  861.6 6.2 collective-permute-done.32
  873.1 8.5 collective-permute-done.33
  886.0 68.5 %reduce-scatter.12.cloned.1.call-done = bf16[2,256,2048]{2,1,0:T(8,128)(2,1)} async-done(((bf16[2,2048,2048]{2,1,0:T(8,128)(2,1)}), bf16[2,256,2048]{2,1,0:T(8,128)(2,1)}) %reduce-scatter.12.cloned.1.call-update) | async-done | bytes 2097168 | tf_op jit(solution)/shard_map/reduce_scatter | solution.py:381
  954.5 4.1 convert_element_type.385
  (526 shorter events, 208.1 us)
Async XLA Ops:
  7.2 86.2 %all-gather.4.cloned.1.call-start = ((), (), s32[]{:S(2)}) async-start(), calls=%async_computation.9 | async-start | bytes 10616832 | tf_op jit(solution)/shard_map/all_gather | solution.py:238
  15.9 241.8 %all-gather.6.cloned.1.call-start = ((), (), s32[]{:S(2)}) async-start(), calls=%async_computation.10 | async-start | bytes 18874368 | tf_op jit(solution)/shard_map/all_gather | solution.py:242
  26.3 30.6 %all-to-all-start = ((bf16[8,40,2048]{2,1,0:T(8,128)(2,1)}), bf16[8,40,2048]{2,1,0:T(8,128)(2,1)S(1)}, u32[]{:S(2)}, u32[]{:S(2)}) async-start(bf16[8,40,2048]{2,1,0:T(8,128)(2,1)} %bitcast.7), calls=%async_computation | async-start | bytes 2621440 | tf_op jit(solution)/shard_map/all_to_all | solution.py:258
  31.5 247.6 %all-gather.8.cloned.1.call-start = ((), (), s32[]{:S(2)}) async-start(), calls=%async_computation.11 | async-start | bytes 9437184 | tf_op jit(solution)/shard_map/all_gather | solution.py:244
  95.3 16.7 %collective-permute-start = (bf16[128,2048]{1,0:T(8,128)(2,1)S(1)}, bf16[128,2048]{1,0:T(8,128)(2,1)S(1)}, u32[]{:S(2)}, u32[]{:S(2)}) collective-permute-start(bf16[128,2048]{1,0:T(8,128)(2,1)S(1)} %multiply_convert_fusion.3), channel_id=1, source_target_pairs={{0,1},{1,2},{2,3},{3,0},{4,5},{5,6},{6,7},{7,4},{8,9},{9,10},{10,1... | collective-permute-start | bytes 1572872 | tf_op jit(solution)/shard_map/ppermute | solution.py:73
  96.8 37.0 %collective-permute-start.1 = (bf16[128,2048]{1,0:T(8,128)(2,1)S(1)}, bf16[128,2048]{1,0:T(8,128)(2,1)S(1)}, u32[]{:S(2)}, u32[]{:S(2)}) collective-permute-start(bf16[128,2048]{1,0:T(8,128)(2,1)S(1)} %multiply_convert_fusion.3), channel_id=1, source_target_pairs={{0,2},{1,3},{2,0},{3,1},{4,6},{5,7},{6,4},{7,5},{8,10},{9,11},{10,... | collective-permute-start | bytes 1572872 | tf_op jit(solution)/shard_map/ppermute | solution.py:73
  99.2 34.6 %collective-permute-start.2 = (bf16[128,2048]{1,0:T(8,128)(2,1)S(1)}, bf16[128,2048]{1,0:T(8,128)(2,1)S(1)}, u32[]{:S(2)}, u32[]{:S(2)}) collective-permute-start(bf16[128,2048]{1,0:T(8,128)(2,1)S(1)} %multiply_convert_fusion.3), channel_id=1, source_target_pairs={{0,3},{1,0},{2,1},{3,2},{4,7},{5,4},{6,5},{7,6},{8,11},{9,8},{10,9... | collective-permute-start | bytes 1572872 | tf_op jit(solution)/shard_map/ppermute | solution.py:73
  162.5 19.6 %collective-permute-start.4 = (bf16[128,2048]{1,0:T(8,128)(2,1)S(1)}, bf16[128,2048]{1,0:T(8,128)(2,1)S(1)}, u32[]{:S(2)}, u32[]{:S(2)}) collective-permute-start(bf16[128,2048]{1,0:T(8,128)(2,1)S(1)} %get-tuple-element.116), channel_id=1, source_target_pairs={{0,3},{1,0},{2,1},{3,2},{4,7},{5,4},{6,5},{7,6},{8,11},{9,8},{10,9... | collective-permute-start | bytes 1572872 | tf_op jit(solution)/shard_map/ppermute | solution.py:73
  175.4 41.0 %collective-permute-start.5 = (bf16[128,2048]{1,0:T(8,128)(2,1)S(1)}, bf16[128,2048]{1,0:T(8,128)(2,1)S(1)}, u32[]{:S(2)}, u32[]{:S(2)}) collective-permute-start(bf16[128,2048]{1,0:T(8,128)(2,1)S(1)} %get-tuple-element.118), channel_id=1, source_target_pairs={{0,2},{1,3},{2,0},{3,1},{4,6},{5,7},{6,4},{7,5},{8,10},{9,11},{10,... | collective-permute-start | bytes 1572872 | tf_op jit(solution)/shard_map/ppermute | solution.py:73
  175.5 40.9 %collective-permute-start.6 = (bf16[128,2048]{1,0:T(8,128)(2,1)S(1)}, bf16[128,2048]{1,0:T(8,128)(2,1)S(1)}, u32[]{:S(2)}, u32[]{:S(2)}) collective-permute-start(bf16[128,2048]{1,0:T(8,128)(2,1)S(1)} %get-tuple-element.117), channel_id=1, source_target_pairs={{0,1},{1,2},{2,3},{3,0},{4,5},{5,6},{6,7},{7,4},{8,9},{9,10},{10,1... | collective-permute-start | bytes 1572872 | tf_op jit(solution)/shard_map/ppermute | solution.py:73
  219.1 30.5 %collective-permute-start.7 = (bf16[128,2048]{1,0:T(8,128)(2,1)}, bf16[128,2048]{1,0:T(8,128)(2,1)}, u32[]{:S(2)}, u32[]{:S(2)}) collective-permute-start(bf16[128,2048]{1,0:T(8,128)(2,1)} %multiply_convert_fusion.2), channel_id=1, source_target_pairs={{0,1},{1,2},{2,3},{3,0},{4,5},{5,6},{6,7},{7,4},{8,9},{9,10},{10,1... | collective-permute-start | bytes 1572872 | tf_op jit(solution)/shard_map/ppermute | solution.py:73
  219.6 38.0 %collective-permute-start.8 = (bf16[128,2048]{1,0:T(8,128)(2,1)}, bf16[128,2048]{1,0:T(8,128)(2,1)}, u32[]{:S(2)}, u32[]{:S(2)}) collective-permute-start(bf16[128,2048]{1,0:T(8,128)(2,1)} %multiply_convert_fusion.2), channel_id=1, source_target_pairs={{0,2},{1,3},{2,0},{3,1},{4,6},{5,7},{6,4},{7,5},{8,10},{9,11},{10,... | collective-permute-start | bytes 1572872 | tf_op jit(solution)/shard_map/ppermute | solution.py:73
  221.6 36.0 %collective-permute-start.9 = (bf16[128,2048]{1,0:T(8,128)(2,1)}, bf16[128,2048]{1,0:T(8,128)(2,1)}, u32[]{:S(2)}, u32[]{:S(2)}) collective-permute-start(bf16[128,2048]{1,0:T(8,128)(2,1)} %multiply_convert_fusion.2), channel_id=1, source_target_pairs={{0,3},{1,0},{2,1},{3,2},{4,7},{5,4},{6,5},{7,6},{8,11},{9,8},{10,9... | collective-permute-start | bytes 1572872 | tf_op jit(solution)/shard_map/ppermute | solution.py:73
  225.7 77.7 %all-to-all-start.1 = ((bf16[8,40,2304]{2,1,0:T(8,128)(2,1)}), bf16[8,40,2304]{2,1,0:T(8,128)(2,1)}, u32[]{:S(2)}, u32[]{:S(2)}) async-start(bf16[8,40,2304]{2,1,0:T(8,128)(2,1)} %bitcast.169), calls=%async_computation.1 | async-start | bytes 2949120 | tf_op jit(solution)/shard_map/all_to_all | solution.py:259
  249.0 464.4 %reduce-scatter.10.cloned.1.call-start = ((), (), s32[]{:S(2)}) async-start(), calls=%async_computation.13 | async-start | bytes 3538944 | tf_op jit(solution)/shard_map/reduce_scatter | solution.py:395
  290.1 24.5 %collective-permute-start.10 = (bf16[128,2048]{1,0:T(8,128)(2,1)}, bf16[128,2048]{1,0:T(8,128)(2,1)}, u32[]{:S(2)}, u32[]{:S(2)}) collective-permute-start(bf16[128,2048]{1,0:T(8,128)(2,1)} %get-tuple-element.113), channel_id=1, source_target_pairs={{0,3},{1,0},{2,1},{3,2},{4,7},{5,4},{6,5},{7,6},{8,11},{9,8},{10,9... | collective-permute-start | bytes 1572872 | tf_op jit(solution)/shard_map/ppermute | solution.py:73
  299.7 49.8 %collective-permute-start.11 = (bf16[128,2048]{1,0:T(8,128)(2,1)}, bf16[128,2048]{1,0:T(8,128)(2,1)}, u32[]{:S(2)}, u32[]{:S(2)}) collective-permute-start(bf16[128,2048]{1,0:T(8,128)(2,1)} %get-tuple-element.115), channel_id=1, source_target_pairs={{0,2},{1,3},{2,0},{3,1},{4,6},{5,7},{6,4},{7,5},{8,10},{9,11},{10,... | collective-permute-start | bytes 1572872 | tf_op jit(solution)/shard_map/ppermute | solution.py:73
  303.4 46.2 %collective-permute-start.12 = (bf16[128,2048]{1,0:T(8,128)(2,1)}, bf16[128,2048]{1,0:T(8,128)(2,1)}, u32[]{:S(2)}, u32[]{:S(2)}) collective-permute-start(bf16[128,2048]{1,0:T(8,128)(2,1)} %get-tuple-element.114), channel_id=1, source_target_pairs={{0,1},{1,2},{2,3},{3,0},{4,5},{5,6},{6,7},{7,4},{8,9},{9,10},{10,1... | collective-permute-start | bytes 1572872 | tf_op jit(solution)/shard_map/ppermute | solution.py:73
  361.4 16.8 %collective-permute-start.16 = (bf16[128,2048]{1,0:T(8,128)(2,1)S(1)}, bf16[128,2048]{1,0:T(8,128)(2,1)S(1)}, u32[]{:S(2)}, u32[]{:S(2)}) collective-permute-start(bf16[128,2048]{1,0:T(8,128)(2,1)S(1)} %fusion.58), channel_id=1, source_target_pairs={{0,1},{1,2},{2,3},{3,0},{4,5},{5,6},{6,7},{7,4},{8,9},{9,10},{10,1... | collective-permute-start | bytes 1572872 | tf_op jit(solution)/shard_map/ppermute | solution.py:73
  361.5 37.8 %collective-permute-start.17 = (bf16[128,2048]{1,0:T(8,128)(2,1)S(1)}, bf16[128,2048]{1,0:T(8,128)(2,1)S(1)}, u32[]{:S(2)}, u32[]{:S(2)}) collective-permute-start(bf16[128,2048]{1,0:T(8,128)(2,1)S(1)} %fusion.58), channel_id=1, source_target_pairs={{0,2},{1,3},{2,0},{3,1},{4,6},{5,7},{6,4},{7,5},{8,10},{9,11},{10,... | collective-permute-start | bytes 1572872 | tf_op jit(solution)/shard_map/ppermute | solution.py:73
  361.6 37.7 %collective-permute-start.18 = (bf16[128,2048]{1,0:T(8,128)(2,1)S(1)}, bf16[128,2048]{1,0:T(8,128)(2,1)S(1)}, u32[]{:S(2)}, u32[]{:S(2)}) collective-permute-start(bf16[128,2048]{1,0:T(8,128)(2,1)S(1)} %fusion.58), channel_id=1, source_target_pairs={{0,3},{1,0},{2,1},{3,2},{4,7},{5,4},{6,5},{7,6},{8,11},{9,8},{10,9... | collective-permute-start | bytes 1572872 | tf_op jit(solution)/shard_map/ppermute | solution.py:73
  431.0 23.1 %collective-permute-start.19 = (bf16[128,2048]{1,0:T(8,128)(2,1)S(1)}, bf16[128,2048]{1,0:T(8,128)(2,1)S(1)}, u32[]{:S(2)}, u32[]{:S(2)}) collective-permute-start(bf16[128,2048]{1,0:T(8,128)(2,1)S(1)} %get-tuple-element.110), channel_id=1, source_target_pairs={{0,3},{1,0},{2,1},{3,2},{4,7},{5,4},{6,5},{7,6},{8,11},{9,8},{10,9... | collective-permute-start | bytes 1572872 | tf_op jit(solution)/shard_map/ppermute | solution.py:73
  441.7 46.1 %collective-permute-start.20 = (bf16[128,2048]{1,0:T(8,128)(2,1)S(1)}, bf16[128,2048]{1,0:T(8,128)(2,1)S(1)}, u32[]{:S(2)}, u32[]{:S(2)}) collective-permute-start(bf16[128,2048]{1,0:T(8,128)(2,1)S(1)} %get-tuple-element.112), channel_id=1, source_target_pairs={{0,2},{1,3},{2,0},{3,1},{4,6},{5,7},{6,4},{7,5},{8,10},{9,11},{10,... | collective-permute-start | bytes 1572872 | tf_op jit(solution)/shard_map/ppermute | solution.py:73
  443.1 44.6 %collective-permute-start.21 = (bf16[128,2048]{1,0:T(8,128)(2,1)S(1)}, bf16[128,2048]{1,0:T(8,128)(2,1)S(1)}, u32[]{:S(2)}, u32[]{:S(2)}) collective-permute-start(bf16[128,2048]{1,0:T(8,128)(2,1)S(1)} %get-tuple-element.111), channel_id=1, source_target_pairs={{0,1},{1,2},{2,3},{3,0},{4,5},{5,6},{6,7},{7,4},{8,9},{9,10},{10,1... | collective-permute-start | bytes 1572872 | tf_op jit(solution)/shard_map/ppermute | solution.py:73
  490.5 16.9 %collective-permute-start.22 = (bf16[128,2048]{1,0:T(8,128)(2,1)S(1)}, bf16[128,2048]{1,0:T(8,128)(2,1)}, u32[]{:S(2)}, u32[]{:S(2)}) collective-permute-start(bf16[128,2048]{1,0:T(8,128)(2,1)S(1)} %get-tuple-element.128), channel_id=1, source_target_pairs={{0,1},{1,2},{2,3},{3,0},{4,5},{5,6},{6,7},{7,4},{8,9},{9,10},{10,1... | collective-permute-start | bytes 1572872 | tf_op jit(solution)/shard_map/ppermute | solution.py:73
  490.5 36.6 %collective-permute-start.23 = (bf16[128,2048]{1,0:T(8,128)(2,1)S(1)}, bf16[128,2048]{1,0:T(8,128)(2,1)}, u32[]{:S(2)}, u32[]{:S(2)}) collective-permute-start(bf16[128,2048]{1,0:T(8,128)(2,1)S(1)} %get-tuple-element.128), channel_id=1, source_target_pairs={{0,2},{1,3},{2,0},{3,1},{4,6},{5,7},{6,4},{7,5},{8,10},{9,11},{10,... | collective-permute-start | bytes 1572872 | tf_op jit(solution)/shard_map/ppermute | solution.py:73
  491.4 35.7 %collective-permute-start.24 = (bf16[128,2048]{1,0:T(8,128)(2,1)S(1)}, bf16[128,2048]{1,0:T(8,128)(2,1)}, u32[]{:S(2)}, u32[]{:S(2)}) collective-permute-start(bf16[128,2048]{1,0:T(8,128)(2,1)S(1)} %get-tuple-element.128), channel_id=1, source_target_pairs={{0,3},{1,0},{2,1},{3,2},{4,7},{5,4},{6,5},{7,6},{8,11},{9,8},{10,9... | collective-permute-start | bytes 1572872 | tf_op jit(solution)/shard_map/ppermute | solution.py:73
  505.6 302.9 %reduce-scatter.16.cloned.1.call-start = ((), (), s32[]{:S(2)}) async-start(), calls=%async_computation.16 | async-start | bytes 1179648
  554.5 19.8 %collective-permute-start.26 = (bf16[128,2048]{1,0:T(8,128)(2,1)S(1)}, bf16[128,2048]{1,0:T(8,128)(2,1)S(1)}, u32[]{:S(2)}, u32[]{:S(2)}) collective-permute-start(bf16[128,2048]{1,0:T(8,128)(2,1)S(1)} %get-tuple-element.107), channel_id=1, source_target_pairs={{0,3},{1,0},{2,1},{3,2},{4,7},{5,4},{6,5},{7,6},{8,11},{9,8},{10,9... | collective-permute-start | bytes 1572872 | tf_op jit(solution)/shard_map/ppermute | solution.py:73
  566.4 25.1 %collective-permute-start.27 = (bf16[128,2048]{1,0:T(8,128)(2,1)S(1)}, bf16[128,2048]{1,0:T(8,128)(2,1)S(1)}, u32[]{:S(2)}, u32[]{:S(2)}) collective-permute-start(bf16[128,2048]{1,0:T(8,128)(2,1)S(1)} %get-tuple-element.109), channel_id=1, source_target_pairs={{0,2},{1,3},{2,0},{3,1},{4,6},{5,7},{6,4},{7,5},{8,10},{9,11},{10,... | collective-permute-start | bytes 1572872 | tf_op jit(solution)/shard_map/ppermute | solution.py:73
  566.9 24.7 %collective-permute-start.28 = (bf16[128,2048]{1,0:T(8,128)(2,1)S(1)}, bf16[128,2048]{1,0:T(8,128)(2,1)S(1)}, u32[]{:S(2)}, u32[]{:S(2)}) collective-permute-start(bf16[128,2048]{1,0:T(8,128)(2,1)S(1)} %get-tuple-element.108), channel_id=1, source_target_pairs={{0,1},{1,2},{2,3},{3,0},{4,5},{5,6},{6,7},{7,4},{8,9},{9,10},{10,1... | collective-permute-start | bytes 1572872 | tf_op jit(solution)/shard_map/ppermute | solution.py:73
  593.3 13.4 %collective-permute-start.36 = (f32[2048]{0:T(1024)S(1)}, f32[2048]{0:T(1024)S(1)}, u32[]{:S(2)}, u32[]{:S(2)}) collective-permute-start(f32[2048]{0:T(1024)S(1)} %get-tuple-element.75), channel_id=1, source_target_pairs={{0,1},{1,0},{2,3},{3,2},{4,5},{5,4},{6,7},{7,6},{8,9},{9,8},{10,11... | collective-permute-start | bytes 24584 | tf_op jit(solution)/shard_map/ppermute | solution.py:78
  613.3 245.4 %reduce-scatter.8.cloned.1.call-start = ((), (), s32[]{:S(2)}) async-start(), calls=%async_computation.12 | async-start | bytes 7077888 | tf_op jit(solution)/shard_map/reduce_scatter | solution.py:405
  619.3 263.9 %reduce-scatter.14.cloned.1.call-start = ((), (), s32[]{:S(2)}) async-start(), calls=%async_computation.15 | async-start | bytes 9437184 | tf_op jit(solution)/shard_map/reduce_scatter | solution.py:387
  629.4 325.1 %reduce-scatter.12.cloned.1.call-start = ((), (), s32[]{:S(2)}) async-start(), calls=%async_computation.14 | async-start | bytes 18874368 | tf_op jit(solution)/shard_map/reduce_scatter | solution.py:381
  653.7 55.6 %all-to-all-start.2 = ((bf16[8,40,2304]{2,1,0:T(8,128)(2,1)}), bf16[8,40,2304]{2,1,0:T(8,128)(2,1)}, u32[]{:S(2)}, u32[]{:S(2)}) async-start(bf16[8,40,2304]{2,1,0:T(8,128)(2,1)} %bitcast.170), calls=%async_computation.2 | async-start | bytes 2949120 | tf_op jit(solution)/shard_map/all_to_all | solution.py:446
  709.3 43.5 %all-to-all-start.3 = ((bf16[8,40,2048]{2,1,0:T(8,128)(2,1)}), bf16[8,40,2048]{2,1,0:T(8,128)(2,1)S(1)}, u32[]{:S(2)}, u32[]{:S(2)}) async-start(bf16[8,40,2048]{2,1,0:T(8,128)(2,1)} %bitcast.46), calls=%async_computation.3 | async-start | bytes 2621440 | tf_op jit(solution)/shard_map/all_to_all | solution.py:446
  714.5 49.2 %collective-permute-start.34 = (f32[256,768]{0,1:T(8,128)S(1)}, f32[256,768]{0,1:T(8,128)}, u32[]{:S(2)}, u32[]{:S(2)}) collective-permute-start(f32[256,768]{0,1:T(8,128)S(1)} %convert_element_type.382), channel_id=1, source_target_pairs={{0,1},{1,0},{2,3},{3,2},{4,5},{5,4},{6,7},{7,6},{8,9},{9,8},{10,11... | collective-permute-start | bytes 2359304 | tf_op jit(solution)/shard_map/ppermute | solution.py:78
  718.4 38.0 %collective-permute-start.13 = (bf16[136,2304]{1,0:T(8,128)(2,1)S(1)}, bf16[136,2304]{1,0:T(8,128)(2,1)}, u32[]{:S(2)}, u32[]{:S(2)}) collective-permute-start(bf16[136,2304]{1,0:T(8,128)(2,1)S(1)} %convolution_convert_fusion.4), channel_id=1, source_target_pairs={{0,1},{1,2},{2,3},{3,0},{4,5},{5,6},{6,7},{7,4},{8,9},{9,10},{10,1... | collective-permute-start | bytes 1880072 | tf_op jit(solution)/shard_map/ppermute | solution.py:73
  718.6 29.3 %collective-permute-start.39 = (f32[2,256]{1,0:T(2,128)S(1)}, f32[2,256]{1,0:T(2,128)S(1)}, u32[]{:S(2)}, u32[]{:S(2)}) collective-permute-start(f32[2,256]{1,0:T(2,128)S(1)} %fusion.192), channel_id=1, source_target_pairs={{0,2},{1,3},{2,0},{3,1},{4,6},{5,7},{6,4},{7,5},{8,10},{9,11},{10,... | collective-permute-start | bytes 6152 | tf_op jit(solution)/shard_map/ppermute | solution.py:78
  720.3 58.8 %collective-permute-start.14 = (bf16[136,2304]{1,0:T(8,128)(2,1)S(1)}, bf16[136,2304]{1,0:T(8,128)(2,1)}, u32[]{:S(2)}, u32[]{:S(2)}) collective-permute-start(bf16[136,2304]{1,0:T(8,128)(2,1)S(1)} %convolution_convert_fusion.4), channel_id=1, source_target_pairs={{0,2},{1,3},{2,0},{3,1},{4,6},{5,7},{6,4},{7,5},{8,10},{9,11},{10,... | collective-permute-start | bytes 1880072 | tf_op jit(solution)/shard_map/ppermute | solution.py:73
  721.6 59.6 %collective-permute-start.15 = (bf16[136,2304]{1,0:T(8,128)(2,1)S(1)}, bf16[136,2304]{1,0:T(8,128)(2,1)}, u32[]{:S(2)}, u32[]{:S(2)}) collective-permute-start(bf16[136,2304]{1,0:T(8,128)(2,1)S(1)} %convolution_convert_fusion.4), channel_id=1, source_target_pairs={{0,3},{1,0},{2,1},{3,2},{4,7},{5,4},{6,5},{7,6},{8,11},{9,8},{10,9... | collective-permute-start | bytes 1880072 | tf_op jit(solution)/shard_map/ppermute | solution.py:73
  754.0 55.5 %collective-permute-start.29 = (bf16[136,2048]{1,0:T(8,128)(2,1)}, bf16[136,2048]{1,0:T(8,128)(2,1)}, u32[]{:S(2)}, u32[]{:S(2)}) collective-permute-start(bf16[136,2048]{1,0:T(8,128)(2,1)} %convolution_convert_fusion.16), channel_id=1, source_target_pairs={{0,1},{1,2},{2,3},{3,0},{4,5},{5,6},{6,7},{7,4},{8,9},{9,10},{10,1... | collective-permute-start | bytes 1671176 | tf_op jit(solution)/shard_map/ppermute | solution.py:73
  756.4 75.0 %collective-permute-start.30 = (bf16[136,2048]{1,0:T(8,128)(2,1)}, bf16[136,2048]{1,0:T(8,128)(2,1)}, u32[]{:S(2)}, u32[]{:S(2)}) collective-permute-start(bf16[136,2048]{1,0:T(8,128)(2,1)} %convolution_convert_fusion.16), channel_id=1, source_target_pairs={{0,2},{1,3},{2,0},{3,1},{4,6},{5,7},{6,4},{7,5},{8,10},{9,11},{10,... | collective-permute-start | bytes 1671176 | tf_op jit(solution)/shard_map/ppermute | solution.py:73
  763.7 67.7 %collective-permute-start.31 = (bf16[136,2048]{1,0:T(8,128)(2,1)}, bf16[136,2048]{1,0:T(8,128)(2,1)}, u32[]{:S(2)}, u32[]{:S(2)}) collective-permute-start(bf16[136,2048]{1,0:T(8,128)(2,1)} %convolution_convert_fusion.16), channel_id=1, source_target_pairs={{0,3},{1,0},{2,1},{3,2},{4,7},{5,4},{6,5},{7,6},{8,11},{9,8},{10,9... | collective-permute-start | bytes 1671176 | tf_op jit(solution)/shard_map/ppermute | solution.py:73
  779.2 28.7 %collective-permute-start.42 = (f32[2,256]{1,0:T(2,128)S(1)}, f32[2,256]{1,0:T(2,128)S(1)}, u32[]{:S(2)}, u32[]{:S(2)}) collective-permute-start(f32[2,256]{1,0:T(2,128)S(1)} %add.721), channel_id=1, source_target_pairs={{0,16},{4,20},{8,24},{12,28},{16,0},{20,4},{24,8},{28,12},{1,17},{... | collective-permute-start | bytes 6152 | tf_op jit(solution)/shard_map/ppermute | solution.py:78
  781.2 77.4 %collective-permute-start.35 = (f32[256,768]{0,1:T(8,128)S(1)}, f32[256,768]{0,1:T(8,128)S(1)}, u32[]{:S(2)}, u32[]{:S(2)}) collective-permute-start(f32[256,768]{0,1:T(8,128)S(1)} %convert_add_fusion.3), channel_id=1, source_target_pairs={{0,2},{1,3},{2,0},{3,1},{4,6},{5,7},{6,4},{7,5},{8,10},{9,11},{10,... | collective-permute-start | bytes 2359304 | tf_op jit(solution)/shard_map/ppermute | solution.py:78
  868.7 12.8 %collective-permute-start.33 = (bf16[256,512]{0,1:T(8,128)(2,1)S(1)}, bf16[256,512]{0,1:T(8,128)(2,1)S(1)}, u32[]{:S(2)}, u32[]{:S(2)}) collective-permute-start(bf16[256,512]{0,1:T(8,128)(2,1)S(1)} %add_convert_fusion.3), channel_id=1, source_target_pairs={{0,2},{1,3},{2,0},{3,1},{4,6},{5,7},{6,4},{7,5},{8,10},{9,11},{10,... | collective-permute-start | bytes 786440 | tf_op jit(solution)/shard_map/ppermute | solution.py:78
  (132 other events, 2519.2 us)
Sparse Core Ops, SparseCore 0:
  16.0 77.3 all-gather.3
  95.3 94.7 all-gather.5
  191.9 55.9 all-gather.7
  505.7 63.9 reduce-scatter.9
  613.4 67.0 reduce-scatter.15
  684.1 75.6 reduce-scatter.7
  763.3 71.2 reduce-scatter.13
  838.5 115.9 reduce-scatter.11

commit v2 on v1

--- a/solution.py
+++ b/solution.py
@@ -1,6 +1,8 @@
 import jax
 import jax.numpy as jnp
 from jax import lax
+from jax.experimental import pallas as pl
+from jax.experimental.pallas import tpu as pltpu
 from jax.sharding import PartitionSpec as P
 
 KVH = 2
@@ -68,6 +70,261 @@
     return jnp.power(10000.0, -2.0 * jnp.arange(half_dim, dtype=f32) / HD)
 
 
+MIB = 1 << 20
+
+
+def small_cost(flops):
+    return pl.CostEstimate(flops=flops, bytes_accessed=1024, transcendentals=0)
+
+
+def whole(shape):
+    zeros = (0,) * len(shape)
+    return pl.BlockSpec(shape, lambda *_: zeros, pipeline_mode=pl.Buffered(1))
+
+
+def attend(queries, keys, values, low_bound, high_bound, key_place):
+    tok, total = queries.shape
+    heads = total // HD
+    span = keys.shape[0]
+    rows = 256
+
+    def kernel(q_ref, k_ref, v_ref, lo_ref, hi_ref, kp_ref, o_ref):
+        scores = against(q_ref[...], k_ref[...])
+        kp = kp_ref[...]
+        allowed = (kp >= lo_ref[...]) & (kp <= hi_ref[...])
+        masked = jnp.where(allowed, scores, masked_value)
+        raised = jnp.exp(masked - jnp.max(masked, axis=1, keepdims=True))
+        inverse = 1.0 / jnp.sum(raised, axis=1, keepdims=True)
+        o_ref[...] = product((raised * inverse).astype(bf16), v_ref[...], bf16)
+
+    return pl.pallas_call(
+        kernel,
+        out_shape=jax.ShapeDtypeStruct((tok, total), bf16),
+        grid=(heads, tok // rows),
+        in_specs=[
+            pl.BlockSpec((rows, HD), lambda h, i: (i, h)),
+            whole((span, HD)),
+            whole((span, HD)),
+            pl.BlockSpec((rows, 1), lambda h, i: (i, 0)),
+            pl.BlockSpec((rows, 1), lambda h, i: (i, 0)),
+            whole((1, span)),
+        ],
+        out_specs=pl.BlockSpec((rows, HD), lambda h, i: (i, h)),
+        compiler_params=pltpu.CompilerParams(vmem_limit_bytes=32 * MIB),
+        cost_estimate=small_cost(4 * tok * span * total),
+        name="attend",
+    )(queries, keys, values, low_bound[:, None], high_bound[:, None], key_place[None, :])
+
+
+def attend_back(queries, keys, values, out_grad, low_bound, high_bound, key_place):
+    tok, total = queries.shape
+    heads = total // HD
+    span = keys.shape[0]
+    rows = 256
+
+    def kernel(q_ref, k_ref, v_ref, g_ref, lo_ref, hi_ref, kp_ref, dq_ref, dk_ref, dv_ref):
+        first = (pl.program_id(0) == 0) & (pl.program_id(1) == 0)
+        q, k, v, g = q_ref[...], k_ref[...], v_ref[...], g_ref[...]
+        scores = against(k, q)
+        kp = kp_ref[...]
+        allowed = (kp >= lo_ref[...]) & (kp <= hi_ref[...])
+        masked = jnp.where(allowed, scores, masked_value)
+        raised = jnp.exp(masked - jnp.max(masked, axis=0, keepdims=True))
+        probs = raised * (1.0 / jnp.sum(raised, axis=0, keepdims=True))
+        prob_grad = against(v, g)
+        centre = jnp.sum(probs * prob_grad, axis=0, keepdims=True)
+        score_grad = (probs * (prob_grad - centre)).astype(bf16)
+        dq_ref[...] = across(score_grad, k)
+        dk_part = product(score_grad, q)
+        dv_part = product(probs.astype(bf16), g)
+
+        @pl.when(first)
+        def _():
+            dk_ref[...] = dk_part
+            dv_ref[...] = dv_part
+
+        @pl.when(jnp.logical_not(first))
+        def _():
+            dk_ref[...] += dk_part
+            dv_ref[...] += dv_part
+
+    return pl.pallas_call(
+        kernel,
+        out_shape=(
+            jax.ShapeDtypeStruct((tok, total), f32),
+            jax.ShapeDtypeStruct((span, HD), f32),
+            jax.ShapeDtypeStruct((span, HD), f32),
+        ),
+        grid=(heads, tok // rows),
+        in_specs=[
+            pl.BlockSpec((rows, HD), lambda h, i: (i, h)),
+            whole((span, HD)),
+            whole((span, HD)),
+            pl.BlockSpec((rows, HD), lambda h, i: (i, h)),
+            pl.BlockSpec((1, rows), lambda h, i: (0, i)),
+            pl.BlockSpec((1, rows), lambda h, i: (0, i)),
+            whole((span, 1)),
+        ],
+        out_specs=(
+            pl.BlockSpec((rows, HD), lambda h, i: (i, h)),
+            pl.BlockSpec((span, HD), lambda h, i: (0, 0)),
+            pl.BlockSpec((span, HD), lambda h, i: (0, 0)),
+        ),
+        compiler_params=pltpu.CompilerParams(vmem_limit_bytes=40 * MIB),
+        cost_estimate=small_cost(10 * tok * span * total),
+        name="attend_back",
+    )(
+        queries,
+        keys,
+        values,
+        out_grad,
+        low_bound[None, :],
+        high_bound[None, :],
+        key_place[:, None],
+    )
+
+
+def feed_forward(mid, w_ff, units):
+    tok, width = mid.shape
+    blk = 512
+
+    def kernel(m_ref, g_ref, u_ref, d_ref, gate_ref, up_ref, hid_ref, out_ref, acc):
+        step = pl.program_id(0)
+        mid_rows = m_ref[...]
+        gate = product(mid_rows, g_ref[...])
+        up = product(mid_rows, u_ref[...])
+        hidden = glu_pair(gate, up).astype(bf16)
+        gate_ref[...] = gate.astype(bf16)
+        up_ref[...] = up.astype(bf16)
+        hid_ref[...] = hidden
+        part = against(hidden, d_ref[...])
+
+        @pl.when(step == 0)
+        def _():
+            acc[...] = part
+
+        @pl.when(step > 0)
+        def _():
+            acc[...] += part
+
+        @pl.when(step == pl.num_programs(0) - 1)
+        def _():
+            out_ref[...] = acc[...].astype(bf16)
+
+    plane = lambda k: pl.BlockSpec((width, blk), lambda j: (0, k * (units // blk) + j))
+    columns = pl.BlockSpec((tok, blk), lambda j: (0, j))
+    return pl.pallas_call(
+        kernel,
+        out_shape=[jax.ShapeDtypeStruct((tok, units), bf16)] * 3
+        + [jax.ShapeDtypeStruct((tok, width), bf16)],
+        grid=(units // blk,),
+        in_specs=[whole((tok, width)), plane(0), plane(1), plane(2)],
+        out_specs=[columns, columns, columns, pl.BlockSpec((tok, width), lambda j: (0, 0))],
+        scratch_shapes=[pltpu.VMEM((tok, width), f32)],
+        compiler_params=pltpu.CompilerParams(vmem_limit_bytes=56 * MIB),
+        cost_estimate=small_cost(6 * tok * width * units),
+        name="feed_forward",
+    )(mid, w_ff, w_ff, w_ff)
+
+
+def feed_back(feed, w_ff, gate_raw, upward):
+    tok, width = feed.shape
+    units = upward.shape[1]
+    blk = 512
+
+    def kernel(f_ref, g_ref, u_ref, d_ref, gate_ref, up_ref, all_ref, out_ref, acc):
+        step = pl.program_id(0)
+        hidden_grad = product(f_ref[...], d_ref[...])
+        gate = gate_ref[...].astype(f32)
+        _, back_glu = jax.vjp(glu_pair, gate, up_ref[...].astype(f32))
+        gate_grad, up_grad = back_glu(hidden_grad)
+        low_gate, low_up = gate_grad.astype(bf16), up_grad.astype(bf16)
+        all_ref[0] = low_gate
+        all_ref[1] = low_up
+        part = against(low_gate, g_ref[...]) + against(low_up, u_ref[...])
+
+        @pl.when(step == 0)
+        def _():
+            acc[...] = part
+
+        @pl.when(step > 0)
+        def _():
+            acc[...] += part
+
+        @pl.when(step == pl.num_programs(0) - 1)
+        def _():
+            out_ref[...] = acc[...].astype(bf16)
+
+    plane = lambda k: pl.BlockSpec((width, blk), lambda j: (0, k * (units // blk) + j))
+    columns = pl.BlockSpec((tok, blk), lambda j: (0, j))
+    return pl.pallas_call(
+        kernel,
+        out_shape=(
+            jax.ShapeDtypeStruct((2, tok, units), bf16),
+            jax.ShapeDtypeStruct((tok, width), bf16),
+        ),
+        grid=(units // blk,),
+        in_specs=[whole((tok, width)), plane(0), plane(1), plane(2), columns, columns],
+        out_specs=(
+            pl.BlockSpec((2, tok, blk), lambda j: (0, 0, j)),
+            pl.BlockSpec((tok, width), lambda j: (0, 0)),
+        ),
+        scratch_shapes=[pltpu.VMEM((tok, width), f32)],
+        compiler_params=pltpu.CompilerParams(vmem_limit_bytes=56 * MIB),
+        cost_estimate=small_cost(6 * tok * width * units),
+        name="feed_back",
+    )(feed, w_ff, w_ff, w_ff, gate_raw, upward)
+
+
+def feed_grads(left_mat, planes):
+    tok, width = left_mat.shape
+    count, _, units = planes.shape
+    blk = 256
+
+    def kernel(l_ref, p_ref, o_ref):
+        o_ref[...] = across(l_ref[...], p_ref[...], bf16)
+
+    return pl.pallas_call(
+        kernel,
+        out_shape=jax.ShapeDtypeStruct((count, width, units), bf16),
+        grid=(count, width // blk),
+        in_specs=[
+            pl.BlockSpec((tok, blk), lambda w, i: (0, i)),
+            pl.BlockSpec((None, tok, units), lambda w, i: (w, 0, 0)),
+        ],
+        out_specs=pl.BlockSpec((None, blk, units), lambda w, i: (w, i, 0)),
+        compiler_params=pltpu.CompilerParams(vmem_limit_bytes=32 * MIB),
+        cost_estimate=small_cost(1024),
+        name="feed_grads",
+    )(left_mat, planes)
+
+
+def attention_grads(all_in, all_branch, low_qkv, low_att):
+    tok, width = all_in.shape
+    first, second = low_qkv.shape[1], low_att.shape[1]
+    blk = 256
+
+    def kernel(i_ref, b_ref, q_ref, a_ref, o_ref):
+        o_ref[:, :first] = across(i_ref[...], q_ref[...], bf16)
+        o_ref[:, first:] = across(b_ref[...], a_ref[...], bf16)
+
+    return pl.pallas_call(
+        kernel,
+        out_shape=jax.ShapeDtypeStruct((width, first + second), bf16),
+        grid=(width // blk,),
+        in_specs=[
+            pl.BlockSpec((tok, blk), lambda i: (0, i)),
+            pl.BlockSpec((tok, blk), lambda i: (0, i)),
+            whole((tok, first)),
+            whole((tok, second)),
+        ],
+        out_specs=pl.BlockSpec((blk, first + second), lambda i: (i, 0)),
+        compiler_params=pltpu.CompilerParams(vmem_limit_bytes=32 * MIB),
+        cost_estimate=small_cost(1024),
+        name="attention_grads",
+    )(all_in, all_branch, low_qkv, low_att)
+
+
 def shifted(piece, axis, by):
     length = lax.axis_size(axis)
     return lax.ppermute(piece, axis, [(i, (i + by) % length) for i in range(length)])
@@ -83,20 +340,33 @@
     return jnp.concatenate([piece] + [shifted(piece, axis, s) for s in range(1, length)], axis=0)
 
 
-def folded(parts, axis):
+def spread_start(piece, axis):
+    length = lax.axis_size(axis)
+    return [shifted(piece, axis, s) for s in range(1, length)]
+
+
+def fold_start(parts, axis):
     length = lax.axis_size(axis)
     rows = parts.shape[0] // length
-    total = parts[:rows].astype(f32)
-    for s in range(1, length):
-        total = total + shifted(parts[s * rows : (s + 1) * rows], axis, -s).astype(f32)
-    return total
+    return [parts[:rows]] + [
+        shifted(parts[s * rows : (s + 1) * rows], axis, -s) for s in range(1, length)
+    ]
+
+
+def folded(parts, axis):
+    return summed(fold_start(parts, axis))
+
+
+def with_work(arrived, work):
+    return lax.optimization_barrier((arrived, work))
 
 
 def butterfly(piece, axis):
     length = lax.axis_size(axis)
     bit = 1
     while bit < length:
-        piece = piece + crossed(piece, axis, bit)
+        piece = piece.astype(bf16)
+        piece = piece.astype(f32) + crossed(piece, axis, bit).astype(f32)
         bit *= 2
     return piece
 
@@ -107,11 +377,11 @@
     return lax.ppermute(shard, axis, pairs)
 
 
-def blocks_of(mat, order_of):
-    width = mat.shape[1] // lax.axis_size("dp")
-    return jnp.concatenate(
-        [lax.dynamic_slice_in_dim(mat, o * width, width, 1) for o in order_of], axis=1
-    )
+def summed(terms):
+    total = terms[0].astype(f32)
+    for term in terms[1:]:
+        total = total + term.astype(f32)
+    return total
 
 
 def rank_among(keys_own):
@@ -138,8 +408,8 @@
     pieces = tok // LMIN + 2
     runs = tok // stretch + 1
     per_piece = block_rows * (-(-tok // stretch)) + (parts - 1) * runs
-    capacity = -(-(pieces * (per_piece // parts)) // 8) * 8
-    kept = -(-(tok // parts + seqs) // 8) * 8
+    capacity = -(-(pieces * (per_piece // parts) + 1) // 8) * 8
+    kept = -(-(tok // parts + seqs + 1) // 8) * 8
 
     def pick(table, index):
         return jnp.sum(jnp.where(index[:, None] == seq_ids[None, :], table[None, :], 0), axis=1)
@@ -180,9 +450,10 @@
     rows = (jnp.arange(own, dtype=jnp.int32)[None, :] * parts + held[:, None]).reshape(tok)
     both = me * tok + jnp.concatenate([rows - tok, rows])
     ext_seq = jnp.sum((both[:, None] >= dealt_start[None, 1:]).astype(jnp.int32), axis=1)
-    ext_pos = both - pick(dealt_start, ext_seq)
-    ext_seg = jnp.where(both >= 0, ext_seq, -1)
-    return sender, receiver, compact, homing, ext_seg, ext_pos
+    start = pick(dealt_start, ext_seq[tok:])
+    high_bound = both[tok:]
+    low_bound = jnp.maximum(start, high_bound - (WIN - 1))
+    return sender, receiver, compact, homing, (low_bound, high_bound, both), high_bound - start
 
 
 def body(
@@ -211,7 +482,7 @@
     per_width = layer_inputs.shape[2]
     tok = micro * block_rows
     assert tok == WIN
-    sender, receiver, compact, homing, ext_seg, ext_pos = plan(lengths, order, micro, block_rows)
+    sender, receiver, compact, homing, bounds, own_pos = plan(lengths, order, micro, block_rows)
 
     kv_cols = part // (parts // KVH) * HD
     kv_own = lax.dynamic_slice_in_dim(w_keyval, kv_cols, HD, 2)
@@ -221,30 +492,17 @@
     gain_cols = jnp.pad(gain_cols, ((0, LANES - gain_cols.shape[0]), (0, 0))).T
     q_width = w_query.shape[1]
     rank = w_left.shape[1]
-    bundle = [
-        w_query,
-        kv_own[0],
-        kv_own[1],
-        w_out.T,
-        w_left,
-        w_right.T,
-        w_pergate,
-        w_perproj.T,
-        gain_cols,
-    ]
-    marks = [0]
-    for piece in bundle:
-        marks.append(marks[-1] + piece.shape[1])
-    bundle_f = lax.all_gather(jnp.concatenate(bundle, axis=1), "dp", axis=0, tiled=True)
-    gathered = [bundle_f[:, a:b] for a, b in zip(marks[:-1], marks[1:])]
-    wq, wk, wv, wo_t, wl, wr_t, wg, wp_t, gain_f = gathered
-    gu_in, _ = lax.optimization_barrier((w_gateup, bundle_f[:8, :LANES]))
-    w_gu = lax.all_gather(gu_in, "dp", axis=1, tiled=True)
-    dn_in, _ = lax.optimization_barrier((w_down, w_gu[0, :8, :LANES]))
-    w_dn = lax.all_gather(dn_in, "dp", axis=1, tiled=True)
-    gain_rows = gain_f.T
-    gains_f = gain_rows[:6].astype(f32) + gain_rows[6:12].astype(f32)
-
+
+    def gather_columns(pieces):
+        marks = [0]
+        for piece in pieces:
+            marks.append(marks[-1] + piece.shape[1])
+        full = lax.all_gather(jnp.concatenate(pieces, axis=1), "dp", axis=0, tiled=True)
+        return full, [full[:, a:b] for a, b in zip(marks[:-1], marks[1:])]
+
+    first = [w_query, kv_own[0], kv_own[1], w_out.T, w_left, w_right.T, gain_cols]
+    bundle_a, (wq, wk, wv, wo_t, wl, wr_t, gain_f) = gather_columns(first)
+    units = w_down.shape[0]
     flat = jnp.concatenate(
         [
             hidden_in.reshape(tok, width),
@@ -256,17 +514,25 @@
     packed = product(sender, flat, bf16)
     first_cols = width + per_width
     come_in = lax.all_to_all(packed[:, :width], "dp", 0, 0, tiled=True)
-    come_rest = lax.all_to_all(packed[:, width:], "dp", 0, 0, tiled=True)
-    inputs = product(receiver, come_in, bf16).astype(f32)
-    rest = product(receiver, come_rest, bf16)
-    layer_in = rest[:, :per_width].astype(f32)
-    cotangent = rest[:, per_width:].astype(f32)
-
-    angles = ext_pos[tok:].astype(f32)[:, None] * frequencies()
-
+    low_inputs = product(receiver, come_in, bf16)
+    inputs = low_inputs.astype(f32)
+    token_pieces = spread_start(low_inputs, "tensor")
+    second = [w_gateup[0], w_gateup[1], w_down.T, w_pergate, w_perproj.T]
+    second[3], gain_f = with_work(second[3], gain_f)
+    second[4], token_pieces[0] = with_work(second[4], token_pieces[0])
+    w_ff, (_, _, _, wg, wp_t) = gather_columns(second)
+    w_gains = gain_f.T
+    gains_f = w_gains[:6].astype(f32) + w_gains[6:12].astype(f32)
+    all_inputs = jnp.concatenate([low_inputs] + token_pieces, axis=0)
+
+    angles = own_pos.astype(f32)[:, None] * frequencies()
+
+    def homeward(rows_own):
+        return lax.all_to_all(across(receiver, rows_own, bf16), "dp", 0, 0, tiled=True)
+
+    all_in = normed(all_inputs.astype(f32), gains_f[0]).astype(bf16)
     normal_in = normed(inputs, gains_f[0])
     low_in = normal_in.astype(bf16)
-    all_in = spread(low_in, "tensor")
     query_raw = product(all_in, wq).reshape(tok, -1, HD)
     key_raw = product(all_in, wk)
     value_raw = product(all_in, wv)
@@ -283,16 +549,8 @@
     tails = passed_along(jnp.concatenate([keys, values], axis=1), "dp", 1)
     ext_keys = jnp.concatenate([tails[:, :HD], keys], axis=0)
     ext_vals = jnp.concatenate([tails[:, HD:], values], axis=0)
-    gap = ext_pos[tok:, None] - ext_pos[None, :]
-    allowed = (ext_seg[tok:, None] == ext_seg[None, :]) & (gap >= 0) & (gap < WIN)
-    scores = jnp.einsum("qhd,kd->hqk", queries, ext_keys, preferred_element_type=f32)
-    masked = jnp.where(allowed[None], scores, masked_value)
-    top_score = jnp.max(masked, axis=-1, keepdims=True)
-    exp_scores = jnp.exp(masked - top_score)
-    probs = exp_scores / jnp.sum(exp_scores, axis=-1, keepdims=True)
-    low_probs = probs.astype(bf16)
-    attended = jnp.einsum("hqk,kd->qhd", low_probs, ext_vals, preferred_element_type=f32)
-    low_att = attended.astype(bf16).reshape(tok, -1)
+    flat_queries = queries.reshape(tok, -1)
+    low_att = attend(flat_queries, ext_keys, ext_vals, *bounds)
     branch = folded(against(low_att, wo_t, bf16), "tensor")
 
     low_rank = product(low_in, wl, bf16)
@@ -302,11 +560,14 @@
     ) * half_root
     low_mid = normed(first_sum, gains_f[3]).astype(bf16)
 
-    all_mid = spread(low_mid, "tensor")
-    gate_raw = product(all_mid, w_gu[0])
-    upward = product(all_mid, w_gu[1])
-    low_hidden = glu_pair(gate_raw, upward).astype(bf16)
-    feed_raw = folded(product(low_hidden, w_dn, bf16), "tensor")
+    mid_pieces = spread_start(low_mid, "tensor")
+    rest_out, mid_pieces[0] = with_work(packed[:, width:], mid_pieces[0])
+    rest = product(receiver, lax.all_to_all(rest_out, "dp", 0, 0, tiled=True), bf16)
+    all_mid = jnp.concatenate([low_mid] + mid_pieces, axis=0)
+    layer_in = rest[:, :per_width].astype(f32)
+    cotangent = rest[:, per_width:].astype(f32)
+    gate_raw, upward, low_hidden, feed_part = feed_forward(all_mid, w_ff, units)
+    feed_raw = folded(feed_part, "tensor")
 
     second_sum = first_sum + normed(feed_raw, gains_f[4])
     low_second = second_sum.astype(bf16)
@@ -319,24 +580,41 @@
     per_grad, grad_g5 = back_per(cotangent)
     low_per = per_grad.astype(bf16)
     gated_grad = product(low_per, wp_t)
-    grad_perproj = across(low_per, low_gated, bf16)
     gelu_out, back_gelu = jax.vjp(gelu_tanh, pre_gate)
     low_pre = back_gelu(gated_grad * layer_in)[0].astype(bf16)
     layer_grad = gated_grad * gelu_out
-    grad_pergate = across(low_second, low_pre, bf16)
     second_grad = cotangent + against(low_pre, wg)
     _, back_feed = jax.vjp(normed, feed_raw, gains_f[4])
     feed_grad, grad_g4 = back_feed(second_grad)
     low_feed = feed_grad.astype(bf16)
 
-    all_feed = spread(low_feed, "tensor")
-    hidden_grad = against(all_feed, w_dn)
-    _, back_glu = jax.vjp(glu_pair, gate_raw, upward)
-    gate_grad, up_grad = back_glu(hidden_grad)
-    low_gate = gate_grad.astype(bf16)
-    low_up = up_grad.astype(bf16)
-    mid_part = against(low_gate, w_gu[0]) + against(low_up, w_gu[1])
-    mid_grad = folded(mid_part.astype(bf16), "tensor")
+    feed_pieces = spread_start(low_feed, "tensor")
+    grad_perproj = across(low_per, low_gated, bf16)
+    grad_pergate = across(low_second, low_pre, bf16)
+    low_result = jnp.concatenate([result.astype(bf16), layer_grad.astype(bf16)], axis=1)
+    low_result, feed_pieces[0] = with_work(low_result, feed_pieces[0])
+    come_one = homeward(low_result)
+    feed_pieces, (grad_perproj, grad_pergate, come_one) = with_work(
+        feed_pieces, (grad_perproj, grad_pergate, come_one)
+    )
+    all_feed = jnp.concatenate([low_feed] + feed_pieces, axis=0)
+
+    home_one = product(compact, come_one, bf16)
+    home_pieces = spread_start(home_one, "tensor")
+    down_grads = feed_grads(all_feed, low_hidden[None])[0]
+    down_grads, all_feed = with_work(down_grads, all_feed)
+    s_down = lax.psum_scatter(down_grads, "dp", scatter_dimension=0, tiled=True)
+    planes, mid_part = feed_back(all_feed, w_ff, gate_raw, upward)
+
+    mid_part, home_pieces[0] = with_work(mid_part, home_pieces[0])
+    mid_part, home_pieces[-1] = with_work(mid_part, home_pieces[-1])
+
+    mid_pieces = fold_start(mid_part, "tensor")
+    gu_grads = feed_grads(all_mid, planes)
+    gu_grads, s_down = with_work(gu_grads, s_down)
+    mid_pieces, gu_grads = with_work(mid_pieces, gu_grads)
+    s_gateup = lax.psum_scatter(gu_grads, "dp", scatter_dimension=1, tiled=True)
+    mid_grad = summed(mid_pieces)
 
     _, back_mid = jax.vjp(normed, first_sum, gains_f[3])
     first_part, grad_g3 = back_mid(mid_grad)
@@ -344,21 +622,25 @@
     _, back_laurel = jax.vjp(normed, laurel_raw, gains_f[2])
     laurel_grad, grad_g2 = back_laurel(shared)
     low_laurel = laurel_grad.astype(bf16)
+    _, back_branch = jax.vjp(normed, branch, gains_f[1])
+    branch_grad, grad_g1 = back_branch(shared)
+    low_branch = branch_grad.astype(bf16)
+
+    branch_pieces = spread_start(low_branch, "tensor")
     low_rank_grad = product(low_laurel, wr_t, bf16)
     grad_right = across(low_laurel, low_rank, bf16)
     grad_left = across(low_in, low_rank_grad, bf16)
-    _, back_branch = jax.vjp(normed, branch, gains_f[1])
-    branch_grad, grad_g1 = back_branch(shared)
-    low_branch = branch_grad.astype(bf16)
-
-    all_branch = spread(low_branch, "tensor")
-    low_att_grad = product(all_branch, wo_t, bf16).reshape(tok, -1, HD)
-    value_grad = jnp.einsum("hqk,qhd->kd", low_probs, low_att_grad, preferred_element_type=f32)
-    prob_grad = jnp.einsum("qhd,kd->hqk", low_att_grad, ext_vals, preferred_element_type=f32)
-    centre = jnp.sum(probs * prob_grad, axis=-1, keepdims=True)
-    score_grad = (probs * (prob_grad - centre)).astype(bf16)
-    query_grad = jnp.einsum("hqk,kd->qhd", score_grad, ext_keys, preferred_element_type=f32)
-    key_grad = jnp.einsum("hqk,qhd->kd", score_grad, queries, preferred_element_type=f32)
+    small = jnp.concatenate([grad_left, grad_right, grad_pergate, grad_perproj], axis=1)
+    gain_part = jnp.stack([grad_g1, grad_g2, grad_g3, grad_g4, grad_g5])
+    branch_pieces, (small, gain_part) = with_work(branch_pieces, (small, gain_part))
+    all_branch = jnp.concatenate([low_branch] + branch_pieces, axis=0)
+
+    low_att_grad = product(all_branch, wo_t, bf16)
+    query_grad, key_grad, value_grad = attend_back(
+        flat_queries, ext_keys, ext_vals, low_att_grad, *bounds
+    )
+    query_grad, home_pieces[1] = with_work(query_grad, home_pieces[1])
+    query_grad = query_grad.reshape(tok, -1, HD)
     both_grad = jnp.concatenate([key_grad, value_grad], axis=1)
     from_next = passed_along(both_grad[:tok].astype(bf16), "dp", -1)
     both_total = both_grad[tok:] + from_next.astype(f32)
@@ -372,41 +654,50 @@
     low_k = key_raw_grad.astype(bf16)
     low_v = value_raw_grad.astype(bf16)
     attn_part = against(low_q, wq) + against(low_k, wk) + against(low_v, wv)
-    in_attn = folded(attn_part.astype(bf16), "tensor")
+
+    in_pieces = fold_start(attn_part.astype(bf16), "tensor")
+    low_qkv = jnp.concatenate([low_q, low_k, low_v], axis=1)
+    at_grads = attention_grads(all_in, all_branch, low_qkv, low_att)
+    head_cols = jnp.stack([grad_hq, grad_hk]).reshape(-1, width // devices)
+    head_count = head_cols.shape[0]
+    head_cols = jnp.tile(head_cols, (1, devices))
+    last_cols = jnp.concatenate([gain_part, head_cols], axis=0).astype(bf16)
+    last_cols = jnp.pad(last_cols, ((0, LANES - last_cols.shape[0]), (0, 0))).T
+    at_grads = jnp.concatenate([at_grads, small, last_cols], axis=1)
+    in_pieces, at_grads = with_work(in_pieces, at_grads)
+    in_attn = summed(in_pieces)
     normal_grad = in_attn + against(low_rank_grad, wl) + shared
     _, back_in = jax.vjp(normed, inputs, gains_f[0])
     in_part, grad_g0 = back_in(normal_grad)
     input_grad = shared + in_part
-
-    s_gateup = lax.psum_scatter(
-        jnp.stack([across(all_mid, low_gate, bf16), across(all_mid, low_up, bf16)]),
-        "dp",
-        scatter_dimension=1,
-        tiled=True,
-    )
-    s_down = lax.psum_scatter(
-        across(low_hidden, all_feed, bf16), "dp", scatter_dimension=1, tiled=True
-    )
-    gain_part = jnp.stack([grad_g1, grad_g2, grad_g3, grad_g4, grad_g5]).astype(bf16)
-    gain_part = jnp.pad(gain_part, ((0, LANES - 5), (0, 0))).T
-    small = jnp.concatenate(
-        [grad_left, grad_right, grad_pergate, grad_perproj, gain_part], axis=1
-    )
-    s_small = lax.psum_scatter(small, "dp", scatter_dimension=0, tiled=True)
-    attn_grads = jnp.concatenate(
-        [
-            across(all_in, low_q, bf16),
-            across(all_in, low_k, bf16),
-            across(all_in, low_v, bf16),
-            across(all_branch, low_att, bf16),
-        ],
-        axis=1,
-    )
-    s_attn = lax.psum_scatter(attn_grads, "dp", scatter_dimension=0, tiled=True)
+    block = width // devices
+    extra = jnp.pad(
+        grad_g0.reshape(devices, 1, block),
+        ((0, 0), (receiver.shape[1] // devices - 1, 0), (0, width - block)),
+    )
+    sent_two = across(receiver, input_grad.astype(bf16)) + extra.reshape(-1, width)
+    come_two = lax.all_to_all(sent_two.astype(bf16), "dp", 0, 0, tiled=True)
+    at_grads, s_gateup = with_work(at_grads, s_gateup)
+    s_at = lax.psum_scatter(at_grads, "dp", scatter_dimension=0, tiled=True)
+    g0_part = jnp.sum(come_two.reshape(devices, -1, width)[:, -1, :block].astype(f32), axis=0)
+    home_two = product(compact, come_two) + jnp.pad(
+        g0_part[None], ((compact.shape[0] - 1, 0), (0, width - block))
+    )
+    all_two = spread(home_two.astype(bf16), "tensor")
+    back_two = product(homing, all_two, bf16)
+    g0_terms = all_two.reshape(parts, -1, width)[:, -1, :block].astype(f32)
+    while g0_terms.shape[0] > 1:
+        middle = g0_terms.shape[0] // 2
+        g0_terms = g0_terms[:middle] + g0_terms[middle:]
 
     shard_gateup = s_gateup.astype(f32)
-    shard_down = s_down.astype(f32)
-    small_sum = butterfly(s_small.astype(f32), "tensor")
+    shard_down = s_down.T.astype(f32)
+    o_kv = q_width + 2 * HD
+    o_small = o_kv + w_out.shape[0]
+    shard_query = s_at[:, :q_width].astype(f32)
+    kv_part = s_at[:, q_width:o_kv]
+    shard_out = s_at[:, o_kv:o_small].T.astype(f32)
+    small_sum = butterfly(s_at[:, o_small:], "tensor")
     o_left, o_right, o_gate, o_proj = (
         rank,
         2 * rank,
@@ -417,13 +708,9 @@
     shard_right = small_sum[:, o_left:o_right].T
     shard_pergate = small_sum[:, o_right:o_gate]
     shard_perproj = small_sum[:, o_gate:o_proj].T
-    gains_rest = small_sum[:, o_proj : o_proj + 5].T
-    g0_sum = butterfly(grad_g0, "tensor")
-    g0_own = lax.psum_scatter(g0_sum.reshape(1, -1), "dp", scatter_dimension=1, tiled=True)
-    shard_gains = jnp.concatenate([g0_own, gains_rest], axis=0)
-    shard_query = s_attn[:, :q_width].astype(f32)
-    kv_part = s_attn[:, q_width : q_width + 2 * HD]
-    shard_out = s_attn[:, q_width + 2 * HD :].T.astype(f32)
+    last_sum = small_sum[:, o_proj:].T
+    shard_gains = jnp.concatenate([g0_terms, last_sum[:5]], axis=0)
+    head_total = last_sum[5 : 5 + head_count].reshape(2, HD)
     group = parts // KVH
     bit = 1
     kv_sum = kv_part
@@ -440,15 +727,7 @@
             jnp.concatenate([low_head[:, HD:], high_head[:, HD:]], axis=1),
         ]
     )
-    head_total = butterfly(butterfly(jnp.stack([grad_hq, grad_hk]), "tensor"), "dp")
-
-    def home(rows_own):
-        arrived = lax.all_to_all(across(receiver, rows_own, bf16), "dp", 0, 0, tiled=True)
-        shared_rows = spread(product(compact, arrived, bf16), "tensor")
-        return product(homing, shared_rows, bf16)
-
-    back_one = home(jnp.concatenate([result.astype(bf16), layer_grad.astype(bf16)], axis=1))
-    back_two = home(input_grad.astype(bf16))
+    back_one = product(homing, jnp.concatenate([home_one] + home_pieces, axis=0), bf16)
     return (
         back_one[:, :width].reshape(micro, block_rows, width),
         back_two.reshape(micro, block_rows, width),

time: 974 us -> 818 us (0.84)
  matrix products: 162 us -> 55.1 us
  waiting for transfers between devices: 471 us -> 365 us
  Pallas kernels: 0 us -> 87.6 us
  starting transfers between devices: 217 us -> 158 us
  local copies, waits for them, and re-layouts: 45.2 us -> 64.1 us
    pallas_call x0 -> x7, Pallas kernels: none -> 87.6 us  [the longest x1 27.4 us: feed_back(): pl.pallas_call(kernel, out_shape=(jax.ShapeDtypeStruct((2, tok, units), b...]
    reduce_scatter x4 -> x3, waiting for transfers between devices: 68.5 us -> 16.9 us  [the longest x1 14.8 us: body(): s_down = lax.psum_scatter(down_grads, 'dp', scatter_dimension=0, tiled=True)]
    dot_general x18 -> x15, matrix products: 67 us -> 32.4 us  [product(): return jnp.dot(left_mat, right_mat, preferred_element_type=f32).astype(kind)]
    dot_general x12 -> x9, matrix products: 48.6 us -> 14.1 us  [against(): lax.dot_general(left_mat, right_mat, (((1,), (1,)), ((), ())), preferred_...]
    ppermute x11 -> x4, starting transfers between devices: 44.3 us -> 10.5 us  [crossed(): return lax.ppermute(piece, axis, [(i, i ^ bit) for i in range(length)])]
    ppermute x11 -> x4, waiting for transfers between devices: 63.2 us -> 30 us  [crossed(): return lax.ppermute(piece, axis, [(i, i ^ bit) for i in range(length)])]
    dot_general x13 -> x6, matrix products: 41.5 us -> 8.6 us  [across(): lax.dot_general(left_mat, right_mat, (((0,), (0,)), ((), ())), preferred_...]
    all_gather x3 -> x2, waiting for transfers between devices: 35.3 us -> 15.1 us  [gather_columns(): lax.all_gather(jnp.concatenate(pieces, axis=1), 'dp', axis=0, tiled=True)]
  transfers between devices with their start and end apart: 55 -> 45, of which waited for: 28 -> 27; matrix products, arithmetic and copies ran while one was open for 20% -> 17% of each run, Pallas kernels for 0% -> 10%
where the time goes in v2:
time: 818 us; the launch traced here: 809 us
  waiting for transfers between devices  365 us (45%)
  starting transfers between devices  158 us (19%)
  Pallas kernels  87.6 us (11%)
  local copies, waits for them, and re-layouts  64.1 us (8%)
  other arithmetic  62.3 us (8%)
  matrix products  55.1 us (7%)
  between operations  16.6 us (2%)
    ppermute x30, waiting for transfers between devices, shifted(): lax.ppermute(piece, axis, [(i, (i + by) % length) for i in range(length)])  262 us
    ppermute x30, starting transfers between devices, shifted(): lax.ppermute(piece, axis, [(i, (i + by) % length) for i in range(length)])  94.4 us
    dot_general x15, matrix products, product(): return jnp.dot(left_mat, right_mat, preferred_element_type=f32).astype(kind)  32.4 us
    unnamed x298, local copies, waits for them, and re-layouts  31.9 us
    ppermute x4, waiting for transfers between devices, crossed(): return lax.ppermute(piece, axis, [(i, i ^ bit) for i in range(length)])  30 us
    pallas_call x1, Pallas kernels, feed_back(): pl.pallas_call(kernel, out_shape=(jax.ShapeDtypeStruct((2, tok, units), b...  27.4 us
    all_to_all x1, starting transfers between devices, body(): come_two = lax.all_to_all(sent_two.astype(bf16), 'dp', 0, 0, tiled=True)  22.3 us
    pallas_call x1, Pallas kernels, feed_forward(): pl.pallas_call(kernel, out_shape=[jax.ShapeDtypeStruct((tok, units), bf16...  21.6 us
  transfers between devices with their start and end apart: 45, of which 27 were waited for; matrix products, arithmetic and copies ran while one was open for 17% of the time, Pallas kernels for 10%

profile of v2, /device:TPU:0, one launch (start us, length us, event | category | flops | bytes accessed | tf_op | source)
XLA Modules:
  0.0 809.2 jit_solution(9717086043365337592)
XLA Ops:
  14.5 3.9 convolution_convert_fusion
  21.2 5.3 all-to-all-start
  28.2 21.3 %all-to-all-done = bf16[8,40,2048]{2,1,0:T(8,128)(2,1)S(1)} async-done(((bf16[8,40,2048]{2,1,0:T(8,128)(2,1)}), bf16[8,40,2048]{2,1,0:T(8,128)(2,1)S(1)}, u32[]{:S(2)}, u32[]{:S(2)}) %all-to-all-start) | async-done | bytes 1310752 | tf_op jit(solution)/shard_map/all_to_all | solution.py:516
  55.8 7.2 collective-permute-done
  63.0 15.1 %all-gather.3.cloned.1.call-done = bf16[2048,1792]{0,1:T(8,128)(2,1)} async-done(((bf16[256,1792]{0,1:T(8,128)(2,1)}), bf16[2048,1792]{0,1:T(8,128)(2,1)}) %all-gather.3.cloned.1.call-update) | async-done | bytes 7340048 | tf_op jit(solution)/shard_map/all_gather | solution.py:500
  85.8 21.4 %collective-permute-done.1 = bf16[128,2048]{1,0:T(8,128)(2,1)S(1)} collective-permute-done((bf16[128,2048]{1,0:T(8,128)(2,1)S(1)}, bf16[128,2048]{1,0:T(8,128)(2,1)S(1)}, u32[]{:S(2)}, u32[]{:S(2)}) %collective-permute-start.1) | collective-permute-done | bytes 524320 | tf_op jit(solution)/shard_map/ppermute | solution.py:330
  109.9 3.5 multiply_reduce_fusion.19
  136.3 4.5 attend.1.a_ref
  140.9 3.5 convolution_convert_fusion.6
  144.6 14.7 %collective-permute-start.4 = (bf16[128,2048]{1,0:T(8,128)(2,1)S(1)}, bf16[128,2048]{1,0:T(8,128)(2,1)S(1)}, u32[]{:S(2)}, u32[]{:S(2)}) collective-permute-start(bf16[128,2048]{1,0:T(8,128)(2,1)S(1)} %get-tuple-element.231), channel_id=1, source_target_pairs={{0,3},{1,0},{2,1},{3,2},{4,7},{5,4},{6,5},{7,6},{8,11},{9,8},{10,9... | collective-permute-start | bytes 1572872 | tf_op jit(solution)/shard_map/ppermute | solution.py:330
  160.8 5.3 collective-permute-done.4
  166.1 31.2 %collective-permute-done.5 = bf16[128,2048]{1,0:T(8,128)(2,1)S(1)} collective-permute-done((bf16[128,2048]{1,0:T(8,128)(2,1)S(1)}, bf16[128,2048]{1,0:T(8,128)(2,1)S(1)}, u32[]{:S(2)}, u32[]{:S(2)}) %collective-permute-start.5) | collective-permute-done | bytes 524320 | tf_op jit(solution)/shard_map/ppermute | solution.py:330
  200.3 7.8 collective-permute-start.7
  214.1 6.4 collective-permute-done.7
  221.3 16.0 %all-to-all-start.1 = ((bf16[8,40,2304]{2,1,0:T(8,128)(2,1)}), bf16[8,40,2304]{2,1,0:T(8,128)(2,1)S(1)}, u32[]{:S(2)}, u32[]{:S(2)}) async-start(bf16[8,40,2304]{2,1,0:T(8,128)(2,1)} %bitcast.138), calls=%async_computation.1 | async-start | bytes 2949120 | tf_op jit(solution)/shard_map/all_to_all | solution.py:565
  246.2 21.6 %feed_forward.1 = (bf16[512,2048]{1,0:T(8,128)(2,1)}, bf16[512,2048]{1,0:T(8,128)(2,1)}, bf16[512,2048]{1,0:T(8,128)(2,1)}, bf16[512,2048]{1,0:T(8,128)(2,1)}) custom-call(bf16[512,2048]{1,0:T(8,128)(2,1)} %pad_maximum_fusion.4.m_ref.l_ref, bf16[2048,6656]{1,0:T(8,128)(2,1)} %all-gather.5.cloned.1.call-done.g_ref.u_ref.d_ref, ...), custom_call_target="tpu_custom_call" | custom-call | flops 12884901888 | bytes 1024 | tf_op jit(solution)/shard_map/feed_forward/pallas_call | solution.py:216
  270.3 16.4 %collective-permute-start.10 = (bf16[128,2048]{1,0:T(8,128)(2,1)}, bf16[128,2048]{1,0:T(8,128)(2,1)}, u32[]{:S(2)}, u32[]{:S(2)}) collective-permute-start(bf16[128,2048]{1,0:T(8,128)(2,1)} %get-tuple-element.228), channel_id=1, source_target_pairs={{0,3},{1,0},{2,1},{3,2},{4,7},{5,4},{6,5},{7,6},{8,11},{9,8},{10,9... | collective-permute-start | bytes 1572872 | tf_op jit(solution)/shard_map/ppermute | solution.py:330
  291.3 8.4 %collective-permute-done.10 = bf16[128,2048]{1,0:T(8,128)(2,1)} collective-permute-done((bf16[128,2048]{1,0:T(8,128)(2,1)}, bf16[128,2048]{1,0:T(8,128)(2,1)}, u32[]{:S(2)}, u32[]{:S(2)}) %collective-permute-start.10) | collective-permute-done | bytes 524320 | tf_op jit(solution)/shard_map/ppermute | solution.py:330
  299.7 35.5 %collective-permute-done.11 = bf16[128,2048]{1,0:T(8,128)(2,1)} collective-permute-done((bf16[128,2048]{1,0:T(8,128)(2,1)}, bf16[128,2048]{1,0:T(8,128)(2,1)}, u32[]{:S(2)}, u32[]{:S(2)}) %collective-permute-start.11) | collective-permute-done | bytes 524320 | tf_op jit(solution)/shard_map/ppermute | solution.py:330
  347.3 15.5 %collective-permute-done.13 = bf16[128,2048]{1,0:T(8,128)(2,1)S(1)} collective-permute-done((bf16[128,2048]{1,0:T(8,128)(2,1)S(1)}, bf16[128,2048]{1,0:T(8,128)(2,1)S(1)}, u32[]{:S(2)}, u32[]{:S(2)}) %collective-permute-start.13) | collective-permute-done | bytes 524320 | tf_op jit(solution)/shard_map/ppermute | solution.py:330
  364.6 5.2 all-to-all-start.2
  375.6 20.2 %collective-permute-done.14 = bf16[128,2048]{1,0:T(8,128)(2,1)} collective-permute-done((bf16[128,2048]{1,0:T(8,128)(2,1)}, bf16[128,2048]{1,0:T(8,128)(2,1)}, u32[]{:S(2)}, u32[]{:S(2)}) %collective-permute-start.14) | collective-permute-done | bytes 524320 | tf_op jit(solution)/shard_map/ppermute | solution.py:330
  401.0 6.2 feed_grads.2
  413.5 10.6 %collective-permute-start.16 = (bf16[136,2304]{1,0:T(8,128)(2,1)S(1)}, bf16[136,2304]{1,0:T(8,128)(2,1)S(1)}, u32[]{:S(2)}, u32[]{:S(2)}) collective-permute-start(bf16[136,2304]{1,0:T(8,128)(2,1)S(1)} %convolution_convert_fusion.3), channel_id=1, source_target_pairs={{0,1},{1,2},{2,3},{3,0},{4,5},{5,6},{6,7},{7,4},{8,9},{9,10},{10,1... | collective-permute-start | bytes 1880072 | tf_op jit(solution)/shard_map/ppermute | solution.py:330
  425.8 27.4 %feed_back.1 = (bf16[2,512,2048]{2,1,0:T(8,128)(2,1)}, bf16[512,2048]{1,0:T(8,128)(2,1)}) custom-call(bf16[512,2048]{1,0:T(8,128)(2,1)} %copy-done.2, bf16[2048,6656]{1,0:T(8,128)(2,1)} %all-gather.5.cloned.1.call-done.g_ref.u_ref.d_ref, bf16[2048,6656]{1,0:T(8,128)(2,1)} %all-gather.5.cloned.1.call-done.g_ref.u_ref.d_ref, ...), custom_call_target="tpu_custom_call" | custom-call | flops 12884901888 | bytes 1024 | tf_op jit(solution)/shard_map/feed_back/pallas_call | solution.py:260
  462.1 15.0 %feed_grads.3 = bf16[2,2048,2048]{2,1,0:T(8,128)(2,1)} custom-call(bf16[512,2048]{1,0:T(8,128)(2,1)S(1)} %copy-done.3, bf16[2,512,2048]{2,1,0:T(8,128)(2,1)S(1)} %copy-done.6), custom_call_target="tpu_custom_call" | custom-call | flops 1024 | bytes 1024 | tf_op jit(solution)/shard_map/feed_grads/pallas_call | solution.py:287
  477.1 14.8 %reduce-scatter.4.cloned.1.call-done = bf16[256,2048]{1,0:T(8,128)(2,1)} async-done(((bf16[2048,2048]{1,0:T(8,128)(2,1)}), bf16[256,2048]{1,0:T(8,128)(2,1)}) %reduce-scatter.4.cloned.1.call-update) | async-done | bytes 1048592 | tf_op jit(solution)/shard_map/reduce_scatter | solution.py:606
  492.0 11.9 %collective-permute-done.19 = bf16[128,2048]{1,0:T(8,128)(2,1)S(1)} collective-permute-done((bf16[128,2048]{1,0:T(8,128)(2,1)}, bf16[128,2048]{1,0:T(8,128)(2,1)S(1)}, u32[]{:S(2)}, u32[]{:S(2)}) %collective-permute-start.19) | collective-permute-done | bytes 524320 | tf_op jit(solution)/shard_map/ppermute | solution.py:330
  512.8 3.8 multiply_reduce_fusion.4
  528.2 8.9 %collective-permute-done.21 = bf16[128,2048]{1,0:T(8,128)(2,1)} collective-permute-done((bf16[128,2048]{1,0:T(8,128)(2,1)}, bf16[128,2048]{1,0:T(8,128)(2,1)}, u32[]{:S(2)}, u32[]{:S(2)}) %collective-permute-start.21) | collective-permute-done | bytes 524320 | tf_op jit(solution)/shard_map/ppermute | solution.py:330
  537.1 34.7 %collective-permute-done.22 = bf16[128,2048]{1,0:T(8,128)(2,1)} collective-permute-done((bf16[128,2048]{1,0:T(8,128)(2,1)}, bf16[128,2048]{1,0:T(8,128)(2,1)}, u32[]{:S(2)}, u32[]{:S(2)}) %collective-permute-start.22) | collective-permute-done | bytes 524320 | tf_op jit(solution)/shard_map/ppermute | solution.py:330
  571.8 3.5 fusion.23.g_ref
  575.4 7.4 attend_back.1
  599.8 11.3 %collective-permute-start.26 = (bf16[128,2048]{1,0:T(8,128)(2,1)}, bf16[128,2048]{1,0:T(8,128)(2,1)}, u32[]{:S(2)}, u32[]{:S(2)}) collective-permute-start(bf16[128,2048]{1,0:T(8,128)(2,1)} %get-tuple-element.222), channel_id=1, source_target_pairs={{0,3},{1,0},{2,1},{3,2},{4,7},{5,4},{6,5},{7,6},{8,11},{9,8},{10,9... | collective-permute-start | bytes 1572872 | tf_op jit(solution)/shard_map/ppermute | solution.py:330
  613.2 5.4 attention_grads.1
  621.8 7.8 pad_maximum_fusion
  629.6 25.3 %collective-permute-done.27 = bf16[128,2048]{1,0:T(8,128)(2,1)} collective-permute-done((bf16[128,2048]{1,0:T(8,128)(2,1)}, bf16[128,2048]{1,0:T(8,128)(2,1)}, u32[]{:S(2)}, u32[]{:S(2)}) %collective-permute-start.27) | collective-permute-done | bytes 524320 | tf_op jit(solution)/shard_map/ppermute | solution.py:330
  661.2 22.3 %all-to-all-start.3 = ((bf16[8,40,2048]{2,1,0:T(8,128)(2,1)}), bf16[8,40,2048]{2,1,0:T(8,128)(2,1)S(1)}, u32[]{:S(2)}, u32[]{:S(2)}) async-start(bf16[8,40,2048]{2,1,0:T(8,128)(2,1)} %bitcast.56), calls=%async_computation.4 | async-start | bytes 2621440 | tf_op jit(solution)/shard_map/all_to_all | solution.py:679
  683.4 19.3 %all-to-all-done.3 = bf16[8,40,2048]{2,1,0:T(8,128)(2,1)S(1)} async-done(((bf16[8,40,2048]{2,1,0:T(8,128)(2,1)}), bf16[8,40,2048]{2,1,0:T(8,128)(2,1)S(1)}, u32[]{:S(2)}, u32[]{:S(2)}) %all-to-all-start.3) | async-done | bytes 1310752 | tf_op jit(solution)/shard_map/all_to_all | solution.py:679
  703.4 4.0 collective-permute-start.31
  710.7 3.5 convolution_convert_fusion.1
  716.5 4.3 collective-permute-done.29
  720.8 19.5 %collective-permute-done.30 = bf16[136,2048]{1,0:T(8,128)(2,1)} collective-permute-done((bf16[136,2048]{1,0:T(8,128)(2,1)S(1)}, bf16[136,2048]{1,0:T(8,128)(2,1)}, u32[]{:S(2)}, u32[]{:S(2)}) %collective-permute-start.30) | collective-permute-done | bytes 557088 | tf_op jit(solution)/shard_map/ppermute | solution.py:330
  741.9 4.6 convolution_convert_fusion.5
  750.9 9.4 %collective-permute-start.32 = (bf16[256,512]{1,0:T(8,128)(2,1)S(1)}, bf16[256,512]{1,0:T(8,128)(2,1)S(1)}, u32[]{:S(2)}, u32[]{:S(2)}) collective-permute-start(bf16[256,512]{1,0:T(8,128)(2,1)S(1)} %get-tuple-element.239), channel_id=1, source_target_pairs={{0,1},{1,0},{2,3},{3,2},{4,5},{5,4},{6,7},{7,6},{8,9},{9,8},{10,11... | collective-permute-start | bytes 786440 | tf_op jit(solution)/shard_map/ppermute | solution.py:335
  761.4 6.1 collective-permute-done.32
  772.1 7.5 collective-permute-done.34
  781.9 15.7 %collective-permute-done.35 = bf16[256,768]{1,0:T(8,128)(2,1)S(1)} collective-permute-done((bf16[256,768]{1,0:T(8,128)(2,1)S(1)}, bf16[256,768]{1,0:T(8,128)(2,1)S(1)}, u32[]{:S(2)}, u32[]{:S(2)}) %collective-permute-start.35) | collective-permute-done | bytes 393248 | tf_op jit(solution)/shard_map/ppermute | solution.py:335
  (544 shorter events, 192.6 us)
Async XLA Ops:
  7.2 70.8 %all-gather.3.cloned.1.call-start = ((), (), s32[]{:S(2)}) async-start(), calls=%async_computation.7 | async-start | bytes 8257536 | tf_op jit(solution)/shard_map/all_gather | solution.py:500
  21.2 28.3 %all-to-all-start = ((bf16[8,40,2048]{2,1,0:T(8,128)(2,1)}), bf16[8,40,2048]{2,1,0:T(8,128)(2,1)S(1)}, u32[]{:S(2)}, u32[]{:S(2)}) async-start(bf16[8,40,2048]{2,1,0:T(8,128)(2,1)} %bitcast.7), calls=%async_computation | async-start | bytes 2621440 | tf_op jit(solution)/shard_map/all_to_all | solution.py:516
  26.5 219.6 %all-gather.5.cloned.1.call-start = ((), (), s32[]{:S(2)}) async-start(), calls=%async_computation.8 | async-start | bytes 30670848 | tf_op jit(solution)/shard_map/all_gather | solution.py:500
  50.1 472.3 %copy-start.18 = (bf16[128,2048]{1,0:T(8,128)(2,1)}, bf16[128,2048]{1,0:T(8,128)(2,1)S(1)}, u32[]{:S(2)}) copy-start(bf16[128,2048]{1,0:T(8,128)(2,1)S(1)} %get-tuple-element.286) | copy-start | bytes 1572868
  50.1 12.8 %collective-permute-start = (bf16[128,2048]{1,0:T(8,128)(2,1)S(1)}, bf16[128,2048]{1,0:T(8,128)(2,1)S(1)}, u32[]{:S(2)}, u32[]{:S(2)}) collective-permute-start(bf16[128,2048]{1,0:T(8,128)(2,1)S(1)} %get-tuple-element.286), channel_id=1, source_target_pairs={{0,1},{1,2},{2,3},{3,0},{4,5},{5,6},{6,7},{7,4},{8,9},{9,10},{10,1... | collective-permute-start | bytes 1572872 | tf_op jit(solution)/shard_map/ppermute | solution.py:330
  80.1 27.0 %collective-permute-start.1 = (bf16[128,2048]{1,0:T(8,128)(2,1)S(1)}, bf16[128,2048]{1,0:T(8,128)(2,1)S(1)}, u32[]{:S(2)}, u32[]{:S(2)}) collective-permute-start(bf16[128,2048]{1,0:T(8,128)(2,1)S(1)} %get-tuple-element.286), channel_id=1, source_target_pairs={{0,2},{1,3},{2,0},{3,1},{4,6},{5,7},{6,4},{7,5},{8,10},{9,11},{10,... | collective-permute-start | bytes 1572872 | tf_op jit(solution)/shard_map/ppermute | solution.py:330
  82.6 24.5 %collective-permute-start.2 = (bf16[128,2048]{1,0:T(8,128)(2,1)S(1)}, bf16[128,2048]{1,0:T(8,128)(2,1)S(1)}, u32[]{:S(2)}, u32[]{:S(2)}) collective-permute-start(bf16[128,2048]{1,0:T(8,128)(2,1)S(1)} %get-tuple-element.286), channel_id=1, source_target_pairs={{0,3},{1,0},{2,1},{3,2},{4,7},{5,4},{6,5},{7,6},{8,11},{9,8},{10,9... | collective-permute-start | bytes 1572872 | tf_op jit(solution)/shard_map/ppermute | solution.py:330
  126.2 8.7 %collective-permute-start.3 = (bf16[512,512]{1,0:T(8,128)(2,1)}, bf16[512,512]{1,0:T(8,128)(2,1)}, u32[]{:S(2)}, u32[]{:S(2)}) collective-permute-start(bf16[512,512]{1,0:T(8,128)(2,1)} %pad_maximum_fusion.11), channel_id=1, source_target_pairs={{0,4},{4,8},{8,12},{12,16},{16,20},{20,24},{24,28},{1,5},{5,9},{9,... | collective-permute-start | bytes 1572872 | tf_op jit(solution)/shard_map/ppermute | solution.py:377
  144.6 21.5 %collective-permute-start.4 = (bf16[128,2048]{1,0:T(8,128)(2,1)S(1)}, bf16[128,2048]{1,0:T(8,128)(2,1)S(1)}, u32[]{:S(2)}, u32[]{:S(2)}) collective-permute-start(bf16[128,2048]{1,0:T(8,128)(2,1)S(1)} %get-tuple-element.231), channel_id=1, source_target_pairs={{0,3},{1,0},{2,1},{3,2},{4,7},{5,4},{6,5},{7,6},{8,11},{9,8},{10,9... | collective-permute-start | bytes 1572872 | tf_op jit(solution)/shard_map/ppermute | solution.py:330
  159.3 38.0 %collective-permute-start.5 = (bf16[128,2048]{1,0:T(8,128)(2,1)S(1)}, bf16[128,2048]{1,0:T(8,128)(2,1)S(1)}, u32[]{:S(2)}, u32[]{:S(2)}) collective-permute-start(bf16[128,2048]{1,0:T(8,128)(2,1)S(1)} %get-tuple-element.233), channel_id=1, source_target_pairs={{0,2},{1,3},{2,0},{3,1},{4,6},{5,7},{6,4},{7,5},{8,10},{9,11},{10,... | collective-permute-start | bytes 1572872 | tf_op jit(solution)/shard_map/ppermute | solution.py:330
  159.3 38.0 %collective-permute-start.6 = (bf16[128,2048]{1,0:T(8,128)(2,1)S(1)}, bf16[128,2048]{1,0:T(8,128)(2,1)S(1)}, u32[]{:S(2)}, u32[]{:S(2)}) collective-permute-start(bf16[128,2048]{1,0:T(8,128)(2,1)S(1)} %get-tuple-element.232), channel_id=1, source_target_pairs={{0,1},{1,2},{2,3},{3,0},{4,5},{5,6},{6,7},{7,4},{8,9},{9,10},{10,1... | collective-permute-start | bytes 1572872 | tf_op jit(solution)/shard_map/ppermute | solution.py:330
  200.3 20.3 %collective-permute-start.7 = (bf16[128,2048]{1,0:T(8,128)(2,1)}, bf16[128,2048]{1,0:T(8,128)(2,1)S(1)}, u32[]{:S(2)}, u32[]{:S(2)}) collective-permute-start(bf16[128,2048]{1,0:T(8,128)(2,1)} %multiply_convert_fusion), channel_id=1, source_target_pairs={{0,1},{1,2},{2,3},{3,0},{4,5},{5,6},{6,7},{7,4},{8,9},{9,10},{10,1... | collective-permute-start | bytes 1572872 | tf_op jit(solution)/shard_map/ppermute | solution.py:330
  208.1 32.0 %collective-permute-start.8 = (bf16[128,2048]{1,0:T(8,128)(2,1)}, bf16[128,2048]{1,0:T(8,128)(2,1)}, u32[]{:S(2)}, u32[]{:S(2)}) collective-permute-start(bf16[128,2048]{1,0:T(8,128)(2,1)} %multiply_convert_fusion), channel_id=1, source_target_pairs={{0,2},{1,3},{2,0},{3,1},{4,6},{5,7},{6,4},{7,5},{8,10},{9,11},{10,... | collective-permute-start | bytes 1572872 | tf_op jit(solution)/shard_map/ppermute | solution.py:330
  210.0 33.1 %collective-permute-start.9 = (bf16[128,2048]{1,0:T(8,128)(2,1)}, bf16[128,2048]{1,0:T(8,128)(2,1)}, u32[]{:S(2)}, u32[]{:S(2)}) collective-permute-start(bf16[128,2048]{1,0:T(8,128)(2,1)} %multiply_convert_fusion), channel_id=1, source_target_pairs={{0,3},{1,0},{2,1},{3,2},{4,7},{5,4},{6,5},{7,6},{8,11},{9,8},{10,9... | collective-permute-start | bytes 1572872 | tf_op jit(solution)/shard_map/ppermute | solution.py:330
  221.3 69.4 %all-to-all-start.1 = ((bf16[8,40,2304]{2,1,0:T(8,128)(2,1)}), bf16[8,40,2304]{2,1,0:T(8,128)(2,1)S(1)}, u32[]{:S(2)}, u32[]{:S(2)}) async-start(bf16[8,40,2304]{2,1,0:T(8,128)(2,1)} %bitcast.138), calls=%async_computation.1 | async-start | bytes 2949120 | tf_op jit(solution)/shard_map/all_to_all | solution.py:565
  270.3 66.8 %copy-start.70 = (f32[1,2048]{1,0:T(1,128)S(1)}, f32[1,2048]{1,0:T(1,128)}, u32[]{:S(2)}) copy-start(f32[1,2048]{1,0:T(1,128)} %get-tuple-element.266) | copy-start | bytes 24580
  270.3 29.3 %collective-permute-start.10 = (bf16[128,2048]{1,0:T(8,128)(2,1)}, bf16[128,2048]{1,0:T(8,128)(2,1)}, u32[]{:S(2)}, u32[]{:S(2)}) collective-permute-start(bf16[128,2048]{1,0:T(8,128)(2,1)} %get-tuple-element.228), channel_id=1, source_target_pairs={{0,3},{1,0},{2,1},{3,2},{4,7},{5,4},{6,5},{7,6},{8,11},{9,8},{10,9... | collective-permute-start | bytes 1572872 | tf_op jit(solution)/shard_map/ppermute | solution.py:330
  286.7 48.4 %collective-permute-start.11 = (bf16[128,2048]{1,0:T(8,128)(2,1)}, bf16[128,2048]{1,0:T(8,128)(2,1)}, u32[]{:S(2)}, u32[]{:S(2)}) collective-permute-start(bf16[128,2048]{1,0:T(8,128)(2,1)} %get-tuple-element.230), channel_id=1, source_target_pairs={{0,2},{1,3},{2,0},{3,1},{4,6},{5,7},{6,4},{7,5},{8,10},{9,11},{10,... | collective-permute-start | bytes 1572872 | tf_op jit(solution)/shard_map/ppermute | solution.py:330
  288.6 46.6 %collective-permute-start.12 = (bf16[128,2048]{1,0:T(8,128)(2,1)}, bf16[128,2048]{1,0:T(8,128)(2,1)}, u32[]{:S(2)}, u32[]{:S(2)}) collective-permute-start(bf16[128,2048]{1,0:T(8,128)(2,1)} %get-tuple-element.229), channel_id=1, source_target_pairs={{0,1},{1,2},{2,3},{3,0},{4,5},{5,6},{6,7},{7,4},{8,9},{9,10},{10,1... | collective-permute-start | bytes 1572872 | tf_op jit(solution)/shard_map/ppermute | solution.py:330
  291.3 53.1 %copy-start.33 = (bf16[128,2304]{1,0:T(8,128)(2,1)}, bf16[128,2304]{1,0:T(8,128)(2,1)S(1)}, u32[]{:S(2)}) copy-start(bf16[128,2304]{1,0:T(8,128)(2,1)S(1)} %convolution_convert_fusion.4) | copy-start | bytes 1769476
  347.2 15.6 %collective-permute-start.13 = (bf16[128,2048]{1,0:T(8,128)(2,1)S(1)}, bf16[128,2048]{1,0:T(8,128)(2,1)S(1)}, u32[]{:S(2)}, u32[]{:S(2)}) collective-permute-start(bf16[128,2048]{1,0:T(8,128)(2,1)S(1)} %fusion.37), channel_id=1, source_target_pairs={{0,1},{1,2},{2,3},{3,0},{4,5},{5,6},{6,7},{7,4},{8,9},{9,10},{10,1... | collective-permute-start | bytes 1572872 | tf_op jit(solution)/shard_map/ppermute | solution.py:330
  364.6 32.3 %all-to-all-start.2 = ((bf16[8,40,2304]{2,1,0:T(8,128)(2,1)}), bf16[8,40,2304]{2,1,0:T(8,128)(2,1)}, u32[]{:S(2)}, u32[]{:S(2)}) async-start(bf16[8,40,2304]{2,1,0:T(8,128)(2,1)} %bitcast.139), calls=%async_computation.2 | async-start | bytes 2949120 | tf_op jit(solution)/shard_map/all_to_all | solution.py:531
  369.8 122.2 %reduce-scatter.4.cloned.1.call-start = ((), (), s32[]{:S(2)}) async-start(), calls=%async_computation.9 | async-start | bytes 9437184 | tf_op jit(solution)/shard_map/reduce_scatter | solution.py:606
  369.8 25.9 %collective-permute-start.14 = (bf16[128,2048]{1,0:T(8,128)(2,1)}, bf16[128,2048]{1,0:T(8,128)(2,1)}, u32[]{:S(2)}, u32[]{:S(2)}) collective-permute-start(bf16[128,2048]{1,0:T(8,128)(2,1)} %copy-done.55), channel_id=1, source_target_pairs={{0,2},{1,3},{2,0},{3,1},{4,6},{5,7},{6,4},{7,5},{8,10},{9,11},{10,... | collective-permute-start | bytes 1572872 | tf_op jit(solution)/shard_map/ppermute | solution.py:330
  371.4 25.5 %collective-permute-start.15 = (bf16[128,2048]{1,0:T(8,128)(2,1)}, bf16[128,2048]{1,0:T(8,128)(2,1)}, u32[]{:S(2)}, u32[]{:S(2)}) collective-permute-start(bf16[128,2048]{1,0:T(8,128)(2,1)} %copy-done.55), channel_id=1, source_target_pairs={{0,3},{1,0},{2,1},{3,2},{4,7},{5,4},{6,5},{7,6},{8,11},{9,8},{10,9... | collective-permute-start | bytes 1572872 | tf_op jit(solution)/shard_map/ppermute | solution.py:330
  410.6 244.3 %reduce-scatter.6.cloned.1.call-start = ((), (), s32[]{:S(2)}) async-start(), calls=%async_computation.10 | async-start | bytes 18874368 | tf_op jit(solution)/shard_map/reduce_scatter | solution.py:616
  413.5 39.7 %collective-permute-start.16 = (bf16[136,2304]{1,0:T(8,128)(2,1)S(1)}, bf16[136,2304]{1,0:T(8,128)(2,1)S(1)}, u32[]{:S(2)}, u32[]{:S(2)}) collective-permute-start(bf16[136,2304]{1,0:T(8,128)(2,1)S(1)} %convolution_convert_fusion.3), channel_id=1, source_target_pairs={{0,1},{1,2},{2,3},{3,0},{4,5},{5,6},{6,7},{7,4},{8,9},{9,10},{10,1... | collective-permute-start | bytes 1880072 | tf_op jit(solution)/shard_map/ppermute | solution.py:330
  424.1 29.9 %collective-permute-start.17 = (bf16[136,2304]{1,0:T(8,128)(2,1)S(1)}, bf16[136,2304]{1,0:T(8,128)(2,1)S(1)}, u32[]{:S(2)}, u32[]{:S(2)}) collective-permute-start(bf16[136,2304]{1,0:T(8,128)(2,1)S(1)} %convolution_convert_fusion.3), channel_id=1, source_target_pairs={{0,3},{1,0},{2,1},{3,2},{4,7},{5,4},{6,5},{7,6},{8,11},{9,8},{10,9... | collective-permute-start | bytes 1880072 | tf_op jit(solution)/shard_map/ppermute | solution.py:330
  457.2 34.8 %collective-permute-start.18 = (bf16[128,2048]{1,0:T(8,128)(2,1)}, bf16[128,2048]{1,0:T(8,128)(2,1)S(1)}, u32[]{:S(2)}, u32[]{:S(2)}) collective-permute-start(bf16[128,2048]{1,0:T(8,128)(2,1)} %get-tuple-element.226), channel_id=1, source_target_pairs={{0,3},{1,0},{2,1},{3,2},{4,7},{5,4},{6,5},{7,6},{8,11},{9,8},{10,9... | collective-permute-start | bytes 1572872 | tf_op jit(solution)/shard_map/ppermute | solution.py:330
  458.9 45.0 %collective-permute-start.19 = (bf16[128,2048]{1,0:T(8,128)(2,1)}, bf16[128,2048]{1,0:T(8,128)(2,1)S(1)}, u32[]{:S(2)}, u32[]{:S(2)}) collective-permute-start(bf16[128,2048]{1,0:T(8,128)(2,1)} %get-tuple-element.225), channel_id=1, source_target_pairs={{0,2},{1,3},{2,0},{3,1},{4,6},{5,7},{6,4},{7,5},{8,10},{9,11},{10,... | collective-permute-start | bytes 1572872 | tf_op jit(solution)/shard_map/ppermute | solution.py:330
  458.9 45.0 %collective-permute-start.20 = (bf16[128,2048]{1,0:T(8,128)(2,1)}, bf16[128,2048]{1,0:T(8,128)(2,1)}, u32[]{:S(2)}, u32[]{:S(2)}) collective-permute-start(bf16[128,2048]{1,0:T(8,128)(2,1)} %get-tuple-element.224), channel_id=1, source_target_pairs={{0,1},{1,2},{2,3},{3,0},{4,5},{5,6},{6,7},{7,4},{8,9},{9,10},{10,1... | collective-permute-start | bytes 1572872 | tf_op jit(solution)/shard_map/ppermute | solution.py:330
  504.7 243.8 %reduce-scatter.8.cloned.1.call-start = ((), (), s32[]{:S(2)}) async-start(), calls=%async_computation.11 | async-start | bytes 10616832 | tf_op jit(solution)/shard_map/reduce_scatter | solution.py:681
  507.9 75.0 %collective-permute-start.24 = (bf16[136,2304]{1,0:T(8,128)(2,1)}, bf16[136,2304]{1,0:T(8,128)(2,1)}, u32[]{:S(2)}, u32[]{:S(2)}) collective-permute-start(bf16[136,2304]{1,0:T(8,128)(2,1)} %copy-done.63), channel_id=1, source_target_pairs={{0,2},{1,3},{2,0},{3,1},{4,6},{5,7},{6,4},{7,5},{8,10},{9,11},{10,... | collective-permute-start | bytes 1880072 | tf_op jit(solution)/shard_map/ppermute | solution.py:330
  517.9 19.2 %collective-permute-start.21 = (bf16[128,2048]{1,0:T(8,128)(2,1)}, bf16[128,2048]{1,0:T(8,128)(2,1)}, u32[]{:S(2)}, u32[]{:S(2)}) collective-permute-start(bf16[128,2048]{1,0:T(8,128)(2,1)} %get-tuple-element.246), channel_id=1, source_target_pairs={{0,1},{1,2},{2,3},{3,0},{4,5},{5,6},{6,7},{7,4},{8,9},{9,10},{10,1... | collective-permute-start | bytes 1572872 | tf_op jit(solution)/shard_map/ppermute | solution.py:330
  517.9 53.9 %collective-permute-start.22 = (bf16[128,2048]{1,0:T(8,128)(2,1)}, bf16[128,2048]{1,0:T(8,128)(2,1)}, u32[]{:S(2)}, u32[]{:S(2)}) collective-permute-start(bf16[128,2048]{1,0:T(8,128)(2,1)} %get-tuple-element.246), channel_id=1, source_target_pairs={{0,2},{1,3},{2,0},{3,1},{4,6},{5,7},{6,4},{7,5},{8,10},{9,11},{10,... | collective-permute-start | bytes 1572872 | tf_op jit(solution)/shard_map/ppermute | solution.py:330
  519.2 52.6 %collective-permute-start.23 = (bf16[128,2048]{1,0:T(8,128)(2,1)}, bf16[128,2048]{1,0:T(8,128)(2,1)}, u32[]{:S(2)}, u32[]{:S(2)}) collective-permute-start(bf16[128,2048]{1,0:T(8,128)(2,1)} %get-tuple-element.246), channel_id=1, source_target_pairs={{0,3},{1,0},{2,1},{3,2},{4,7},{5,4},{6,5},{7,6},{8,11},{9,8},{10,9... | collective-permute-start | bytes 1572872 | tf_op jit(solution)/shard_map/ppermute | solution.py:330
  585.4 4.9 collective-permute-start.25
  599.8 29.9 %collective-permute-start.26 = (bf16[128,2048]{1,0:T(8,128)(2,1)}, bf16[128,2048]{1,0:T(8,128)(2,1)}, u32[]{:S(2)}, u32[]{:S(2)}) collective-permute-start(bf16[128,2048]{1,0:T(8,128)(2,1)} %get-tuple-element.222), channel_id=1, source_target_pairs={{0,3},{1,0},{2,1},{3,2},{4,7},{5,4},{6,5},{7,6},{8,11},{9,8},{10,9... | collective-permute-start | bytes 1572872 | tf_op jit(solution)/shard_map/ppermute | solution.py:330
  611.0 43.9 %collective-permute-start.27 = (bf16[128,2048]{1,0:T(8,128)(2,1)}, bf16[128,2048]{1,0:T(8,128)(2,1)}, u32[]{:S(2)}, u32[]{:S(2)}) collective-permute-start(bf16[128,2048]{1,0:T(8,128)(2,1)} %get-tuple-element.221), channel_id=1, source_target_pairs={{0,2},{1,3},{2,0},{3,1},{4,6},{5,7},{6,4},{7,5},{8,10},{9,11},{10,... | collective-permute-start | bytes 1572872 | tf_op jit(solution)/shard_map/ppermute | solution.py:330
  613.1 41.8 %collective-permute-start.28 = (bf16[128,2048]{1,0:T(8,128)(2,1)}, bf16[128,2048]{1,0:T(8,128)(2,1)}, u32[]{:S(2)}, u32[]{:S(2)}) collective-permute-start(bf16[128,2048]{1,0:T(8,128)(2,1)} %get-tuple-element.220), channel_id=1, source_target_pairs={{0,1},{1,2},{2,3},{3,0},{4,5},{5,6},{6,7},{7,4},{8,9},{9,10},{10,1... | collective-permute-start | bytes 1572872 | tf_op jit(solution)/shard_map/ppermute | solution.py:330
  661.2 41.5 %all-to-all-start.3 = ((bf16[8,40,2048]{2,1,0:T(8,128)(2,1)}), bf16[8,40,2048]{2,1,0:T(8,128)(2,1)S(1)}, u32[]{:S(2)}, u32[]{:S(2)}) async-start(bf16[8,40,2048]{2,1,0:T(8,128)(2,1)} %bitcast.56), calls=%async_computation.4 | async-start | bytes 2621440 | tf_op jit(solution)/shard_map/all_to_all | solution.py:679
  703.2 17.6 %collective-permute-start.29 = (bf16[136,2048]{1,0:T(8,128)(2,1)S(1)}, bf16[136,2048]{1,0:T(8,128)(2,1)}, u32[]{:S(2)}, u32[]{:S(2)}) collective-permute-start(bf16[136,2048]{1,0:T(8,128)(2,1)S(1)} %fusion.16), channel_id=1, source_target_pairs={{0,1},{1,2},{2,3},{3,0},{4,5},{5,6},{6,7},{7,4},{8,9},{9,10},{10,1... | collective-permute-start | bytes 1671176 | tf_op jit(solution)/shard_map/ppermute | solution.py:330
  703.3 37.0 %collective-permute-start.30 = (bf16[136,2048]{1,0:T(8,128)(2,1)S(1)}, bf16[136,2048]{1,0:T(8,128)(2,1)}, u32[]{:S(2)}, u32[]{:S(2)}) collective-permute-start(bf16[136,2048]{1,0:T(8,128)(2,1)S(1)} %fusion.16), channel_id=1, source_target_pairs={{0,2},{1,3},{2,0},{3,1},{4,6},{5,7},{6,4},{7,5},{8,10},{9,11},{10,... | collective-permute-start | bytes 1671176 | tf_op jit(solution)/shard_map/ppermute | solution.py:330
  703.4 36.9 %collective-permute-start.31 = (bf16[136,2048]{1,0:T(8,128)(2,1)S(1)}, bf16[136,2048]{1,0:T(8,128)(2,1)}, u32[]{:S(2)}, u32[]{:S(2)}) collective-permute-start(bf16[136,2048]{1,0:T(8,128)(2,1)S(1)} %fusion.16), channel_id=1, source_target_pairs={{0,3},{1,0},{2,1},{3,2},{4,7},{5,4},{6,5},{7,6},{8,11},{9,8},{10,9... | collective-permute-start | bytes 1671176 | tf_op jit(solution)/shard_map/ppermute | solution.py:330
  750.9 16.6 %collective-permute-start.32 = (bf16[256,512]{1,0:T(8,128)(2,1)S(1)}, bf16[256,512]{1,0:T(8,128)(2,1)S(1)}, u32[]{:S(2)}, u32[]{:S(2)}) collective-permute-start(bf16[256,512]{1,0:T(8,128)(2,1)S(1)} %get-tuple-element.239), channel_id=1, source_target_pairs={{0,1},{1,0},{2,3},{3,2},{4,5},{5,4},{6,7},{7,6},{8,9},{9,8},{10,11... | collective-permute-start | bytes 786440 | tf_op jit(solution)/shard_map/ppermute | solution.py:335
  761.3 18.2 %collective-permute-start.34 = (bf16[256,768]{1,0:T(8,128)(2,1)S(1)}, bf16[256,768]{1,0:T(8,128)(2,1)S(1)}, u32[]{:S(2)}, u32[]{:S(2)}) collective-permute-start(bf16[256,768]{1,0:T(8,128)(2,1)S(1)} %slice.386), channel_id=1, source_target_pairs={{0,1},{1,0},{2,3},{3,2},{4,5},{5,4},{6,7},{7,6},{8,9},{9,8},{10,11... | collective-permute-start | bytes 1179656 | tf_op jit(solution)/shard_map/ppermute | solution.py:335
  767.6 13.0 %collective-permute-start.33 = (bf16[256,512]{1,0:T(8,128)(2,1)S(1)}, bf16[256,512]{1,0:T(8,128)(2,1)S(1)}, u32[]{:S(2)}, u32[]{:S(2)}) collective-permute-start(bf16[256,512]{1,0:T(8,128)(2,1)S(1)} %add_convert_fusion.3), channel_id=1, source_target_pairs={{0,2},{1,3},{2,0},{3,1},{4,6},{5,7},{6,4},{7,5},{8,10},{9,11},{10,... | collective-permute-start | bytes 786440 | tf_op jit(solution)/shard_map/ppermute | solution.py:335
  779.6 17.9 %collective-permute-start.35 = (bf16[256,768]{1,0:T(8,128)(2,1)S(1)}, bf16[256,768]{1,0:T(8,128)(2,1)S(1)}, u32[]{:S(2)}, u32[]{:S(2)}) collective-permute-start(bf16[256,768]{1,0:T(8,128)(2,1)S(1)} %add_convert_fusion.2), channel_id=1, source_target_pairs={{0,2},{1,3},{2,0},{3,1},{4,6},{5,7},{6,4},{7,5},{8,10},{9,11},{10,... | collective-permute-start | bytes 1179656 | tf_op jit(solution)/shard_map/ppermute | solution.py:335
  (135 other events, 1535.5 us)
Sparse Core Ops, SparseCore 0:
  11.6 66.4 all-gather.2
  80.5 134.1 all-gather.4
  410.8 81.1 reduce-scatter.3
  504.8 115.0 reduce-scatter.5
  655.1 93.4 reduce-scatter.7

commit v3 on v2

v3 whole, which is shorter than its diff:
```python
import jax
import jax.numpy as jnp
from jax import lax
from jax.experimental import pallas as pl
from jax.experimental.pallas import tpu as pltpu
from jax.sharding import PartitionSpec as P

KVH = 2
HD = 256
WIN = 512
LMIN = 1024
LANES = 128

half_root = 0.7071067811865476
masked_value = -1e30
bf16 = jnp.bfloat16
f32 = jnp.float32


def normed(values_in, gain_vec):
    norm_scale = lax.rsqrt(jnp.mean(values_in * values_in, axis=-1, keepdims=True) + 1e-06)
    return values_in * norm_scale * gain_vec


def rotate(values_in, angles):
    half_dim = values_in.shape[-1] // 2
    first_half = values_in[..., :half_dim]
    second_half = values_in[..., half_dim:]
    cosine = jnp.cos(angles)
    sine_part = jnp.sin(angles)
    return jnp.concatenate(
        [
            first_half * cosine - second_half * sine_part,
            second_half * cosine + first_half * sine_part,
        ],
        axis=-1,
    )


def gelu_tanh(values_in):
    return jax.nn.gelu(values_in, approximate=True)


def glu_pair(gate_raw, upward):
    return gelu_tanh(gate_raw) * upward


def value_map(raw_value):
    return normed(raw_value, 1.0)


def product(left_mat, right_mat, kind=f32):
    return jnp.dot(left_mat, right_mat, preferred_element_type=f32).astype(kind)


def against(left_mat, right_mat, kind=f32):
    return lax.dot_general(
        left_mat, right_mat, (((1,), (1,)), ((), ())), preferred_element_type=f32
    ).astype(kind)


def across(left_mat, right_mat, kind=f32):
    return lax.dot_general(
        left_mat, right_mat, (((0,), (0,)), ((), ())), preferred_element_type=f32
    ).astype(kind)


def frequencies():
    half_dim = HD // 2
    return jnp.power(10000.0, -2.0 * jnp.arange(half_dim, dtype=f32) / HD)


MIB = 1 << 20


def small_cost(flops):
    return pl.CostEstimate(flops=flops, bytes_accessed=1024, transcendentals=0)


def whole(shape):
    zeros = (0,) * len(shape)
    return pl.BlockSpec(shape, lambda *_: zeros, pipeline_mode=pl.Buffered(1))


def in_pieces_of(count, rows, width):
    return [whole((rows, width)) for _ in range(count)]


def gather_rows(piece_refs, full_ref):
    rows = piece_refs[0].shape[0]
    for index, piece in enumerate(piece_refs):
        full_ref[index * rows : (index + 1) * rows, :] = piece[...]


def give_rows(step, value, piece_refs):
    rows = piece_refs[0].shape[0]
    each = value.shape[0] // rows
    for index, piece in enumerate(piece_refs):
        place = index % each * rows

        @pl.when(step == index // each)
        def _():
            piece[...] = value[place : place + rows, :].astype(bf16)


def mean_scale(values):
    return lax.rsqrt(jnp.mean(values * values, axis=1, keepdims=True) + 1e-06)


def turned(values, cosine, sine):
    half = values.shape[1] // 2
    first, second = values[:, :half], values[:, half:]
    return jnp.concatenate(
        [first * cosine - second * sine, second * cosine + first * sine], axis=1
    )


def project(pieces, gain, bundle, head_gains, cosine, sine, heads):
    count = len(pieces)
    own, width = pieces[0].shape
    tok = count * own
    total = (heads + 2) * HD
    rows = tok // 2

    def kernel(*refs):
        piece_refs = refs[:count]
        g_ref, w_ref, hg_ref, c_ref, s_ref, in_ref, raw_ref, q_ref, kv_ref, full = refs[count:]
        step = pl.program_id(0)

        @pl.when(step == 0)
        def _():
            gather_rows(piece_refs, full)

        x = full[pl.ds(pl.multiple_of(step * rows, rows), rows), :].astype(f32)
        low = (x * mean_scale(x) * g_ref[...]).astype(bf16)
        in_ref[...] = low
        raw = product(low, w_ref[...])
        raw_ref[...] = raw
        cosine, sine = c_ref[...], s_ref[...]
        for head in range(heads):
            part = raw[:, head * HD : (head + 1) * HD]
            part = part * mean_scale(part) * hg_ref[0:1, :]
            q_ref[:, head * HD : (head + 1) * HD] = turned(part, cosine, sine).astype(bf16)
        part = raw[:, heads * HD : (heads + 1) * HD]
        part = part * mean_scale(part) * hg_ref[1:2, :]
        kv_ref[:, :HD] = turned(part, cosine, sine).astype(bf16)
        part = raw[:, (heads + 1) * HD :]
        kv_ref[:, HD:] = (part * mean_scale(part)).astype(bf16)

    def row_block(columns):
        return pl.BlockSpec((rows, columns), lambda i: (i, 0))

    return pl.pallas_call(
        kernel,
        out_shape=(
            jax.ShapeDtypeStruct((tok, width), bf16),
            jax.ShapeDtypeStruct((tok, total), f32),
            jax.ShapeDtypeStruct((tok, heads * HD), bf16),
            jax.ShapeDtypeStruct((tok, 2 * HD), bf16),
        ),
        grid=(2,),
        in_specs=in_pieces_of(count, own, width)
        + [
            whole((1, width)),
            whole((width, total)),
            whole((2, HD)),
            row_block(HD // 2),
            row_block(HD // 2),
        ],
        out_specs=(row_block(width), row_block(total), row_block(heads * HD), row_block(2 * HD)),
        scratch_shapes=[pltpu.VMEM((tok, width), bf16)],
        compiler_params=pltpu.CompilerParams(vmem_limit_bytes=60 * MIB),
        cost_estimate=small_cost(2 * tok * width * total),
        name="project",
    )(*pieces, gain, bundle, head_gains, cosine, sine)


def attend(queries, tails, own_kv, low_bound, high_bound, key_place, bundle, count):
    tok, total = queries.shape
    heads = total // HD
    width = bundle.shape[0]
    span = 2 * tok
    rows = tok // 2
    first = heads + 2

    def kernel(q_ref, t_ref, o_ref, lo_ref, hi_ref, kp_ref, w_ref, att_ref, *rest):
        piece_refs, (kv, acc) = rest[:count], rest[count:]
        step, head = pl.program_id(0), pl.program_id(1)

        @pl.when((step == 0) & (head == 0))
        def _():
            kv[:tok, :] = t_ref[...]
            kv[tok:, :] = o_ref[...]

        scores = against(q_ref[...], kv[:, :HD])
        kp = kp_ref[...]
        allowed = (kp >= lo_ref[...]) & (kp <= hi_ref[...])
        masked = jnp.where(allowed, scores, masked_value)
        raised = jnp.exp(masked - jnp.max(masked, axis=1, keepdims=True))
        inverse = 1.0 / jnp.sum(raised, axis=1, keepdims=True)
        attended = product((raised * inverse).astype(bf16), kv[:, HD:], bf16)
        att_ref[...] = attended
        part = against(attended, w_ref[...])

        @pl.when(head == 0)
        def _():
            acc[...] = part

        @pl.when(head > 0)
        def _():
            acc[...] += part

        @pl.when(head == heads - 1)
        def _():
            give_rows(step, acc[...], piece_refs)

    result = pl.pallas_call(
        kernel,
        out_shape=[jax.ShapeDtypeStruct((tok, total), bf16)]
        + [jax.ShapeDtypeStruct((tok // count, width), bf16)] * count,
        grid=(2, heads),
        in_specs=[
            pl.BlockSpec((rows, HD), lambda i, h: (i, h)),
            whole((tok, 2 * HD)),
            whole((tok, 2 * HD)),
            pl.BlockSpec((rows, 1), lambda i, h: (i, 0)),
            pl.BlockSpec((rows, 1), lambda i, h: (i, 0)),
            whole((1, span)),
            pl.BlockSpec((width, HD), lambda i, h: (0, first + h)),
        ],
        out_specs=[pl.BlockSpec((rows, HD), lambda i, h: (i, h))]
        + [pl.BlockSpec((tok // count, width), lambda i, h: (0, 0))] * count,
        scratch_shapes=[pltpu.VMEM((span, 2 * HD), bf16), pltpu.VMEM((rows, width), f32)],
        compiler_params=pltpu.CompilerParams(vmem_limit_bytes=60 * MIB),
        cost_estimate=small_cost(4 * tok * span * total),
        name="attend",
    )(
        queries,
        tails,
        own_kv,
        low_bound[:, None],
        high_bound[:, None],
        key_place[None, :],
        bundle,
    )
    return result[0], result[1:]


def attend_back(queries, tails, own_kv, pieces, low_bound, high_bound, key_place, bundle):
    tok, total = queries.shape
    heads = total // HD
    count = len(pieces)
    own, width = pieces[0].shape
    span = 2 * tok
    rows = tok // 2
    first = heads + 2

    def kernel(q_ref, t_ref, o_ref, lo_ref, hi_ref, kp_ref, w_ref, *rest):
        piece_refs = rest[:count]
        dq_ref, own_ref, halo_ref, kv, full, acc = rest[count:]
        head, step = pl.program_id(0), pl.program_id(1)
        begin = (head == 0) & (step == 0)

        @pl.when(begin)
        def _():
            kv[:tok, :] = t_ref[...]
            kv[tok:, :] = o_ref[...]
            gather_rows(piece_refs, full)

        here = pl.ds(pl.multiple_of(step * rows, rows), rows)
        g = product(full[here, :], w_ref[...], bf16)
        q, k, v = q_ref[...], kv[:, :HD], kv[:, HD:]
        scores = against(k, q)
        kp = kp_ref[...]
        allowed = (kp >= lo_ref[...]) & (kp <= hi_ref[...])
        masked = jnp.where(allowed, scores, masked_value)
        raised = jnp.exp(masked - jnp.max(masked, axis=0, keepdims=True))
        probs = raised * (1.0 / jnp.sum(raised, axis=0, keepdims=True))
        prob_grad = against(v, g)
        centre = jnp.sum(probs * prob_grad, axis=0, keepdims=True)
        score_grad = (probs * (prob_grad - centre)).astype(bf16)
        dq_ref[...] = across(score_grad, k)
        dk_part = product(score_grad, q)
        dv_part = product(probs.astype(bf16), g)

        @pl.when(begin)
        def _():
            acc[:, :HD] = dk_part
            acc[:, HD:] = dv_part

        @pl.when(jnp.logical_not(begin))
        def _():
            acc[:, :HD] += dk_part
            acc[:, HD:] += dv_part

        @pl.when((head == heads - 1) & (step == 1))
        def _():
            halo_ref[...] = acc[:tok, :].astype(bf16)
            own_ref[...] = acc[tok:, :]

    return pl.pallas_call(
        kernel,
        out_shape=(
            jax.ShapeDtypeStruct((tok, total), f32),
            jax.ShapeDtypeStruct((tok, 2 * HD), f32),
            jax.ShapeDtypeStruct((tok, 2 * HD), bf16),
        ),
        grid=(heads, 2),
        in_specs=[
            pl.BlockSpec((rows, HD), lambda h, i: (i, h)),
            whole((tok, 2 * HD)),
            whole((tok, 2 * HD)),
            pl.BlockSpec((1, rows), lambda h, i: (0, i)),
            pl.BlockSpec((1, rows), lambda h, i: (0, i)),
            whole((span, 1)),
            pl.BlockSpec((width, HD), lambda h, i: (0, first + h)),
        ]
        + in_pieces_of(count, own, width),
        out_specs=(
            pl.BlockSpec((rows, HD), lambda h, i: (i, h)),
            pl.BlockSpec((tok, 2 * HD), lambda h, i: (0, 0)),
            pl.BlockSpec((tok, 2 * HD), lambda h, i: (0, 0)),
        ),
        scratch_shapes=[
            pltpu.VMEM((span, 2 * HD), bf16),
            pltpu.VMEM((tok, width), bf16),
            pltpu.VMEM((span, 2 * HD), f32),
        ],
        compiler_params=pltpu.CompilerParams(vmem_limit_bytes=60 * MIB),
        cost_estimate=small_cost(10 * tok * span * total),
        name="attend_back",
    )(
        queries,
        tails,
        own_kv,
        low_bound[None, :],
        high_bound[None, :],
        key_place[:, None],
        bundle,
        *pieces,
    )


def project_back(query_grad, own_grad, next_grad, raw, head_gains, cosine, sine, bundle, count):
    tok, total = raw.shape
    heads = query_grad.shape[1] // HD
    width = bundle.shape[0]
    rows = tok // 2

    def kernel(dq_ref, o_ref, n_ref, raw_ref, hg_ref, c_ref, s_ref, w_ref, low_ref, hg_out, *pieces):
        step = pl.program_id(0)
        cosine, sine = c_ref[...], s_ref[...]
        both = o_ref[...] + n_ref[...].astype(f32)
        raw_rows = raw_ref[...]

        def norm_back(grad, values, gain):
            scale = mean_scale(values)
            weighted = grad if gain is None else grad * gain
            centre = jnp.mean(weighted * values, axis=1, keepdims=True)
            back = scale * weighted - values * (scale * scale * scale * centre)
            return back, jnp.sum(grad * values * scale, axis=0, keepdims=True)

        gain_grad = jnp.zeros((1, HD), f32)
        for head in range(heads):
            columns = slice(head * HD, (head + 1) * HD)
            grad = turned(dq_ref[:, columns], cosine, -sine)
            back, part = norm_back(grad, raw_rows[:, columns], hg_ref[0:1, :])
            low_ref[:, columns] = back.astype(bf16)
            gain_grad = gain_grad + part
        columns = slice(heads * HD, (heads + 1) * HD)
        grad = turned(both[:, :HD], cosine, -sine)
        back, key_gain = norm_back(grad, raw_rows[:, columns], hg_ref[1:2, :])
        low_ref[:, columns] = back.astype(bf16)
        columns = slice((heads + 1) * HD, (heads + 2) * HD)
        back, _ = norm_back(both[:, HD:], raw_rows[:, columns], None)
        low_ref[:, columns] = back.astype(bf16)

        @pl.when(step == 0)
        def _():
            hg_out[0:1, :] = gain_grad
            hg_out[1:2, :] = key_gain

        @pl.when(step > 0)
        def _():
            hg_out[0:1, :] += gain_grad
            hg_out[1:2, :] += key_gain

        give_rows(step, against(low_ref[...], w_ref[...]), pieces)

    def row_block(columns):
        return pl.BlockSpec((rows, columns), lambda i: (i, 0))

    result = pl.pallas_call(
        kernel,
        out_shape=[
            jax.ShapeDtypeStruct((tok, total), bf16),
            jax.ShapeDtypeStruct((2, HD), f32),
        ]
        + [jax.ShapeDtypeStruct((tok // count, width), bf16)] * count,
        grid=(2,),
        in_specs=[
            row_block(heads * HD),
            row_block(2 * HD),
            row_block(2 * HD),
            row_block(total),
            whole((2, HD)),
            row_block(HD // 2),
            row_block(HD // 2),
            whole((width, total)),
        ],
        out_specs=[row_block(total), pl.BlockSpec((2, HD), lambda i: (0, 0))]
        + [pl.BlockSpec((tok // count, width), lambda i: (0, 0))] * count,
        compiler_params=pltpu.CompilerParams(vmem_limit_bytes=60 * MIB),
        cost_estimate=small_cost(2 * tok * width * total),
        name="project_back",
    )(query_grad, own_grad, next_grad, raw, head_gains, cosine, sine, bundle)
    return result[0], result[1], result[2:]


def feed_forward(pieces, w_ff, units):
    count = len(pieces)
    own, width = pieces[0].shape
    tok = count * own
    blk = 512

    def kernel(*refs):
        piece_refs = refs[:count]
        g_ref, u_ref, d_ref, gate_ref, up_ref, hid_ref = refs[count : count + 6]
        out_refs, (full, acc) = refs[count + 6 : 2 * count + 6], refs[2 * count + 6 :]
        step = pl.program_id(0)

        @pl.when(step == 0)
        def _():
            gather_rows(piece_refs, full)

        mid_rows = full[...]
        gate = product(mid_rows, g_ref[...])
        up = product(mid_rows, u_ref[...])
        hidden = glu_pair(gate, up).astype(bf16)
        gate_ref[...] = gate.astype(bf16)
        up_ref[...] = up.astype(bf16)
        hid_ref[...] = hidden
        part = against(hidden, d_ref[...])

        @pl.when(step == 0)
        def _():
            acc[...] = part

        @pl.when(step > 0)
        def _():
            acc[...] += part

        @pl.when(step == pl.num_programs(0) - 1)
        def _():
            for index, piece in enumerate(out_refs):
                piece[...] = acc[index * own : (index + 1) * own, :].astype(bf16)

    plane = lambda k: pl.BlockSpec((width, blk), lambda j: (0, k * (units // blk) + j))
    columns = pl.BlockSpec((tok, blk), lambda j: (0, j))
    result = pl.pallas_call(
        kernel,
        out_shape=[jax.ShapeDtypeStruct((tok, units), bf16)] * 3
        + [jax.ShapeDtypeStruct((own, width), bf16)] * count,
        grid=(units // blk,),
        in_specs=in_pieces_of(count, own, width) + [plane(0), plane(1), plane(2)],
        out_specs=[columns] * 3 + [pl.BlockSpec((own, width), lambda j: (0, 0))] * count,
        scratch_shapes=[pltpu.VMEM((tok, width), bf16), pltpu.VMEM((tok, width), f32)],
        compiler_params=pltpu.CompilerParams(vmem_limit_bytes=60 * MIB),
        cost_estimate=small_cost(6 * tok * width * units),
        name="feed_forward",
    )(*pieces, w_ff, w_ff, w_ff)
    return result[0], result[1], result[2], result[3:]


def feed_back(pieces, w_ff, gate_raw, upward):
    count = len(pieces)
    own, width = pieces[0].shape
    tok = count * own
    units = upward.shape[1]
    blk = 512

    def kernel(*refs):
        piece_refs = refs[:count]
        g_ref, u_ref, d_ref, gate_ref, up_ref, low_g_ref, low_u_ref = refs[count : count + 7]
        out_refs, (full, acc) = refs[count + 7 : 2 * count + 7], refs[2 * count + 7 :]
        step = pl.program_id(0)

        @pl.when(step == 0)
        def _():
            gather_rows(piece_refs, full)

        hidden_grad = product(full[...], d_ref[...])
        gate = gate_ref[...].astype(f32)
        _, back_glu = jax.vjp(glu_pair, gate, up_ref[...].astype(f32))
        gate_grad, up_grad = back_glu(hidden_grad)
        low_gate, low_up = gate_grad.astype(bf16), up_grad.astype(bf16)
        low_g_ref[...] = low_gate
        low_u_ref[...] = low_up
        part = against(low_gate, g_ref[...]) + against(low_up, u_ref[...])

        @pl.when(step == 0)
        def _():
            acc[...] = part

        @pl.when(step > 0)
        def _():
            acc[...] += part

        @pl.when(step == pl.num_programs(0) - 1)
        def _():
            for index, piece in enumerate(out_refs):
                piece[...] = acc[index * own : (index + 1) * own, :].astype(bf16)

    plane = lambda k: pl.BlockSpec((width, blk), lambda j: (0, k * (units // blk) + j))
    columns = pl.BlockSpec((tok, blk), lambda j: (0, j))
    result = pl.pallas_call(
        kernel,
        out_shape=[jax.ShapeDtypeStruct((tok, units), bf16)] * 2
        + [jax.ShapeDtypeStruct((own, width), bf16)] * count,
        grid=(units // blk,),
        in_specs=in_pieces_of(count, own, width)
        + [plane(0), plane(1), plane(2), columns, columns],
        out_specs=[columns] * 2
        + [pl.BlockSpec((own, width), lambda j: (0, 0))] * count,
        scratch_shapes=[pltpu.VMEM((tok, width), bf16), pltpu.VMEM((tok, width), f32)],
        compiler_params=pltpu.CompilerParams(vmem_limit_bytes=60 * MIB),
        cost_estimate=small_cost(6 * tok * width * units),
        name="feed_back",
    )(*pieces, w_ff, w_ff, w_ff, gate_raw, upward)
    return result[0], result[1], result[2:]


def column_grads(products, others, name, blk, every, parity, added=None):
    width = products[0][0][0].shape[1]
    operands, specs = [], []
    for left, right in products:
        operands += [*left, right]
        specs += [
            pl.BlockSpec((piece.shape[0], blk), lambda i, par: (0, every * i + par[0]))
            for piece in left
        ]
        specs.append(whole(right.shape))
    operands += others
    specs += [
        pl.BlockSpec((blk, other.shape[1]), lambda i, par: (every * i + par[0], 0))
        for other in others
    ]
    total = sum(mat.shape[1] for _, mat in products) + sum(other.shape[1] for other in others)
    counts = [len(left) for left, _ in products]
    out_spec = pl.BlockSpec((blk, total), lambda i, par: (i, 0))
    if added is not None:
        operands.append(added)
        specs.append(out_spec)

    def kernel(par_ref, *refs):
        o_ref, refs = refs[-1], list(refs[:-1])
        a_ref = refs.pop() if added is not None else None

        def give(value, place):
            columns = slice(place, place + value.shape[1])
            if a_ref is not None:
                value = value.astype(f32) + a_ref[:, columns].astype(f32)
            o_ref[:, columns] = value.astype(bf16)
            return columns.stop

        place = 0
        for count in counts:
            rows = jnp.concatenate([ref[...] for ref in refs[:count]], axis=0)
            place = give(across(rows, refs[count][...]), place)
            refs = refs[count + 1 :]
        for ref in refs:
            place = give(ref[...], place)

    return pl.pallas_call(
        kernel,
        out_shape=jax.ShapeDtypeStruct((width // every, total), bf16),
        grid_spec=pltpu.PrefetchScalarGridSpec(
            num_scalar_prefetch=1,
            grid=(width // blk // every,),
            in_specs=specs,
            out_specs=out_spec,
        ),
        compiler_params=pltpu.CompilerParams(vmem_limit_bytes=60 * MIB),
        cost_estimate=small_cost(1024),
        name=name,
    )(parity.reshape(1), *operands)


def crossed(piece, axis, bit):
    length = lax.axis_size(axis)
    return lax.ppermute(piece, axis, [(i, i ^ bit) for i in range(length)])


def spread_start(piece, axis):
    held = {0: piece}
    bit = lax.axis_size(axis) // 2
    while bit:
        held.update({k | bit: crossed(held[k], axis, bit) for k in list(held)})
        bit //= 2
    return [held[k] for k in range(1, len(held))]


def fold_start(chunks, axis):
    terms = {k: [chunk] for k, chunk in enumerate(chunks)}
    bit = 1
    while bit < len(chunks):
        for k in [k for k in terms if k & bit]:
            going = terms.pop(k)
            going = going[0] if len(going) == 1 else summed(going).astype(bf16)
            terms[k ^ bit].append(crossed(going, axis, bit))
        bit *= 2
    return terms[0]


def folded(chunks, axis):
    return summed(fold_start(chunks, axis))


def with_work(arrived, work):
    return lax.optimization_barrier((arrived, work))


def passed_along(shard, axis, by):
    length = lax.axis_size(axis)
    pairs = [(i, i + by) for i in range(length) if 0 <= i + by < length]
    return lax.ppermute(shard, axis, pairs)


def summed(terms):
    total = terms[0].astype(f32)
    for term in terms[1:]:
        total = total + term.astype(f32)
    return total


def rank_among(keys_own):
    count = keys_own.shape[0]
    place = jnp.arange(count, dtype=jnp.int32)
    same = (keys_own[None, :] == keys_own[:, None]) & (place[None, :] < place[:, None])
    return jnp.sum(same.astype(jnp.int32), axis=1)


def plan(lengths, order, micro, block_rows):
    devices = lax.axis_size("dp")
    parts = lax.axis_size("tensor")
    me = lax.axis_index("dp")
    part = lax.axis_index("tensor")
    tok = micro * block_rows
    own = tok // parts
    stretch = devices * block_rows
    seqs = lengths.shape[0]
    given_len = jnp.take(lengths, order)
    given_start = jnp.cumsum(given_len) - given_len
    dealt_start = jnp.cumsum(lengths) - lengths
    seq_ids = jnp.arange(seqs, dtype=jnp.int32)
    shift_given = jnp.take(dealt_start, order) - given_start
    pieces = tok // LMIN + 2
    runs = tok // stretch + 1
    per_piece = block_rows * (-(-tok // stretch)) + (parts - 1) * runs
    capacity = -(-(pieces * (per_piece // parts) + 1) // 8) * 8
    kept = -(-(tok // parts + seqs + 1) // 8) * 8

    def pick(table, index):
        return jnp.sum(jnp.where(index[:, None] == seq_ids[None, :], table[None, :], 0), axis=1)

    local = jnp.arange(tok, dtype=jnp.int32)
    stream = local // block_rows * stretch + me * block_rows + local % block_rows
    arrival = jnp.sum((stream[:, None] >= given_start[None, 1:]).astype(jnp.int32), axis=1)
    dealt = stream + pick(shift_given, arrival)
    target = dealt // tok
    quarter = dealt % parts
    send_slot = target * capacity + rank_among(target * parts + quarter)
    send_slot = jnp.where(quarter == part, send_slot, -1)
    keep_rank = rank_among(quarter)
    keep_slot = (part ^ quarter) * kept + keep_rank

    place = me * tok + jnp.arange(own, dtype=jnp.int32) * parts + part
    own_seq = jnp.sum((place[:, None] >= dealt_start[None, 1:]).astype(jnp.int32), axis=1)
    shift_dealt = jnp.sum(
        jnp.where(order[None, :] == seq_ids[:, None], -shift_given[None, :], 0), axis=1
    )
    anchor = place + pick(shift_dealt, own_seq)
    source = anchor % stretch // block_rows
    prior = (anchor[None, :] < anchor[:, None]) & (source[None, :] == source[:, None])
    recv_slot = source * capacity + jnp.sum(prior.astype(jnp.int32), axis=1)

    total = devices * capacity
    slots = jnp.arange(total, dtype=jnp.int32)
    sender = (slots[:, None] == send_slot[None, :]).astype(bf16)
    receiver = (recv_slot[:, None] == slots[None, :]).astype(bf16)
    mine = jnp.where(quarter == part, keep_rank, -1)
    chosen = (jnp.arange(kept, dtype=jnp.int32)[:, None] == mine[None, :]).astype(bf16)
    compact = against(chosen, sender, bf16)
    homing = (
        keep_slot[:, None] == jnp.arange(parts * kept, dtype=jnp.int32)[None, :]
    ).astype(bf16)

    held = part ^ jnp.arange(parts, dtype=jnp.int32)
    rows = (jnp.arange(own, dtype=jnp.int32)[None, :] * parts + held[:, None]).reshape(tok)
    both = me * tok + jnp.concatenate([rows - tok, rows])
    ext_seq = jnp.sum((both[:, None] >= dealt_start[None, 1:]).astype(jnp.int32), axis=1)
    start = pick(dealt_start, ext_seq[tok:])
    high_bound = both[tok:]
    low_bound = jnp.maximum(start, high_bound - (WIN - 1))
    return sender, receiver, compact, homing, (low_bound, high_bound, both), high_bound - start


def body(
    hidden_in,
    layer_inputs,
    out_grad,
    lengths,
    order,
    w_query,
    w_keyval,
    w_out,
    w_left,
    w_right,
    w_gateup,
    w_down,
    w_pergate,
    w_perproj,
    gains,
    head_gains,
):
    devices = lax.axis_size("dp")
    me = lax.axis_index("dp")
    parts = lax.axis_size("tensor")
    part = lax.axis_index("tensor")
    micro, block_rows, width = hidden_in.shape
    per_width = layer_inputs.shape[2]
    tok = micro * block_rows
    assert tok == WIN
    sender, receiver, compact, homing, bounds, own_pos = plan(lengths, order, micro, block_rows)

    kv_cols = part // (parts // KVH) * HD
    kv_own = lax.dynamic_slice_in_dim(w_keyval, kv_cols, HD, 2)
    gains_high = lax.reduce_precision(gains, 8, 7)
    gains_low = (gains - gains_high).astype(bf16)
    gain_cols = jnp.concatenate([gains_high.astype(bf16), gains_low], axis=0)
    gain_cols = jnp.pad(gain_cols, ((0, LANES - gain_cols.shape[0]), (0, 0))).T
    q_width = w_query.shape[1]
    rank = w_left.shape[1]

    def gather_columns(pieces):
        marks = [0]
        for piece in pieces:
            marks.append(marks[-1] + piece.shape[1])
        full = lax.all_gather(jnp.concatenate(pieces, axis=1), "dp", axis=0, tiled=True)
        return full, [full[:, a:b] for a, b in zip(marks[:-1], marks[1:])]

    first = [w_query, kv_own[0], kv_own[1], w_out.T, w_left, w_right.T, gain_cols]
    bundle_a, (wq, wk, wv, wo_t, wl, wr_t, gain_f) = gather_columns(first)
    units = w_down.shape[0]
    flat = jnp.concatenate(
        [
            hidden_in.reshape(tok, width),
            layer_inputs.reshape(tok, per_width),
            out_grad.reshape(tok, width),
        ],
        axis=1,
    )
    packed = product(sender, flat, bf16)
    first_cols = width + per_width
    come_in = lax.all_to_all(packed[:, :width], "dp", 0, 0, tiled=True)
    low_inputs = product(receiver, come_in, bf16)
    inputs = low_inputs.astype(f32)
    token_pieces = spread_start(low_inputs, "tensor")
    second = [w_gateup[0], w_gateup[1], w_down.T, w_pergate, w_perproj.T]
    w_ff, (_, _, _, wg, wp_t) = gather_columns(second)
    w_gains = gain_f.T
    gains_f = w_gains[:6].astype(f32) + w_gains[6:12].astype(f32)
    angles = own_pos.astype(f32)[:, None] * frequencies()

    def homeward(rows_own):
        return lax.all_to_all(across(receiver, rows_own, bf16), "dp", 0, 0, tiled=True)

    block = width // devices
    paired = devices > 1 and block % (2 * LANES) == 0
    low_bit = me % 2
    groups = [list(range(k, devices, 2)) for k in range(2)] if paired else None

    def scattered(grads, swap):
        return lax.psum_scatter(
            grads,
            "dp",
            scatter_dimension=0,
            axis_index_groups=groups if swap else None,
            tiled=True,
        )

    def grads_beside_fold(chunks, products, others, name, swap):
        def make(*where):
            return column_grads(products, others, name, *where)

        if not (paired and swap):
            return fold_start(chunks, "tensor"), make(2 * LANES, 1, jnp.zeros((), jnp.int32))
        leaving = make(block, 2, 1 - low_bit)
        chunks, leaving = with_work(chunks, leaving)
        pieces = fold_start(chunks, "tensor")
        return pieces, make(block, 2, low_bit, crossed(leaving, "dp", 1))

    cosine, sine = jnp.cos(angles), jnp.sin(angles)
    heads = q_width // HD
    all_in, raw, queries, own_kv = project(
        [low_inputs] + token_pieces, gains_f[:1], bundle_a, head_gains, cosine, sine, heads
    )
    normal_in = normed(inputs, gains_f[0])
    low_in = normal_in.astype(bf16)
    tails = passed_along(own_kv, "dp", 1)
    low_att, branch_parts = attend(queries, tails, own_kv, *bounds, bundle_a, parts)
    branch = folded(branch_parts, "tensor")

    low_rank = product(low_in, wl, bf16)
    laurel_raw = against(low_rank, wr_t)
    first_sum = (
        inputs + normed(branch, gains_f[1]) + normal_in + normed(laurel_raw, gains_f[2])
    ) * half_root
    low_mid = normed(first_sum, gains_f[3]).astype(bf16)

    all_mid = [low_mid] + spread_start(low_mid, "tensor")
    rest_out, w_ff = with_work(packed[:, width:], w_ff)
    come_rest = lax.all_to_all(rest_out, "dp", 0, 0, tiled=True)
    gate_raw, upward, low_hidden, feed_parts = feed_forward(all_mid, w_ff, units)
    feed_parts, come_rest = with_work(feed_parts, come_rest)
    fed_pieces = fold_start(feed_parts, "tensor")
    rest = product(receiver, come_rest, bf16)
    layer_in = rest[:, :per_width].astype(f32)
    cotangent = rest[:, per_width:].astype(f32)
    feed_raw = summed(fed_pieces)

    second_sum = first_sum + normed(feed_raw, gains_f[4])
    low_second = second_sum.astype(bf16)
    pre_gate = product(low_second, wg)
    low_gated = (gelu_tanh(pre_gate) * layer_in).astype(bf16)
    per_raw = against(low_gated, wp_t)
    result = second_sum + normed(per_raw, gains_f[5])

    _, back_per = jax.vjp(normed, per_raw, gains_f[5])
    per_grad, grad_g5 = back_per(cotangent)
    low_per = per_grad.astype(bf16)
    gated_grad = product(low_per, wp_t)
    gelu_out, back_gelu = jax.vjp(gelu_tanh, pre_gate)
    low_pre = back_gelu(gated_grad * layer_in)[0].astype(bf16)
    layer_grad = gated_grad * gelu_out
    second_grad = cotangent + against(low_pre, wg)
    _, back_feed = jax.vjp(normed, feed_raw, gains_f[4])
    feed_grad, grad_g4 = back_feed(second_grad)
    low_feed = feed_grad.astype(bf16)

    feed_pieces = spread_start(low_feed, "tensor")
    grad_perproj = across(low_per, low_gated, bf16)
    grad_pergate = across(low_second, low_pre, bf16)
    low_result = jnp.concatenate([result.astype(bf16), layer_grad.astype(bf16)], axis=1)
    come_one = homeward(low_result)
    feed_pieces, (grad_perproj, grad_pergate, come_one) = with_work(
        feed_pieces, (grad_perproj, grad_pergate, come_one)
    )
    all_feed = [low_feed] + feed_pieces

    home_one = product(compact, come_one, bf16)
    home_pieces = spread_start(home_one, "tensor")
    low_gate, low_up, mid_parts = feed_back(all_feed, w_ff, gate_raw, upward)
    mid_parts, home_pieces[0] = with_work(mid_parts, home_pieces[0])
    mid_parts, home_pieces[1] = with_work(mid_parts, home_pieces[1])

    mid_pieces, ff_grads = grads_beside_fold(
        mid_parts,
        [(all_mid, low_gate), (all_mid, low_up), (all_feed, low_hidden)],
        [grad_pergate, grad_perproj],
        "feed_grads",
        False,
    )
    mid_pieces, ff_grads = with_work(mid_pieces, ff_grads)
    s_ff = scattered(ff_grads, False)
    mid_grad = summed(mid_pieces)

    _, back_mid = jax.vjp(normed, first_sum, gains_f[3])
    first_part, grad_g3 = back_mid(mid_grad)
    shared = (second_grad + first_part) * half_root
    _, back_laurel = jax.vjp(normed, laurel_raw, gains_f[2])
    laurel_grad, grad_g2 = back_laurel(shared)
    low_laurel = laurel_grad.astype(bf16)
    _, back_branch = jax.vjp(normed, branch, gains_f[1])
    branch_grad, grad_g1 = back_branch(shared)
    low_branch = branch_grad.astype(bf16)

    branch_pieces = spread_start(low_branch, "tensor")
    low_rank_grad = product(low_laurel, wr_t, bf16)
    grad_right = across(low_laurel, low_rank, bf16)
    grad_left = across(low_in, low_rank_grad, bf16)
    small = jnp.concatenate([grad_left, grad_right], axis=1)
    gain_part = jnp.stack([grad_g1, grad_g2, grad_g3, grad_g4, grad_g5])
    branch_pieces, (small, gain_part) = with_work(branch_pieces, (small, gain_part))
    all_branch = [low_branch] + branch_pieces

    query_grad, own_grad, halo_grad = attend_back(
        queries, tails, own_kv, all_branch, *bounds, bundle_a
    )
    query_grad, home_pieces[-1] = with_work(query_grad, home_pieces[-1])
    next_grad = passed_along(halo_grad, "dp", -1)
    low_qkv, head_grads, in_parts = project_back(
        query_grad, own_grad, next_grad, raw, head_gains, cosine, sine, bundle_a, parts
    )

    head_cols = head_grads.reshape(-1, width // devices)
    head_count = head_cols.shape[0]
    head_cols = jnp.tile(head_cols, (1, devices))
    last_cols = jnp.concatenate([gain_part, head_cols], axis=0).astype(bf16)
    last_cols = jnp.pad(last_cols, ((0, LANES - last_cols.shape[0]), (0, 0))).T
    in_pieces, at_grads = grads_beside_fold(
        in_parts,
        [([all_in], low_qkv), (all_branch, low_att)],
        [small, last_cols],
        "attention_grads",
        True,
    )
    in_pieces, at_grads = with_work(in_pieces, at_grads)
    in_attn = summed(in_pieces)
    normal_grad = in_attn + against(low_rank_grad, wl) + shared
    _, back_in = jax.vjp(normed, inputs, gains_f[0])
    in_part, grad_g0 = back_in(normal_grad)
    input_grad = shared + in_part
    extra = jnp.pad(
        grad_g0.reshape(devices, 1, block),
        ((0, 0), (receiver.shape[1] // devices - 1, 0), (0, width - block)),
    )
    sent_two = across(receiver, input_grad.astype(bf16)) + extra.reshape(-1, width)
    come_two = lax.all_to_all(sent_two.astype(bf16), "dp", 0, 0, tiled=True)
    at_grads, (s_ff, come_two) = with_work(at_grads, (s_ff, come_two))
    s_at = scattered(at_grads, True)
    early = s_ff[:, 3 * units :]
    bit = 1
    while bit < parts:
        early = summed([early, crossed(early, "tensor", bit)])
        early = early.astype(bf16) if 2 * bit < parts else early
        bit *= 2
    g0_part = jnp.sum(come_two.reshape(devices, -1, width)[:, -1, :block].astype(f32), axis=0)
    home_two = product(compact, come_two) + jnp.pad(
        g0_part[None], ((compact.shape[0] - 1, 0), (0, width - block))
    )
    home_two = home_two.astype(bf16)
    all_two = jnp.concatenate([home_two] + spread_start(home_two, "tensor"), axis=0)
    back_two = product(homing, all_two, bf16)
    g0_terms = all_two.reshape(parts, -1, width)[:, -1, :block].astype(f32)
    while g0_terms.shape[0] > 1:
        middle = g0_terms.shape[0] // 2
        g0_terms = g0_terms[:middle] + g0_terms[middle:]

    shard_gateup = jnp.stack([s_ff[:, :units], s_ff[:, units : 2 * units]]).astype(f32)
    shard_down = s_ff[:, 2 * units : 3 * units].T.astype(f32)
    o_kv = q_width + 2 * HD
    o_small = o_kv + w_out.shape[0]
    shard_query = s_at[:, :q_width].astype(f32)
    shard_out = s_at[:, o_kv:o_small].T.astype(f32)
    kv_cols = 2 * HD
    exchanged = jnp.concatenate([s_at[:, q_width:o_kv], s_at[:, o_small:]], axis=1)
    bit = 1
    while bit < parts // KVH:
        exchanged = summed([exchanged, crossed(exchanged, "tensor", bit)]).astype(bf16)
        bit *= 2
    arrived = crossed(exchanged, "tensor", bit)
    kv_sum, kv_other = exchanged[:, :kv_cols], arrived[:, :kv_cols]
    small_sum = summed([exchanged[:, kv_cols:], arrived[:, kv_cols:]])
    shard_left = small_sum[:, :rank]
    shard_right = small_sum[:, rank : 2 * rank].T
    shard_pergate = early[:, :per_width]
    shard_perproj = early[:, per_width:].T
    last_sum = small_sum[:, 2 * rank :].T
    shard_gains = jnp.concatenate([g0_terms, last_sum[:5]], axis=0)
    head_total = last_sum[5 : 5 + head_count].reshape(2, HD)
    upper = part // (parts // KVH) == 1
    low_head = jnp.where(upper, kv_other, kv_sum).astype(f32)
    high_head = jnp.where(upper, kv_sum, kv_other).astype(f32)
    shard_keyval = jnp.stack(
        [
            jnp.concatenate([low_head[:, :HD], high_head[:, :HD]], axis=1),
            jnp.concatenate([low_head[:, HD:], high_head[:, HD:]], axis=1),
        ]
    )
    back_one = product(homing, jnp.concatenate([home_one] + home_pieces, axis=0), bf16)
    return (
        back_one[:, :width].reshape(micro, block_rows, width),
        back_two.reshape(micro, block_rows, width),
        back_one[:, width:].reshape(micro, block_rows, per_width),
        shard_query,
        shard_keyval,
        shard_out,
        shard_left,
        shard_right,
        shard_gateup,
        shard_down,
        shard_pergate,
        shard_perproj,
        shard_gains,
        head_total,
    )


def solution(mesh):
    placed = (
        P(None, "dp", None),
        P(None, "dp", None),
        P(None, "dp", None),
        P(),
        P(),
        P("dp", "tensor"),
        P(None, "dp", None),
        P("tensor", "dp"),
        P("dp", None),
        P(None, "dp"),
        P(None, "dp", "tensor"),
        P("tensor", "dp"),
        P("dp", None),
        P(None, "dp"),
        P(None, "dp"),
        P(),
    )
    return jax.shard_map(
        body,
        mesh=mesh,
        in_specs=placed,
        out_specs=(
            P(None, "dp", None),
            P(None, "dp", None),
            P(None, "dp", None),
            P("dp", "tensor"),
            P(None, "dp", None),
            P("tensor", "dp"),
            P("dp", None),
            P(None, "dp"),
            P(None, "dp", "tensor"),
            P("tensor", "dp"),
            P("dp", None),
            P(None, "dp"),
            P(None, "dp"),
            P(),
        ),
        check_vma=False,
    )
```

time: 818 us -> 718 us (0.88)
  starting transfers between devices: 158 us -> 84.7 us
  waiting for transfers between devices: 365 us -> 329 us
  blocking collectives: 0 us -> 35.5 us
  Pallas kernels: 87.6 us -> 122 us
  other arithmetic: 62.3 us -> 38.3 us
  local copies, waits for them, and re-layouts: 64.1 us -> 44 us
  matrix products: 55.1 us -> 39.7 us
    ppermute x30 -> x0, waiting for transfers between devices: 262 us -> none  [shifted(): lax.ppermute(piece, axis, [(i, (i + by) % length) for i in range(length)])]
    ppermute x4 -> x35, waiting for transfers between devices: 30 us -> 256 us  [crossed(): return lax.ppermute(piece, axis, [(i, i ^ bit) for i in range(length)])]
    ppermute x30 -> x0, starting transfers between devices: 94.4 us -> none  [shifted(): lax.ppermute(piece, axis, [(i, (i + by) % length) for i in range(length)])]
    ppermute x4 -> x35, starting transfers between devices: 10.5 us -> 67.1 us  [crossed(): return lax.ppermute(piece, axis, [(i, i ^ bit) for i in range(length)])]
    all_to_all x0 -> x1, blocking collectives: none -> 35.5 us  [body(): come_two = lax.all_to_all(sent_two.astype(bf16), 'dp', 0, 0, tiled=True)]
    all_to_all x2 -> x1, starting transfers between devices: 38.2 us -> 4.31 us  [body(): come_rest = lax.all_to_all(rest_out, 'dp', 0, 0, tiled=True)]
    pallas_call x5 -> x7, Pallas kernels: 58.6 us -> 87.5 us  [the longest x3 34.9 us: column_grads(): pl.pallas_call(kernel, out_shape=jax.ShapeDtypeStruct((width // every, to...]
    all_gather x2, waiting for transfers between devices: 15.1 us -> 39.2 us  [gather_columns(): lax.all_gather(jnp.concatenate(pieces, axis=1), 'dp', axis=0, tiled=True)]
  transfers between devices with their start and end apart: 45 -> 44, of which waited for: 27 -> 28; matrix products, arithmetic and copies ran while one was open for 17% -> 13% of each run, Pallas kernels for 10% -> 17%
where the time goes in v3:
time: 718 us; the launch traced here: 708 us
  waiting for transfers between devices  329 us (46%)
  Pallas kernels  122 us (17%)
  starting transfers between devices  84.7 us (12%)
  local copies, waits for them, and re-layouts  44 us (6%)
  matrix products  39.7 us (6%)
  other arithmetic  38.3 us (5%)
  blocking collectives  35.5 us (5%)
  between operations  15.7 us (2%)
    ppermute x35, waiting for transfers between devices, crossed(): return lax.ppermute(piece, axis, [(i, i ^ bit) for i in range(length)])  256 us
    ppermute x35, starting transfers between devices, crossed(): return lax.ppermute(piece, axis, [(i, i ^ bit) for i in range(length)])  67.1 us
    all_gather x2, waiting for transfers between devices, gather_columns(): lax.all_gather(jnp.concatenate(pieces, axis=1), 'dp', axis=0, tiled=True)  39.2 us
    all_to_all x1, blocking collectives, body(): come_two = lax.all_to_all(sent_two.astype(bf16), 'dp', 0, 0, tiled=True)  35.5 us
    pallas_call x3, Pallas kernels, column_grads(): pl.pallas_call(kernel, out_shape=jax.ShapeDtypeStruct((width // every, to...  34.9 us
    all_to_all x1, waiting for transfers between devices, body(): come_in = lax.all_to_all(packed[:, :width], 'dp', 0, 0, tiled=True)  25.2 us
    pallas_call x1, Pallas kernels, feed_back(): pl.pallas_call(kernel, out_shape=[jax.ShapeDtypeStruct((tok, units), bf16...  25.2 us
    dot_general x11, matrix products, product(): return jnp.dot(left_mat, right_mat, preferred_element_type=f32).astype(kind)  23.8 us
  transfers between devices with their start and end apart: 44, of which 28 were waited for; matrix products, arithmetic and copies ran while one was open for 13% of the time, Pallas kernels for 17%

profile of v3, /device:TPU:0, one launch (start us, length us, event | category | flops | bytes accessed | tf_op | source)
XLA Modules:
  0.0 708.4 jit_solution(16243847688249273247)
XLA Ops:
  23.3 4.3 convolution_convert_fusion
  30.4 5.1 all-to-all-start
  36.5 25.2 %all-to-all-done = bf16[8,40,2048]{2,1,0:T(8,128)(2,1)S(1)} async-done(((bf16[8,40,2048]{2,1,0:T(8,128)(2,1)}), bf16[8,40,2048]{2,1,0:T(8,128)(2,1)S(1)}, u32[]{:S(2)}, u32[]{:S(2)}) %all-to-all-start) | async-done | bytes 1310752 | tf_op jit(solution)/shard_map/all_to_all | solution.py:765
  68.5 16.3 %collective-permute-done.1.refs_2_ = bf16[128,2048]{1,0:T(8,128)(2,1)S(1)} collective-permute-done((bf16[128,2048]{1,0:T(8,128)(2,1)S(1)}, bf16[128,2048]{1,0:T(8,128)(2,1)S(1)}, u32[]{:S(2)}, u32[]{:S(2)}) %collective-permute-start.1) | collective-permute-done | bytes 524320 | tf_op jit(solution)/shard_map/ppermute | solution.py:591
  86.8 3.1 slice_reduce_fusion.1
  90.8 7.3 %collective-permute-done.2.refs_3_ = bf16[128,2048]{1,0:T(8,128)(2,1)S(1)} collective-permute-done((bf16[128,2048]{1,0:T(8,128)(2,1)S(1)}, bf16[128,2048]{1,0:T(8,128)(2,1)S(1)}, u32[]{:S(2)}, u32[]{:S(2)}) %collective-permute-start.2) | collective-permute-done | bytes 524320 | tf_op jit(solution)/shard_map/ppermute | solution.py:591
  98.9 7.9 %project.1 = (bf16[512,2048]{1,0:T(8,128)(2,1)}, f32[512,1024]{1,0:T(8,128)}, bf16[512,512]{1,0:T(8,128)(2,1)}, bf16[512,512]{1,0:T(8,128)(2,1)}) custom-call(bf16[128,2048]{1,0:T(8,128)(2,1)} %copy-done.1, bf16[128,2048]{1,0:T(8,128)(2,1)} %copy-done.44, bf16[128,2048]{1,0:T(8,128)(2,1)} %copy-done.42, bf16[128,2048]{1,0:T(8,128)(2,1)} %copy-done.45, ...), custom_call_target="tpu_custom_call" | custom-call | flops 2147483648 | bytes 1024 | tf_op jit(solution)/shard_map/project/pallas_call | solution.py:153
  111.7 10.1 %attend.1 = (bf16[512,512]{1,0:T(8,128)(2,1)}, bf16[128,2048]{1,0:T(8,128)(2,1)}, bf16[128,2048]{1,0:T(8,128)(2,1)}, bf16[128,2048]{1,0:T(8,128)(2,1)}, bf16[128,2048]{1,0:T(8,128)(2,1)}) custom-call(bf16[512,512]{1,0:T(8,128)(2,1)} %get-tuple-element.92.q_ref, bf16[512,512]{1,0:T(8,128)(2,1)} %copy-done.37, bf16[512,512]{1,0:T(8,128)(2,1)} %get-tuple-element.93.o_ref, ...), custom_call_target="tpu_custom_call" | custom-call | flops 1073741824 | bytes 1024 | tf_op jit(solution)/shard_map/attend/pallas_call | solution.py:217
  123.9 7.3 %collective-permute-done.5 = bf16[128,2048]{1,0:T(8,128)(2,1)S(1)} collective-permute-done((bf16[128,2048]{1,0:T(8,128)(2,1)}, bf16[128,2048]{1,0:T(8,128)(2,1)S(1)}, u32[]{:S(2)}, u32[]{:S(2)}) %collective-permute-start.5) | collective-permute-done | bytes 524320 | tf_op jit(solution)/shard_map/ppermute | solution.py:591
  138.3 9.9 %collective-permute-done.6 = bf16[128,2048]{1,0:T(8,128)(2,1)S(1)} collective-permute-done((bf16[128,2048]{1,0:T(8,128)(2,1)S(1)}, bf16[128,2048]{1,0:T(8,128)(2,1)S(1)}, u32[]{:S(2)}, u32[]{:S(2)}) %collective-permute-start.6) | collective-permute-done | bytes 524320 | tf_op jit(solution)/shard_map/ppermute | solution.py:591
  150.3 4.3 collective-permute-start.7
  154.6 21.3 %collective-permute-done.8.refs_2_.refs_7_ = bf16[128,2048]{1,0:T(8,128)(2,1)S(1)} collective-permute-done((bf16[128,2048]{1,0:T(8,128)(2,1)S(1)}, bf16[128,2048]{1,0:T(8,128)(2,1)S(1)}, u32[]{:S(2)}, u32[]{:S(2)}) %collective-permute-start.8) | collective-permute-done | bytes 524320 | tf_op jit(solution)/shard_map/ppermute | solution.py:591
  177.3 39.2 %all-gather.5.cloned.1.call-done.refs_4_.refs_5_.refs_6_ = bf16[2048,6656]{1,0:T(8,128)(2,1)} async-done(((bf16[256,6656]{1,0:T(8,128)(2,1)}), bf16[2048,6656]{1,0:T(8,128)(2,1)}) %all-gather.5.cloned.1.call-update) | async-done | bytes 27262992 | tf_op jit(solution)/shard_map/all_gather | solution.py:749
  216.6 4.3 all-to-all-start.1
  220.9 22.0 %feed_forward.1 = (bf16[512,2048]{1,0:T(8,128)(2,1)}, bf16[512,2048]{1,0:T(8,128)(2,1)}, bf16[512,2048]{1,0:T(8,128)(2,1)}, bf16[128,2048]{1,0:T(8,128)(2,1)}, b...) custom-call(bf16[128,2048]{1,0:T(8,128)(2,1)} %copy-done.4, ...), custom_call_target="tpu_custom_call" | custom-call | flops 12884901888 | bytes 1024 | tf_op jit(solution)/shard_map/feed_forward/pallas_call | solution.py:460
  245.1 12.9 %collective-permute-done.11 = bf16[128,2048]{1,0:T(8,128)(2,1)S(1)} collective-permute-done((bf16[128,2048]{1,0:T(8,128)(2,1)}, bf16[128,2048]{1,0:T(8,128)(2,1)S(1)}, u32[]{:S(2)}, u32[]{:S(2)}) %collective-permute-start.11) | collective-permute-done | bytes 524320 | tf_op jit(solution)/shard_map/ppermute | solution.py:591
  263.5 14.0 %collective-permute-done.10 = bf16[128,2048]{1,0:T(8,128)(2,1)S(1)} collective-permute-done((bf16[128,2048]{1,0:T(8,128)(2,1)}, bf16[128,2048]{1,0:T(8,128)(2,1)S(1)}, u32[]{:S(2)}, u32[]{:S(2)}) %collective-permute-start.10) | collective-permute-done | bytes 524320 | tf_op jit(solution)/shard_map/ppermute | solution.py:591
  277.5 6.7 collective-permute-done.12
  293.6 4.3 all-to-all-start.2
  298.2 3.3 multiply_reduce_fusion
  302.6 3.7 collective-permute-start.13
  306.3 22.1 %collective-permute-done.14.refs_2_.refs_12_ = bf16[128,2048]{1,0:T(8,128)(2,1)S(1)} collective-permute-done((bf16[128,2048]{1,0:T(8,128)(2,1)S(1)}, bf16[128,2048]{1,0:T(8,128)(2,1)S(1)}, u32[]{:S(2)}, u32[]{:S(2)}) %collective-permute-start.14) | collective-permute-done | bytes 524320 | tf_op jit(solution)/shard_map/ppermute | solution.py:591
  333.1 8.7 %collective-permute-done.15.refs_3_.refs_13_ = bf16[128,2048]{1,0:T(8,128)(2,1)} collective-permute-done((bf16[128,2048]{1,0:T(8,128)(2,1)S(1)}, bf16[128,2048]{1,0:T(8,128)(2,1)}, u32[]{:S(2)}, u32[]{:S(2)}) %collective-permute-start.15) | collective-permute-done | bytes 524320 | tf_op jit(solution)/shard_map/ppermute | solution.py:591
  346.0 25.2 %feed_back.1 = (bf16[512,2048]{1,0:T(8,128)(2,1)}, bf16[512,2048]{1,0:T(8,128)(2,1)}, bf16[128,2048]{1,0:T(8,128)(2,1)}, bf16[128,2048]{1,0:T(8,128)(2,1)}, bf16...) custom-call(bf16[128,2048]{1,0:T(8,128)(2,1)} %copy-done.15, bf16[128,2048]{1,0:T(8,128)(2,1)} %copy-done.32, ...), custom_call_target="tpu_custom_call" | custom-call | flops 12884901888 | bytes 1024 | tf_op jit(solution)/shard_map/feed_back/pallas_call | solution.py:516
  375.2 18.7 %collective-permute-done.19 = bf16[128,2048]{1,0:T(8,128)(2,1)S(1)} collective-permute-done((bf16[128,2048]{1,0:T(8,128)(2,1)}, bf16[128,2048]{1,0:T(8,128)(2,1)S(1)}, u32[]{:S(2)}, u32[]{:S(2)}) %collective-permute-start.19) | collective-permute-done | bytes 524320 | tf_op jit(solution)/shard_map/ppermute | solution.py:591
  396.4 21.8 %feed_grads.1 = bf16[2048,6656]{1,0:T(8,128)(2,1)} custom-call(s32[1]{0:T(128)} %constant.205.clone.1.par_ref, bf16[128,2048]{1,0:T(8,128)(2,1)} %copy-done.4, bf16[128,2048]{1,0:T(8,128)(2,1)} %collective-permute-done.7.refs_1_.refs_6_, bf16[128,2048]{1,0:T(8,128)(2,1)} %copy-done.14, bf16[128,2048]{1,0:T(8,128)(2,1)} %collective-permute-done.9.refs_3_.refs_8_, ...), custom_call_target="tpu_custom_call" | custom-call | flops 1024 | bytes 1024 | tf_op jit(solution)/shard_map/feed_grads/pallas_call | solution.py:574
  421.6 3.3 multiply_reduce_fusion.2
  435.7 5.2 collective-permute-done.22.rest_2_.refs_4_
  440.9 3.4 collective-permute-start.23
  449.8 11.9 %collective-permute-done.21.rest_1_.refs_3_ = bf16[128,2048]{1,0:T(8,128)(2,1)} collective-permute-done((bf16[128,2048]{1,0:T(8,128)(2,1)S(1)}, bf16[128,2048]{1,0:T(8,128)(2,1)}, u32[]{:S(2)}, u32[]{:S(2)}) %collective-permute-start.21) | collective-permute-done | bytes 524320 | tf_op jit(solution)/shard_map/ppermute | solution.py:591
  461.7 5.6 collective-permute-done.23.rest_3_.refs_5_
  467.3 12.5 %attend_back.1 = (f32[512,512]{1,0:T(8,128)}, f32[512,512]{1,0:T(8,128)}, bf16[512,512]{1,0:T(8,128)(2,1)}) custom-call(bf16[512,512]{1,0:T(8,128)(2,1)} %get-tuple-element.92.q_ref, bf16[512,512]{1,0:T(8,128)(2,1)} %copy-done.37, bf16[512,512]{1,0:T(8,128)(2,1)} %get-tuple-element.93.o_ref, s32[1,512]{1,0:T(1,128)} %bitcast.129, s32[1,512]{1,0:T(1,128)} %bitcast.131, ...), custom_call_target="tpu_custom_call" | custom-call | flops 2684354560 | bytes 1024 | tf_op jit(solution)/shard_map/attend_back/pallas_call | solution.py:301
  484.7 9.4 %project_back.1 = (bf16[512,1024]{1,0:T(8,128)(2,1)}, f32[2,256]{1,0:T(2,128)}, bf16[128,2048]{1,0:T(8,128)(2,1)}, bf16[128,2048]{1,0:T(8,128)(2,1)}, bf16[128,2...) custom-call(f32[512,512]{1,0:T(8,128)} %get-tuple-element.142.dq_ref, f32[512,512]{1,0:T(8,128)} %get-tuple-element.143.o_ref, ...), custom_call_target="tpu_custom_call" | custom-call | flops 2147483648 | bytes 1024 | tf_op jit(solution)/shard_map/project_back/pallas_call | solution.py:393
  496.1 6.1 attention_grads.2
  502.2 19.4 %collective-permute-start.29 = (bf16[1024,1792]{1,0:T(8,128)(2,1)}, bf16[1024,1792]{1,0:T(8,128)(2,1)}, u32[]{:S(2)}, u32[]{:S(2)}) collective-permute-start(bf16[1024,1792]{1,0:T(8,128)(2,1)} %attention_grads.2), channel_id=1, source_target_pairs={{0,4},{4,0},{8,12},{12,8},{16,20},{20,16},{24,28},{28,24},{1,5},{5... | collective-permute-start | bytes 11010056 | tf_op jit(solution)/shard_map/ppermute | solution.py:591
  523.6 12.8 %collective-permute-done.27 = bf16[128,2048]{1,0:T(8,128)(2,1)S(1)} collective-permute-done((bf16[128,2048]{1,0:T(8,128)(2,1)S(1)}, bf16[128,2048]{1,0:T(8,128)(2,1)S(1)}, u32[]{:S(2)}, u32[]{:S(2)}) %collective-permute-start.27) | collective-permute-done | bytes 524320 | tf_op jit(solution)/shard_map/ppermute | solution.py:591
  538.7 7.1 attention_grads.3
  545.8 8.2 %collective-permute-done.26 = bf16[128,2048]{1,0:T(8,128)(2,1)} collective-permute-done((bf16[128,2048]{1,0:T(8,128)(2,1)}, bf16[128,2048]{1,0:T(8,128)(2,1)}, u32[]{:S(2)}, u32[]{:S(2)}) %collective-permute-start.26) | collective-permute-done | bytes 524320 | tf_op jit(solution)/shard_map/ppermute | solution.py:591
  554.0 8.1 %collective-permute-done.28 = bf16[128,2048]{1,0:T(8,128)(2,1)} collective-permute-done((bf16[128,2048]{1,0:T(8,128)(2,1)}, bf16[128,2048]{1,0:T(8,128)(2,1)}, u32[]{:S(2)}, u32[]{:S(2)}) %collective-permute-start.28) | collective-permute-done | bytes 524320 | tf_op jit(solution)/shard_map/ppermute | solution.py:591
  565.3 35.5 %all_to_all.48 = bf16[8,40,2048]{2,1,0:T(8,128)(2,1)S(1)} all-to-all(bf16[8,40,2048]{2,1,0:T(8,128)(2,1)S(1)} %bitcast.111), channel_id=1, replica_groups=mesh['dp'=8,'tensor'=4] {'dp'}, dimensions={0} | all-to-all | bytes 2621440 | tf_op jit(solution)/shard_map/all_to_all | solution.py:929
  600.8 5.2 reduce-scatter.3.cloned.1.call-done
  606.0 3.5 convolution_convert_fusion.1
  617.4 28.1 %collective-permute-done.35 = bf16[256,512]{1,0:T(8,128)(2,1)S(1)} collective-permute-done((bf16[256,512]{1,0:T(8,128)(2,1)S(1)}, bf16[256,512]{1,0:T(8,128)(2,1)S(1)}, u32[]{:S(2)}, u32[]{:S(2)}) %collective-permute-start.35) | collective-permute-done | bytes 262176 | tf_op jit(solution)/shard_map/ppermute | solution.py:591
  652.7 6.4 collective-permute-done.36
  661.8 3.6 collective-permute-done.32
  670.8 8.6 %collective-permute-done.33 = bf16[256,768]{1,0:T(8,128)(2,1)S(1)} collective-permute-done((bf16[256,768]{1,0:T(8,128)(2,1)S(1)}, bf16[256,768]{1,0:T(8,128)(2,1)S(1)}, u32[]{:S(2)}, u32[]{:S(2)}) %collective-permute-start.33) | collective-permute-done | bytes 393248 | tf_op jit(solution)/shard_map/ppermute | solution.py:591
  680.9 4.4 convolution_convert_fusion.5
  686.2 10.8 %collective-permute-done.34 = bf16[256,768]{1,0:T(8,128)(2,1)S(1)} collective-permute-done((bf16[256,768]{1,0:T(8,128)(2,1)S(1)}, bf16[256,768]{1,0:T(8,128)(2,1)S(1)}, u32[]{:S(2)}, u32[]{:S(2)}) %collective-permute-start.34) | collective-permute-done | bytes 393248 | tf_op jit(solution)/shard_map/ppermute | solution.py:591
  (367 shorter events, 144.7 us)
Async XLA Ops:
  7.2 78.1 %all-gather.3.cloned.1.call-start = ((), (), s32[]{:S(2)}) async-start(), calls=%async_computation.6 | async-start | bytes 8257536 | tf_op jit(solution)/shard_map/all_gather | solution.py:749
  14.1 202.5 %all-gather.5.cloned.1.call-start = ((), (), s32[]{:S(2)}) async-start(), calls=%async_computation.7 | async-start | bytes 30670848 | tf_op jit(solution)/shard_map/all_gather | solution.py:749
  30.4 31.2 %all-to-all-start = ((bf16[8,40,2048]{2,1,0:T(8,128)(2,1)}), bf16[8,40,2048]{2,1,0:T(8,128)(2,1)S(1)}, u32[]{:S(2)}, u32[]{:S(2)}) async-start(bf16[8,40,2048]{2,1,0:T(8,128)(2,1)} %bitcast.7), calls=%async_computation | async-start | bytes 2621440 | tf_op jit(solution)/shard_map/all_to_all | solution.py:765
  36.5 255.3 %copy-start.51 = (s32[128]{0:T(128)}, s32[128]{0:T(128)S(1)}, u32[]{:S(2)}) copy-start(s32[128]{0:T(128)S(1)} %multiply_add_fusion.9) | copy-start | bytes 1540
  62.3 60.6 %copy-start.65 = (f32[128]{0:T(128)}, f32[128]{0:T(128)S(1)}, u32[]{:S(2)}) copy-start(f32[128]{0:T(128)S(1)} %get-tuple-element.309) | copy-start | bytes 1540
  62.3 22.5 %collective-permute-start.1 = (bf16[128,2048]{1,0:T(8,128)(2,1)S(1)}, bf16[128,2048]{1,0:T(8,128)(2,1)S(1)}, u32[]{:S(2)}, u32[]{:S(2)}) collective-permute-start(bf16[128,2048]{1,0:T(8,128)(2,1)S(1)} %get-tuple-element.310.refs_0_), channel_id=1, source_target_pairs={{0,2},{1,3},{2,0},{3,1},{4,6},{5,7},{6,4},{7,5},{8,10},{9,11},{10,... | collective-permute-start | bytes 1572872 | tf_op jit(solution)/shard_map/ppermute | solution.py:591
  66.9 23.9 %collective-permute-start = (bf16[128,2048]{1,0:T(8,128)(2,1)S(1)}, bf16[128,2048]{1,0:T(8,128)(2,1)S(1)}, u32[]{:S(2)}, u32[]{:S(2)}) collective-permute-start(bf16[128,2048]{1,0:T(8,128)(2,1)S(1)} %get-tuple-element.310.refs_0_), channel_id=1, source_target_pairs={{0,1},{1,0},{2,3},{3,2},{4,5},{5,4},{6,7},{7,6},{8,9},{9,8},{10,11... | collective-permute-start | bytes 1572872 | tf_op jit(solution)/shard_map/ppermute | solution.py:591
  84.8 13.3 %collective-permute-start.2 = (bf16[128,2048]{1,0:T(8,128)(2,1)S(1)}, bf16[128,2048]{1,0:T(8,128)(2,1)S(1)}, u32[]{:S(2)}, u32[]{:S(2)}) collective-permute-start(bf16[128,2048]{1,0:T(8,128)(2,1)S(1)} %collective-permute-done.1.refs_2_), channel_id=1, source_target_pairs={{0,1},{1,0},{2,3},{3,2},{4,5},{5,4},{6,7},{7,6},{8,9},{9,8},{10,11... | collective-permute-start | bytes 1572872 | tf_op jit(solution)/shard_map/ppermute | solution.py:591
  106.7 4.1 collective-permute-start.3
  121.8 9.5 %collective-permute-start.5 = (bf16[128,2048]{1,0:T(8,128)(2,1)}, bf16[128,2048]{1,0:T(8,128)(2,1)S(1)}, u32[]{:S(2)}, u32[]{:S(2)}) collective-permute-start(bf16[128,2048]{1,0:T(8,128)(2,1)} %get-tuple-element.97), channel_id=1, source_target_pairs={{0,1},{1,0},{2,3},{3,2},{4,5},{5,4},{6,7},{7,6},{8,9},{9,8},{10,11... | collective-permute-start | bytes 1572872 | tf_op jit(solution)/shard_map/ppermute | solution.py:591
  122.9 15.4 %collective-permute-start.4 = (bf16[128,2048]{1,0:T(8,128)(2,1)}, bf16[128,2048]{1,0:T(8,128)(2,1)S(1)}, u32[]{:S(2)}, u32[]{:S(2)}) collective-permute-start(bf16[128,2048]{1,0:T(8,128)(2,1)} %get-tuple-element.95), channel_id=1, source_target_pairs={{0,1},{1,0},{2,3},{3,2},{4,5},{5,4},{6,7},{7,6},{8,9},{9,8},{10,11... | collective-permute-start | bytes 1572872 | tf_op jit(solution)/shard_map/ppermute | solution.py:591
  132.4 15.9 %collective-permute-start.6 = (bf16[128,2048]{1,0:T(8,128)(2,1)S(1)}, bf16[128,2048]{1,0:T(8,128)(2,1)S(1)}, u32[]{:S(2)}, u32[]{:S(2)}) collective-permute-start(bf16[128,2048]{1,0:T(8,128)(2,1)S(1)} %add_convert_fusion.4), channel_id=1, source_target_pairs={{0,2},{1,3},{2,0},{3,1},{4,6},{5,7},{6,4},{7,5},{8,10},{9,11},{10,... | collective-permute-start | bytes 1572872 | tf_op jit(solution)/shard_map/ppermute | solution.py:591
  150.0 66.5 %copy-start.59 = (f32[128]{0:T(128)}, f32[128]{0:T(128)S(1)}, u32[]{:S(2)}) copy-start(f32[128]{0:T(128)S(1)} %get-tuple-element.308) | copy-start | bytes 1540
  150.2 66.4 %copy-start.4 = (bf16[128,2048]{1,0:T(8,128)(2,1)}, bf16[128,2048]{1,0:T(8,128)(2,1)S(1)}, u32[]{:S(2)}) copy-start(bf16[128,2048]{1,0:T(8,128)(2,1)S(1)} %multiply_convert_fusion.refs_0_.refs_5_) | copy-start | bytes 1572868
  150.2 25.7 %collective-permute-start.8 = (bf16[128,2048]{1,0:T(8,128)(2,1)S(1)}, bf16[128,2048]{1,0:T(8,128)(2,1)S(1)}, u32[]{:S(2)}, u32[]{:S(2)}) collective-permute-start(bf16[128,2048]{1,0:T(8,128)(2,1)S(1)} %multiply_convert_fusion.refs_0_.refs_5_), channel_id=1, source_target_pairs={{0,2},{1,3},{2,0},{3,1},{4,6},{5,7},{6,4},{7,5},{8,10},{9,11},{10,... | collective-permute-start | bytes 1572872 | tf_op jit(solution)/shard_map/ppermute | solution.py:591
  150.3 70.6 %collective-permute-start.7 = (bf16[128,2048]{1,0:T(8,128)(2,1)S(1)}, bf16[128,2048]{1,0:T(8,128)(2,1)}, u32[]{:S(2)}, u32[]{:S(2)}) collective-permute-start(bf16[128,2048]{1,0:T(8,128)(2,1)S(1)} %multiply_convert_fusion.refs_0_.refs_5_), channel_id=1, source_target_pairs={{0,1},{1,0},{2,3},{3,2},{4,5},{5,4},{6,7},{7,6},{8,9},{9,8},{10,11... | collective-permute-start | bytes 1572872 | tf_op jit(solution)/shard_map/ppermute | solution.py:591
  175.9 45.0 %collective-permute-start.9 = (bf16[128,2048]{1,0:T(8,128)(2,1)S(1)}, bf16[128,2048]{1,0:T(8,128)(2,1)}, u32[]{:S(2)}, u32[]{:S(2)}) collective-permute-start(bf16[128,2048]{1,0:T(8,128)(2,1)S(1)} %collective-permute-done.8.refs_2_.refs_7_), channel_id=1, source_target_pairs={{0,1},{1,0},{2,3},{3,2},{4,5},{5,4},{6,7},{7,6},{8,9},{9,8},{10,11... | collective-permute-start | bytes 1572872 | tf_op jit(solution)/shard_map/ppermute | solution.py:591
  216.6 26.4 %all-to-all-start.1 = ((bf16[8,40,2304]{2,1,0:T(8,128)(2,1)}), bf16[8,40,2304]{2,1,0:T(8,128)(2,1)}, u32[]{:S(2)}, u32[]{:S(2)}) async-start(bf16[8,40,2304]{2,1,0:T(8,128)(2,1)} %bitcast.108), calls=%async_computation.1 | async-start | bytes 2949120 | tf_op jit(solution)/shard_map/all_to_all | solution.py:823
  243.0 15.0 %collective-permute-start.11 = (bf16[128,2048]{1,0:T(8,128)(2,1)}, bf16[128,2048]{1,0:T(8,128)(2,1)S(1)}, u32[]{:S(2)}, u32[]{:S(2)}) collective-permute-start(bf16[128,2048]{1,0:T(8,128)(2,1)} %get-tuple-element.108), channel_id=1, source_target_pairs={{0,1},{1,0},{2,3},{3,2},{4,5},{5,4},{6,7},{7,6},{8,9},{9,8},{10,11... | collective-permute-start | bytes 1572872 | tf_op jit(solution)/shard_map/ppermute | solution.py:591
  244.5 33.0 %collective-permute-start.10 = (bf16[128,2048]{1,0:T(8,128)(2,1)}, bf16[128,2048]{1,0:T(8,128)(2,1)S(1)}, u32[]{:S(2)}, u32[]{:S(2)}) collective-permute-start(bf16[128,2048]{1,0:T(8,128)(2,1)} %get-tuple-element.106), channel_id=1, source_target_pairs={{0,1},{1,0},{2,3},{3,2},{4,5},{5,4},{6,7},{7,6},{8,9},{9,8},{10,11... | collective-permute-start | bytes 1572872 | tf_op jit(solution)/shard_map/ppermute | solution.py:591
  259.2 25.1 %collective-permute-start.12 = (bf16[128,2048]{1,0:T(8,128)(2,1)S(1)}, bf16[128,2048]{1,0:T(8,128)(2,1)S(1)}, u32[]{:S(2)}, u32[]{:S(2)}) collective-permute-start(bf16[128,2048]{1,0:T(8,128)(2,1)S(1)} %add_convert_fusion.3), channel_id=1, source_target_pairs={{0,2},{1,3},{2,0},{3,1},{4,6},{5,7},{6,4},{7,5},{8,10},{9,11},{10,... | collective-permute-start | bytes 1572872 | tf_op jit(solution)/shard_map/ppermute | solution.py:591
  293.6 48.2 %all-to-all-start.2 = ((bf16[8,40,2304]{2,1,0:T(8,128)(2,1)}), bf16[8,40,2304]{2,1,0:T(8,128)(2,1)}, u32[]{:S(2)}, u32[]{:S(2)}) async-start(bf16[8,40,2304]{2,1,0:T(8,128)(2,1)} %bitcast.107), calls=%async_computation.2 | async-start | bytes 2949120 | tf_op jit(solution)/shard_map/all_to_all | solution.py:776
  297.9 308.0 %reduce-scatter.3.cloned.1.call-start = ((), (), s32[]{:S(2)}) async-start(), calls=%async_computation.8 | async-start | bytes 30670848 | tf_op jit(solution)/shard_map/reduce_scatter | solution.py:784
  302.0 26.5 %collective-permute-start.14 = (bf16[128,2048]{1,0:T(8,128)(2,1)S(1)}, bf16[128,2048]{1,0:T(8,128)(2,1)S(1)}, u32[]{:S(2)}, u32[]{:S(2)}) collective-permute-start(bf16[128,2048]{1,0:T(8,128)(2,1)S(1)} %fusion.25.refs_0_.refs_10_), channel_id=1, source_target_pairs={{0,2},{1,3},{2,0},{3,1},{4,6},{5,7},{6,4},{7,5},{8,10},{9,11},{10,... | collective-permute-start | bytes 1572872 | tf_op jit(solution)/shard_map/ppermute | solution.py:591
  302.6 29.7 %collective-permute-start.13 = (bf16[128,2048]{1,0:T(8,128)(2,1)S(1)}, bf16[128,2048]{1,0:T(8,128)(2,1)S(1)}, u32[]{:S(2)}, u32[]{:S(2)}) collective-permute-start(bf16[128,2048]{1,0:T(8,128)(2,1)S(1)} %fusion.25.refs_0_.refs_10_), channel_id=1, source_target_pairs={{0,1},{1,0},{2,3},{3,2},{4,5},{5,4},{6,7},{7,6},{8,9},{9,8},{10,11... | collective-permute-start | bytes 1572872 | tf_op jit(solution)/shard_map/ppermute | solution.py:591
  328.4 13.4 %collective-permute-start.15 = (bf16[128,2048]{1,0:T(8,128)(2,1)S(1)}, bf16[128,2048]{1,0:T(8,128)(2,1)}, u32[]{:S(2)}, u32[]{:S(2)}) collective-permute-start(bf16[128,2048]{1,0:T(8,128)(2,1)S(1)} %collective-permute-done.14.refs_2_.refs_12_), channel_id=1, source_target_pairs={{0,1},{1,0},{2,3},{3,2},{4,5},{5,4},{6,7},{7,6},{8,9},{9,8},{10,11... | collective-permute-start | bytes 1572872 | tf_op jit(solution)/shard_map/ppermute | solution.py:591
  343.7 27.9 %collective-permute-start.16 = (bf16[136,2304]{1,0:T(8,128)(2,1)S(1)}, bf16[136,2304]{1,0:T(8,128)(2,1)}, u32[]{:S(2)}, u32[]{:S(2)}) collective-permute-start(bf16[136,2304]{1,0:T(8,128)(2,1)S(1)} %convolution_convert_fusion.3), channel_id=1, source_target_pairs={{0,1},{1,0},{2,3},{3,2},{4,5},{5,4},{6,7},{7,6},{8,9},{9,8},{10,11... | collective-permute-start | bytes 1880072 | tf_op jit(solution)/shard_map/ppermute | solution.py:591
  344.1 29.1 %collective-permute-start.17 = (bf16[136,2304]{1,0:T(8,128)(2,1)S(1)}, bf16[136,2304]{1,0:T(8,128)(2,1)}, u32[]{:S(2)}, u32[]{:S(2)}) collective-permute-start(bf16[136,2304]{1,0:T(8,128)(2,1)S(1)} %convolution_convert_fusion.3), channel_id=1, source_target_pairs={{0,2},{1,3},{2,0},{3,1},{4,6},{5,7},{6,4},{7,5},{8,10},{9,11},{10,... | collective-permute-start | bytes 1880072 | tf_op jit(solution)/shard_map/ppermute | solution.py:591
  373.1 20.7 %collective-permute-start.19 = (bf16[128,2048]{1,0:T(8,128)(2,1)}, bf16[128,2048]{1,0:T(8,128)(2,1)S(1)}, u32[]{:S(2)}, u32[]{:S(2)}) collective-permute-start(bf16[128,2048]{1,0:T(8,128)(2,1)} %get-tuple-element.128), channel_id=1, source_target_pairs={{0,1},{1,0},{2,3},{3,2},{4,5},{5,4},{6,7},{7,6},{8,9},{9,8},{10,11... | collective-permute-start | bytes 1572872 | tf_op jit(solution)/shard_map/ppermute | solution.py:591
  373.4 44.8 %collective-permute-start.18 = (bf16[128,2048]{1,0:T(8,128)(2,1)}, bf16[128,2048]{1,0:T(8,128)(2,1)S(1)}, u32[]{:S(2)}, u32[]{:S(2)}) collective-permute-start(bf16[128,2048]{1,0:T(8,128)(2,1)} %get-tuple-element.126), channel_id=1, source_target_pairs={{0,1},{1,0},{2,3},{3,2},{4,5},{5,4},{6,7},{7,6},{8,9},{9,8},{10,11... | collective-permute-start | bytes 1572872 | tf_op jit(solution)/shard_map/ppermute | solution.py:591
  395.8 22.4 %collective-permute-start.20 = (bf16[128,2048]{1,0:T(8,128)(2,1)}, bf16[128,2048]{1,0:T(8,128)(2,1)}, u32[]{:S(2)}, u32[]{:S(2)}) collective-permute-start(bf16[128,2048]{1,0:T(8,128)(2,1)} %add_convert_fusion.1), channel_id=1, source_target_pairs={{0,2},{1,3},{2,0},{3,1},{4,6},{5,7},{6,4},{7,5},{8,10},{9,11},{10,... | collective-permute-start | bytes 1572872 | tf_op jit(solution)/shard_map/ppermute | solution.py:591
  418.3 248.5 %reduce-scatter.5.cloned.1.call-start = ((), (), s32[]{:S(2)}) async-start(), calls=%async_computation.9 | async-start | bytes 4587520 | tf_op jit(solution)/shard_map/reduce_scatter | solution.py:784
  426.2 14.7 %collective-permute-start.22 = (bf16[128,2048]{1,0:T(8,128)(2,1)S(1)}, bf16[128,2048]{1,0:T(8,128)(2,1)S(1)}, u32[]{:S(2)}, u32[]{:S(2)}) collective-permute-start(bf16[128,2048]{1,0:T(8,128)(2,1)S(1)} %get-tuple-element.278.rest_0_.refs_2_), channel_id=1, source_target_pairs={{0,2},{1,3},{2,0},{3,1},{4,6},{5,7},{6,4},{7,5},{8,10},{9,11},{10,... | collective-permute-start | bytes 1572872 | tf_op jit(solution)/shard_map/ppermute | solution.py:591
  431.5 49.9 %collective-permute-start.24 = (bf16[136,2304]{1,0:T(8,128)(2,1)}, bf16[136,2304]{1,0:T(8,128)(2,1)}, u32[]{:S(2)}, u32[]{:S(2)}) collective-permute-start(bf16[136,2304]{1,0:T(8,128)(2,1)} %collective-permute-done.17), channel_id=1, source_target_pairs={{0,1},{1,0},{2,3},{3,2},{4,5},{5,4},{6,7},{7,6},{8,9},{9,8},{10,11... | collective-permute-start | bytes 1880072 | tf_op jit(solution)/shard_map/ppermute | solution.py:591
  431.5 30.2 %collective-permute-start.21 = (bf16[128,2048]{1,0:T(8,128)(2,1)S(1)}, bf16[128,2048]{1,0:T(8,128)(2,1)}, u32[]{:S(2)}, u32[]{:S(2)}) collective-permute-start(bf16[128,2048]{1,0:T(8,128)(2,1)S(1)} %get-tuple-element.278.rest_0_.refs_2_), channel_id=1, source_target_pairs={{0,1},{1,0},{2,3},{3,2},{4,5},{5,4},{6,7},{7,6},{8,9},{9,8},{10,11... | collective-permute-start | bytes 1572872 | tf_op jit(solution)/shard_map/ppermute | solution.py:591
  440.9 26.4 %collective-permute-start.23 = (bf16[128,2048]{1,0:T(8,128)(2,1)S(1)}, bf16[128,2048]{1,0:T(8,128)(2,1)}, u32[]{:S(2)}, u32[]{:S(2)}) collective-permute-start(bf16[128,2048]{1,0:T(8,128)(2,1)S(1)} %collective-permute-done.22.rest_2_.refs_4_), channel_id=1, source_target_pairs={{0,1},{1,0},{2,3},{3,2},{4,5},{5,4},{6,7},{7,6},{8,9},{9,8},{10,11... | collective-permute-start | bytes 1572872 | tf_op jit(solution)/shard_map/ppermute | solution.py:591
  479.9 4.0 collective-permute-start.25
  502.2 36.6 %collective-permute-start.29 = (bf16[1024,1792]{1,0:T(8,128)(2,1)}, bf16[1024,1792]{1,0:T(8,128)(2,1)}, u32[]{:S(2)}, u32[]{:S(2)}) collective-permute-start(bf16[1024,1792]{1,0:T(8,128)(2,1)} %attention_grads.2), channel_id=1, source_target_pairs={{0,4},{4,0},{8,12},{12,8},{16,20},{20,16},{24,28},{28,24},{1,5},{5... | collective-permute-start | bytes 11010056 | tf_op jit(solution)/shard_map/ppermute | solution.py:591
  521.5 14.8 %collective-permute-start.27 = (bf16[128,2048]{1,0:T(8,128)(2,1)S(1)}, bf16[128,2048]{1,0:T(8,128)(2,1)S(1)}, u32[]{:S(2)}, u32[]{:S(2)}) collective-permute-start(bf16[128,2048]{1,0:T(8,128)(2,1)S(1)} %copy-done.75), channel_id=1, source_target_pairs={{0,1},{1,0},{2,3},{3,2},{4,5},{5,4},{6,7},{7,6},{8,9},{9,8},{10,11... | collective-permute-start | bytes 1572872 | tf_op jit(solution)/shard_map/ppermute | solution.py:591
  521.5 32.4 %collective-permute-start.26 = (bf16[128,2048]{1,0:T(8,128)(2,1)}, bf16[128,2048]{1,0:T(8,128)(2,1)}, u32[]{:S(2)}, u32[]{:S(2)}) collective-permute-start(bf16[128,2048]{1,0:T(8,128)(2,1)} %get-tuple-element.157), channel_id=1, source_target_pairs={{0,1},{1,0},{2,3},{3,2},{4,5},{5,4},{6,7},{7,6},{8,9},{9,8},{10,11... | collective-permute-start | bytes 1572872 | tf_op jit(solution)/shard_map/ppermute | solution.py:591
  537.2 24.8 %collective-permute-start.28 = (bf16[128,2048]{1,0:T(8,128)(2,1)}, bf16[128,2048]{1,0:T(8,128)(2,1)}, u32[]{:S(2)}, u32[]{:S(2)}) collective-permute-start(bf16[128,2048]{1,0:T(8,128)(2,1)} %add_convert_fusion), channel_id=1, source_target_pairs={{0,2},{1,3},{2,0},{3,1},{4,6},{5,7},{6,4},{7,5},{8,10},{9,11},{10,... | collective-permute-start | bytes 1572872 | tf_op jit(solution)/shard_map/ppermute | solution.py:591
  612.4 34.6 %collective-permute-start.31 = (bf16[136,2048]{1,0:T(8,128)(2,1)S(1)}, bf16[136,2048]{1,0:T(8,128)(2,1)S(1)}, u32[]{:S(2)}, u32[]{:S(2)}) collective-permute-start(bf16[136,2048]{1,0:T(8,128)(2,1)S(1)} %fusion.13), channel_id=1, source_target_pairs={{0,2},{1,3},{2,0},{3,1},{4,6},{5,7},{6,4},{7,5},{8,10},{9,11},{10,... | collective-permute-start | bytes 1671176 | tf_op jit(solution)/shard_map/ppermute | solution.py:591
  614.8 46.9 %collective-permute-start.30 = (bf16[136,2048]{1,0:T(8,128)(2,1)S(1)}, bf16[136,2048]{1,0:T(8,128)(2,1)}, u32[]{:S(2)}, u32[]{:S(2)}) collective-permute-start(bf16[136,2048]{1,0:T(8,128)(2,1)S(1)} %fusion.13), channel_id=1, source_target_pairs={{0,1},{1,0},{2,3},{3,2},{4,5},{5,4},{6,7},{7,6},{8,9},{9,8},{10,11... | collective-permute-start | bytes 1671176 | tf_op jit(solution)/shard_map/ppermute | solution.py:591
  616.4 29.1 %collective-permute-start.35 = (bf16[256,512]{1,0:T(8,128)(2,1)S(1)}, bf16[256,512]{1,0:T(8,128)(2,1)S(1)}, u32[]{:S(2)}, u32[]{:S(2)}) collective-permute-start(bf16[256,512]{1,0:T(8,128)(2,1)S(1)} %slice.225), channel_id=1, source_target_pairs={{0,1},{1,0},{2,3},{3,2},{4,5},{5,4},{6,7},{7,6},{8,9},{9,8},{10,11... | collective-permute-start | bytes 786440 | tf_op jit(solution)/shard_map/ppermute | solution.py:591
  645.5 13.6 %collective-permute-start.36 = (bf16[256,512]{1,0:T(8,128)(2,1)S(1)}, bf16[256,512]{1,0:T(8,128)(2,1)}, u32[]{:S(2)}, u32[]{:S(2)}) collective-permute-start(bf16[256,512]{1,0:T(8,128)(2,1)S(1)} %add_convert_fusion.6), channel_id=1, source_target_pairs={{0,2},{1,3},{2,0},{3,1},{4,6},{5,7},{6,4},{7,5},{8,10},{9,11},{10,... | collective-permute-start | bytes 786440 | tf_op jit(solution)/shard_map/ppermute | solution.py:591
  646.9 18.4 %collective-permute-start.32 = (bf16[136,2048]{1,0:T(8,128)(2,1)S(1)}, bf16[136,2048]{1,0:T(8,128)(2,1)}, u32[]{:S(2)}, u32[]{:S(2)}) collective-permute-start(bf16[136,2048]{1,0:T(8,128)(2,1)S(1)} %collective-permute-done.31), channel_id=1, source_target_pairs={{0,1},{1,0},{2,3},{3,2},{4,5},{5,4},{6,7},{7,6},{8,9},{9,8},{10,11... | collective-permute-start | bytes 1671176 | tf_op jit(solution)/shard_map/ppermute | solution.py:591
  669.8 9.6 %collective-permute-start.33 = (bf16[256,768]{1,0:T(8,128)(2,1)S(1)}, bf16[256,768]{1,0:T(8,128)(2,1)S(1)}, u32[]{:S(2)}, u32[]{:S(2)}) collective-permute-start(bf16[256,768]{1,0:T(8,128)(2,1)S(1)} %pad_maximum_fusion.3), channel_id=1, source_target_pairs={{0,1},{1,0},{2,3},{3,2},{4,5},{5,4},{6,7},{7,6},{8,9},{9,8},{10,11... | collective-permute-start | bytes 1179656 | tf_op jit(solution)/shard_map/ppermute | solution.py:591
  679.5 17.6 %collective-permute-start.34 = (bf16[256,768]{1,0:T(8,128)(2,1)S(1)}, bf16[256,768]{1,0:T(8,128)(2,1)S(1)}, u32[]{:S(2)}, u32[]{:S(2)}) collective-permute-start(bf16[256,768]{1,0:T(8,128)(2,1)S(1)} %add_convert_fusion.5), channel_id=1, source_target_pairs={{0,2},{1,3},{2,0},{3,1},{4,6},{5,7},{6,4},{7,5},{8,10},{9,11},{10,... | collective-permute-start | bytes 1179656 | tf_op jit(solution)/shard_map/ppermute | solution.py:591
  (72 other events, 938.8 us)
Sparse Core Ops, SparseCore 0:
  14.2 60.2 all-gather.2
  76.9 139.6 all-gather.4
  418.4 187.5 reduce-scatter.2
  608.8 48.3 reduce-scatter.4

commit v4 on v3

--- a/solution.py
+++ b/solution.py
@@ -752,22 +752,12 @@
     first = [w_query, kv_own[0], kv_own[1], w_out.T, w_left, w_right.T, gain_cols]
     bundle_a, (wq, wk, wv, wo_t, wl, wr_t, gain_f) = gather_columns(first)
     units = w_down.shape[0]
-    flat = jnp.concatenate(
-        [
-            hidden_in.reshape(tok, width),
-            layer_inputs.reshape(tok, per_width),
-            out_grad.reshape(tok, width),
-        ],
-        axis=1,
-    )
-    packed = product(sender, flat, bf16)
-    first_cols = width + per_width
-    come_in = lax.all_to_all(packed[:, :width], "dp", 0, 0, tiled=True)
+    packed_in = product(sender, hidden_in.reshape(tok, width), bf16)
+    come_in = lax.all_to_all(packed_in, "dp", 0, 0, tiled=True)
     low_inputs = product(receiver, come_in, bf16)
     inputs = low_inputs.astype(f32)
     token_pieces = spread_start(low_inputs, "tensor")
-    second = [w_gateup[0], w_gateup[1], w_down.T, w_pergate, w_perproj.T]
-    w_ff, (_, _, _, wg, wp_t) = gather_columns(second)
+    w_ff, _ = gather_columns([w_gateup[0], w_gateup[1], w_down.T])
     w_gains = gain_f.T
     gains_f = w_gains[:6].astype(f32) + w_gains[6:12].astype(f32)
     angles = own_pos.astype(f32)[:, None] * frequencies()
@@ -780,25 +770,24 @@
     low_bit = me % 2
     groups = [list(range(k, devices, 2)) for k in range(2)] if paired else None
 
-    def scattered(grads, swap):
+    def scattered(grads):
         return lax.psum_scatter(
-            grads,
-            "dp",
-            scatter_dimension=0,
-            axis_index_groups=groups if swap else None,
-            tiled=True,
+            grads, "dp", scatter_dimension=0, axis_index_groups=groups, tiled=True
         )
 
-    def grads_beside_fold(chunks, products, others, name, swap):
-        def make(*where):
-            return column_grads(products, others, name, *where)
-
-        if not (paired and swap):
-            return fold_start(chunks, "tensor"), make(2 * LANES, 1, jnp.zeros((), jnp.int32))
-        leaving = make(block, 2, 1 - low_bit)
-        chunks, leaving = with_work(chunks, leaving)
-        pieces = fold_start(chunks, "tensor")
-        return pieces, make(block, 2, low_bit, crossed(leaving, "dp", 1))
+    def grads_leaving(make):
+        return make(block, 2, 1 - low_bit) if paired else make(2 * LANES, 1, me * 0)
+
+    def beside_first(chunks, work):
+        chunks = list(chunks)
+        chunks[-2], work = with_work(chunks[-2], work)
+        return chunks, work
+
+    def grads_come(leaving):
+        return crossed(leaving, "dp", 1) if paired else leaving
+
+    def grads_staying(make, come):
+        return make(block, 2, low_bit, come) if paired else come
 
     cosine, sine = jnp.cos(angles), jnp.sin(angles)
     heads = q_width // HD
@@ -819,7 +808,13 @@
     low_mid = normed(first_sum, gains_f[3]).astype(bf16)
 
     all_mid = [low_mid] + spread_start(low_mid, "tensor")
-    rest_out, w_ff = with_work(packed[:, width:], w_ff)
+    rest_in = jnp.concatenate(
+        [layer_inputs.reshape(tok, per_width), out_grad.reshape(tok, width)], axis=1
+    )
+    third = [w_pergate, w_perproj.T]
+    rest_out = product(sender, rest_in, bf16)
+    (rest_out, third), w_ff = with_work((rest_out, third), w_ff)
+    _, (wg, wp_t) = gather_columns(third)
     come_rest = lax.all_to_all(rest_out, "dp", 0, 0, tiled=True)
     gate_raw, upward, low_hidden, feed_parts = feed_forward(all_mid, w_ff, units)
     feed_parts, come_rest = with_work(feed_parts, come_rest)
@@ -864,15 +859,19 @@
     mid_parts, home_pieces[0] = with_work(mid_parts, home_pieces[0])
     mid_parts, home_pieces[1] = with_work(mid_parts, home_pieces[1])
 
-    mid_pieces, ff_grads = grads_beside_fold(
-        mid_parts,
-        [(all_mid, low_gate), (all_mid, low_up), (all_feed, low_hidden)],
-        [grad_pergate, grad_perproj],
-        "feed_grads",
-        False,
-    )
+    def ff_grads_of(*where):
+        return column_grads(
+            [(all_mid, low_gate), (all_mid, low_up), (all_feed, low_hidden)],
+            [grad_pergate, grad_perproj],
+            "feed_grads",
+            *where,
+        )
+
+    mid_parts, ff_leaving = beside_first(mid_parts, grads_leaving(ff_grads_of))
+    mid_pieces = fold_start(mid_parts, "tensor")
+    ff_grads = grads_staying(ff_grads_of, grads_come(ff_leaving))
     mid_pieces, ff_grads = with_work(mid_pieces, ff_grads)
-    s_ff = scattered(ff_grads, False)
+    s_ff = scattered(ff_grads)
     mid_grad = summed(mid_pieces)
 
     _, back_mid = jax.vjp(normed, first_sum, gains_f[3])
@@ -908,14 +907,17 @@
     head_cols = jnp.tile(head_cols, (1, devices))
     last_cols = jnp.concatenate([gain_part, head_cols], axis=0).astype(bf16)
     last_cols = jnp.pad(last_cols, ((0, LANES - last_cols.shape[0]), (0, 0))).T
-    in_pieces, at_grads = grads_beside_fold(
-        in_parts,
-        [([all_in], low_qkv), (all_branch, low_att)],
-        [small, last_cols],
-        "attention_grads",
-        True,
-    )
-    in_pieces, at_grads = with_work(in_pieces, at_grads)
+    def at_grads_of(*where):
+        return column_grads(
+            [([all_in], low_qkv), (all_branch, low_att)],
+            [small, last_cols],
+            "attention_grads",
+            *where,
+        )
+
+    in_parts, at_leaving = beside_first(in_parts, grads_leaving(at_grads_of))
+    in_pieces = fold_start(in_parts, "tensor")
+    in_pieces, at_come = with_work(in_pieces, grads_come(at_leaving))
     in_attn = summed(in_pieces)
     normal_grad = in_attn + against(low_rank_grad, wl) + shared
     _, back_in = jax.vjp(normed, inputs, gains_f[0])
@@ -927,38 +929,41 @@
     )
     sent_two = across(receiver, input_grad.astype(bf16)) + extra.reshape(-1, width)
     come_two = lax.all_to_all(sent_two.astype(bf16), "dp", 0, 0, tiled=True)
-    at_grads, (s_ff, come_two) = with_work(at_grads, (s_ff, come_two))
-    s_at = scattered(at_grads, True)
+    at_grads = grads_staying(at_grads_of, at_come)
+    at_grads, s_ff = with_work(at_grads, s_ff)
+    s_at = scattered(at_grads)
     early = s_ff[:, 3 * units :]
     bit = 1
     while bit < parts:
         early = summed([early, crossed(early, "tensor", bit)])
         early = early.astype(bf16) if 2 * bit < parts else early
         bit *= 2
+    come_two, early = with_work(come_two, early)
     g0_part = jnp.sum(come_two.reshape(devices, -1, width)[:, -1, :block].astype(f32), axis=0)
     home_two = product(compact, come_two) + jnp.pad(
         g0_part[None], ((compact.shape[0] - 1, 0), (0, width - block))
     )
-    home_two = home_two.astype(bf16)
-    all_two = jnp.concatenate([home_two] + spread_start(home_two, "tensor"), axis=0)
-    back_two = product(homing, all_two, bf16)
-    g0_terms = all_two.reshape(parts, -1, width)[:, -1, :block].astype(f32)
-    while g0_terms.shape[0] > 1:
-        middle = g0_terms.shape[0] // 2
-        g0_terms = g0_terms[:middle] + g0_terms[middle:]
-
-    shard_gateup = jnp.stack([s_ff[:, :units], s_ff[:, units : 2 * units]]).astype(f32)
-    shard_down = s_ff[:, 2 * units : 3 * units].T.astype(f32)
     o_kv = q_width + 2 * HD
     o_small = o_kv + w_out.shape[0]
-    shard_query = s_at[:, :q_width].astype(f32)
-    shard_out = s_at[:, o_kv:o_small].T.astype(f32)
     kv_cols = 2 * HD
     exchanged = jnp.concatenate([s_at[:, q_width:o_kv], s_at[:, o_small:]], axis=1)
     bit = 1
     while bit < parts // KVH:
         exchanged = summed([exchanged, crossed(exchanged, "tensor", bit)]).astype(bf16)
         bit *= 2
+    home_two = home_two.astype(bf16)
+    two_pieces, exchanged = with_work(spread_start(home_two, "tensor"), exchanged)
+    all_two = jnp.concatenate([home_two] + two_pieces, axis=0)
+    back_two = product(homing, all_two, bf16)
+    g0_terms = all_two.reshape(parts, -1, width)[:, -1, :block].astype(f32)
+    while g0_terms.shape[0] > 1:
+        middle = g0_terms.shape[0] // 2
+        g0_terms = g0_terms[:middle] + g0_terms[middle:]
+
+    shard_gateup = jnp.stack([s_ff[:, :units], s_ff[:, units : 2 * units]]).astype(f32)
+    shard_down = s_ff[:, 2 * units : 3 * units].T.astype(f32)
+    shard_query = s_at[:, :q_width].astype(f32)
+    shard_out = s_at[:, o_kv:o_small].T.astype(f32)
     arrived = crossed(exchanged, "tensor", bit)
     kv_sum, kv_other = exchanged[:, :kv_cols], arrived[:, :kv_cols]
     small_sum = summed([exchanged[:, kv_cols:], arrived[:, kv_cols:]])

time: 718 us -> 711 us (level)
  blocking collectives: 35.5 us -> 0 us
  waiting for transfers between devices: 329 us -> 351 us
  Pallas kernels: 122 us -> 131 us
  other arithmetic: 38.3 us -> 45.5 us
    all_to_all x1 -> x0, blocking collectives: 35.5 us -> none  [body(): come_two = lax.all_to_all(sent_two.astype(bf16), 'dp', 0, 0, tiled=True)]
    ppermute x35 -> x36, waiting for transfers between devices: 256 us -> 278 us  [crossed(): return lax.ppermute(piece, axis, [(i, i ^ bit) for i in range(length)])]
    ppermute x35 -> x36, starting transfers between devices: 67.1 us -> 58.3 us  [crossed(): return lax.ppermute(piece, axis, [(i, i ^ bit) for i in range(length)])]
    pallas_call x3 -> x4, Pallas kernels: 34.9 us -> 43.6 us  [column_grads(): pl.pallas_call(kernel, out_shape=jax.ShapeDtypeStruct((width // every, to...]
    unnamed x169 -> x166, local copies, waits for them, and re-layouts: 21 us -> 15.7 us
    all_gather x2 -> x3, waiting for transfers between devices: 39.2 us -> 43.7 us  [gather_columns(): lax.all_gather(jnp.concatenate(pieces, axis=1), 'dp', axis=0, tiled=True)]
    all_to_all x1 -> x2, waiting for transfers between devices: 25.2 us -> 27.5 us  [the longest x1 21.3 us: body(): come_in = lax.all_to_all(packed_in, 'dp', 0, 0, tiled=True)]
    dot_general x11 -> x12, matrix products: 23.8 us -> 23.8 us  [product(): return jnp.dot(left_mat, right_mat, preferred_element_type=f32).astype(kind)]
  transfers between devices with their start and end apart: 44 -> 47, of which waited for: 28 -> 29; matrix products, arithmetic and copies ran while one was open for 13% -> 14% of each run, Pallas kernels for 17% -> 19%
where the time goes in v4:
time: 711 us; the launch traced here: 703 us
  waiting for transfers between devices  351 us (49%)
  Pallas kernels  131 us (18%)
  starting transfers between devices  80.2 us (11%)
  other arithmetic  45.5 us (6%)
  matrix products  40.8 us (6%)
  local copies, waits for them, and re-layouts  38.9 us (5%)
  between operations  15.6 us (2%)
    ppermute x36, waiting for transfers between devices, crossed(): return lax.ppermute(piece, axis, [(i, i ^ bit) for i in range(length)])  278 us
    ppermute x36, starting transfers between devices, crossed(): return lax.ppermute(piece, axis, [(i, i ^ bit) for i in range(length)])  58.3 us
    all_gather x3, waiting for transfers between devices, gather_columns(): lax.all_gather(jnp.concatenate(pieces, axis=1), 'dp', axis=0, tiled=True)  43.7 us
    pallas_call x4, Pallas kernels, column_grads(): pl.pallas_call(kernel, out_shape=jax.ShapeDtypeStruct((width // every, to...  43.6 us
    pallas_call x1, Pallas kernels, feed_back(): pl.pallas_call(kernel, out_shape=[jax.ShapeDtypeStruct((tok, units), bf16...  24.9 us
    dot_general x12, matrix products, product(): return jnp.dot(left_mat, right_mat, preferred_element_type=f32).astype(kind)  23.8 us
    pallas_call x1, Pallas kernels, feed_forward(): pl.pallas_call(kernel, out_shape=[jax.ShapeDtypeStruct((tok, units), bf16...  21.7 us
    all_to_all x1, waiting for transfers between devices, body(): come_in = lax.all_to_all(packed_in, 'dp', 0, 0, tiled=True)  21.3 us
  transfers between devices with their start and end apart: 47, of which 29 were waited for; matrix products, arithmetic and copies ran while one was open for 14% of the time, Pallas kernels for 19%

profile of v4, /device:TPU:0, one launch (start us, length us, event | category | flops | bytes accessed | tf_op | source)
XLA Modules:
  0.0 702.9 jit_solution(18097161929149353316)
XLA Ops:
  24.7 5.2 all-to-all-start
  30.8 21.3 %all-to-all-done = bf16[8,40,2048]{2,1,0:T(8,128)(2,1)S(1)} async-done(((bf16[8,40,2048]{2,1,0:T(8,128)(2,1)}), bf16[8,40,2048]{2,1,0:T(8,128)(2,1)S(1)}, u32[]{:S(2)}, u32[]{:S(2)}) %all-to-all-start) | async-done | bytes 1310752 | tf_op jit(solution)/shard_map/all_to_all | solution.py:756
  58.5 17.6 %collective-permute-done.1.refs_2_ = bf16[128,2048]{1,0:T(8,128)(2,1)} collective-permute-done((bf16[128,2048]{1,0:T(8,128)(2,1)S(1)}, bf16[128,2048]{1,0:T(8,128)(2,1)}, u32[]{:S(2)}, u32[]{:S(2)}) %collective-permute-start.1) | collective-permute-done | bytes 524320 | tf_op jit(solution)/shard_map/ppermute | solution.py:591
  83.7 5.5 collective-permute-done.2.refs_3_
  89.2 8.8 %project.1 = (bf16[512,2048]{1,0:T(8,128)(2,1)}, f32[512,1024]{1,0:T(8,128)}, bf16[512,512]{1,0:T(8,128)(2,1)}, bf16[512,512]{1,0:T(8,128)(2,1)}) custom-call(bf16[128,2048]{1,0:T(8,128)(2,1)} %copy-done.5, bf16[128,2048]{1,0:T(8,128)(2,1)} %collective-permute-done.refs_1_, bf16[128,2048]{1,0:T(8,128)(2,1)} %collective-permute-done.1.refs_2_, ...), custom_call_target="tpu_custom_call" | custom-call | flops 2147483648 | bytes 1024 | tf_op jit(solution)/shard_map/project/pallas_call | solution.py:153
  102.8 10.1 %attend.1 = (bf16[512,512]{1,0:T(8,128)(2,1)}, bf16[128,2048]{1,0:T(8,128)(2,1)}, bf16[128,2048]{1,0:T(8,128)(2,1)}, bf16[128,2048]{1,0:T(8,128)(2,1)}, bf16[128,2048]{1,0:T(8,128)(2,1)}) custom-call(bf16[512,512]{1,0:T(8,128)(2,1)} %get-tuple-element.98.q_ref, bf16[512,512]{1,0:T(8,128)(2,1)} %copy-done.34, bf16[512,512]{1,0:T(8,128)(2,1)} %get-tuple-element.99.o_ref, ...), custom_call_target="tpu_custom_call" | custom-call | flops 1073741824 | bytes 1024 | tf_op jit(solution)/shard_map/attend/pallas_call | solution.py:217
  115.1 7.3 %collective-permute-done.5 = bf16[128,2048]{1,0:T(8,128)(2,1)S(1)} collective-permute-done((bf16[128,2048]{1,0:T(8,128)(2,1)}, bf16[128,2048]{1,0:T(8,128)(2,1)S(1)}, u32[]{:S(2)}, u32[]{:S(2)}) %collective-permute-start.5) | collective-permute-done | bytes 524320 | tf_op jit(solution)/shard_map/ppermute | solution.py:591
  123.6 3.5 collective-permute-start.6
  130.1 9.8 %collective-permute-done.6 = bf16[128,2048]{1,0:T(8,128)(2,1)S(1)} collective-permute-done((bf16[128,2048]{1,0:T(8,128)(2,1)S(1)}, bf16[128,2048]{1,0:T(8,128)(2,1)S(1)}, u32[]{:S(2)}, u32[]{:S(2)}) %collective-permute-start.6) | collective-permute-done | bytes 524320 | tf_op jit(solution)/shard_map/ppermute | solution.py:591
  142.0 4.4 collective-permute-start.7
  146.4 20.4 %collective-permute-done.8.refs_2_.refs_7_ = bf16[128,2048]{1,0:T(8,128)(2,1)S(1)} collective-permute-done((bf16[128,2048]{1,0:T(8,128)(2,1)S(1)}, bf16[128,2048]{1,0:T(8,128)(2,1)S(1)}, u32[]{:S(2)}, u32[]{:S(2)}) %collective-permute-start.8) | collective-permute-done | bytes 524320 | tf_op jit(solution)/shard_map/ppermute | solution.py:591
  169.6 41.8 %all-gather.6.cloned.1.call-done.refs_4_.refs_5_.refs_6_ = bf16[2048,6144]{1,0:T(8,128)(2,1)} async-done(((bf16[256,6144]{1,0:T(8,128)(2,1)}), bf16[2048,6144]{1,0:T(8,128)(2,1)}) %all-gather.6.cloned.1.call-update) | async-done | bytes 25165840 | tf_op jit(solution)/shard_map/all_gather | solution.py:749
  211.4 4.3 all-to-all-start.1
  218.1 21.7 %feed_forward.1 = (bf16[512,2048]{1,0:T(8,128)(2,1)}, bf16[512,2048]{1,0:T(8,128)(2,1)}, bf16[512,2048]{1,0:T(8,128)(2,1)}, bf16[128,2048]{1,0:T(8,128)(2,1)}, b...) custom-call(bf16[128,2048]{1,0:T(8,128)(2,1)} %copy-done.3, ...), custom_call_target="tpu_custom_call" | custom-call | flops 12884901888 | bytes 1024 | tf_op jit(solution)/shard_map/feed_forward/pallas_call | solution.py:460
  241.9 12.9 %collective-permute-done.11 = bf16[128,2048]{1,0:T(8,128)(2,1)S(1)} collective-permute-done((bf16[128,2048]{1,0:T(8,128)(2,1)}, bf16[128,2048]{1,0:T(8,128)(2,1)S(1)}, u32[]{:S(2)}, u32[]{:S(2)}) %collective-permute-start.11) | collective-permute-done | bytes 524320 | tf_op jit(solution)/shard_map/ppermute | solution.py:591
  261.2 13.2 %collective-permute-done.10 = bf16[128,2048]{1,0:T(8,128)(2,1)S(1)} collective-permute-done((bf16[128,2048]{1,0:T(8,128)(2,1)}, bf16[128,2048]{1,0:T(8,128)(2,1)S(1)}, u32[]{:S(2)}, u32[]{:S(2)}) %collective-permute-start.10) | collective-permute-done | bytes 524320 | tf_op jit(solution)/shard_map/ppermute | solution.py:591
  274.4 6.7 collective-permute-done.12
  290.7 4.3 all-to-all-start.2
  300.1 4.0 collective-permute-start.13
  304.0 22.4 %collective-permute-done.14.refs_2_.refs_12_ = bf16[128,2048]{1,0:T(8,128)(2,1)} collective-permute-done((bf16[128,2048]{1,0:T(8,128)(2,1)}, bf16[128,2048]{1,0:T(8,128)(2,1)}, u32[]{:S(2)}, u32[]{:S(2)}) %collective-permute-start.14) | collective-permute-done | bytes 524320 | tf_op jit(solution)/shard_map/ppermute | solution.py:591
  330.5 9.6 %collective-permute-done.15.refs_3_.refs_13_ = bf16[128,2048]{1,0:T(8,128)(2,1)} collective-permute-done((bf16[128,2048]{1,0:T(8,128)(2,1)}, bf16[128,2048]{1,0:T(8,128)(2,1)}, u32[]{:S(2)}, u32[]{:S(2)}) %collective-permute-start.15) | collective-permute-done | bytes 524320 | tf_op jit(solution)/shard_map/ppermute | solution.py:591
  344.3 24.9 %feed_back.1 = (bf16[512,2048]{1,0:T(8,128)(2,1)}, bf16[512,2048]{1,0:T(8,128)(2,1)}, bf16[128,2048]{1,0:T(8,128)(2,1)}, bf16[128,2048]{1,0:T(8,128)(2,1)}, bf16...) custom-call(bf16[128,2048]{1,0:T(8,128)(2,1)} %fusion.23.refs_0_.refs_10_, ...), custom_call_target="tpu_custom_call" | custom-call | flops 12884901888 | bytes 1024 | tf_op jit(solution)/shard_map/feed_back/pallas_call | solution.py:516
  369.2 13.4 %feed_grads.2 = bf16[1024,6656]{1,0:T(8,128)(2,1)} custom-call(s32[1]{0:T(128)} %bitcast.32.par_ref, bf16[128,2048]{1,0:T(8,128)(2,1)} %copy-done.3, bf16[128,2048]{1,0:T(8,128)(2,1)} %collective-permute-done.7.refs_1_.refs_6_, bf16[128,2048]{1,0:T(8,128)(2,1)} %copy-done.4, bf16[128,2048]{1,0:T(8,128)(2,1)} %collective-permute-done.9.refs_3_.refs_8_, ...), custom_call_target="tpu_custom_call" | custom-call | flops 1024 | bytes 1024 | tf_op jit(solution)/shard_map/feed_grads/pallas_call | solution.py:574
  385.7 13.0 %collective-permute-done.19 = bf16[128,2048]{1,0:T(8,128)(2,1)S(1)} collective-permute-done((bf16[128,2048]{1,0:T(8,128)(2,1)}, bf16[128,2048]{1,0:T(8,128)(2,1)S(1)}, u32[]{:S(2)}, u32[]{:S(2)}) %collective-permute-start.19) | collective-permute-done | bytes 524320 | tf_op jit(solution)/shard_map/ppermute | solution.py:591
  403.8 17.0 %feed_grads.3 = bf16[1024,6656]{1,0:T(8,128)(2,1)} custom-call(s32[1]{0:T(128)} %bitcast.33.par_ref, bf16[128,2048]{1,0:T(8,128)(2,1)} %copy-done.3, bf16[128,2048]{1,0:T(8,128)(2,1)} %collective-permute-done.7.refs_1_.refs_6_, bf16[128,2048]{1,0:T(8,128)(2,1)} %copy-done.4, bf16[128,2048]{1,0:T(8,128)(2,1)} %collective-permute-done.9.refs_3_.refs_8_, ...), custom_call_target="tpu_custom_call" | custom-call | flops 1024 | bytes 1024 | tf_op jit(solution)/shard_map/feed_grads/pallas_call | solution.py:574
  420.8 3.5 collective-permute-done.20
  427.0 3.3 multiply_reduce_fusion.2
  438.3 15.8 %collective-permute-done.23.rest_2_.refs_4_ = bf16[128,2048]{1,0:T(8,128)(2,1)S(1)} collective-permute-done((bf16[128,2048]{1,0:T(8,128)(2,1)S(1)}, bf16[128,2048]{1,0:T(8,128)(2,1)S(1)}, u32[]{:S(2)}, u32[]{:S(2)}) %collective-permute-start.23) | collective-permute-done | bytes 524320 | tf_op jit(solution)/shard_map/ppermute | solution.py:591
  459.7 14.7 %collective-permute-done.22.rest_1_.refs_3_ = bf16[128,2048]{1,0:T(8,128)(2,1)} collective-permute-done((bf16[128,2048]{1,0:T(8,128)(2,1)S(1)}, bf16[128,2048]{1,0:T(8,128)(2,1)}, u32[]{:S(2)}, u32[]{:S(2)}) %collective-permute-start.22) | collective-permute-done | bytes 524320 | tf_op jit(solution)/shard_map/ppermute | solution.py:591
  474.4 7.6 %collective-permute-done.24.rest_3_.refs_5_ = bf16[128,2048]{1,0:T(8,128)(2,1)} collective-permute-done((bf16[128,2048]{1,0:T(8,128)(2,1)S(1)}, bf16[128,2048]{1,0:T(8,128)(2,1)}, u32[]{:S(2)}, u32[]{:S(2)}) %collective-permute-start.24) | collective-permute-done | bytes 524320 | tf_op jit(solution)/shard_map/ppermute | solution.py:591
  482.0 12.5 %attend_back.1 = (f32[512,512]{1,0:T(8,128)}, f32[512,512]{1,0:T(8,128)}, bf16[512,512]{1,0:T(8,128)(2,1)}) custom-call(bf16[512,512]{1,0:T(8,128)(2,1)} %get-tuple-element.98.q_ref, bf16[512,512]{1,0:T(8,128)(2,1)} %copy-done.34, bf16[512,512]{1,0:T(8,128)(2,1)} %get-tuple-element.99.o_ref, s32[1,512]{1,0:T(1,128)} %bitcast.131, s32[1,512]{1,0:T(1,128)} %bitcast.133, ...), custom_call_target="tpu_custom_call" | custom-call | flops 2684354560 | bytes 1024 | tf_op jit(solution)/shard_map/attend_back/pallas_call | solution.py:301
  499.3 9.0 %project_back.1 = (bf16[512,1024]{1,0:T(8,128)(2,1)}, f32[2,256]{1,0:T(2,128)}, bf16[128,2048]{1,0:T(8,128)(2,1)}, bf16[128,2048]{1,0:T(8,128)(2,1)}, bf16[128,2...) custom-call(f32[512,512]{1,0:T(8,128)} %get-tuple-element.152.dq_ref, f32[512,512]{1,0:T(8,128)} %get-tuple-element.153.o_ref, ...), custom_call_target="tpu_custom_call" | custom-call | flops 2147483648 | bytes 1024 | tf_op jit(solution)/shard_map/project_back/pallas_call | solution.py:393
  510.3 6.1 attention_grads.2
  516.4 12.6 %collective-permute-start.30 = (bf16[1024,1792]{1,0:T(8,128)(2,1)}, bf16[1024,1792]{1,0:T(8,128)(2,1)}, u32[]{:S(2)}, u32[]{:S(2)}) collective-permute-start(bf16[1024,1792]{1,0:T(8,128)(2,1)} %attention_grads.2), channel_id=1, source_target_pairs={{0,4},{4,0},{8,12},{12,8},{16,20},{20,16},{24,28},{28,24},{1,5},{5... | collective-permute-start | bytes 11010056 | tf_op jit(solution)/shard_map/ppermute | solution.py:591
  531.0 12.8 %collective-permute-done.28 = bf16[128,2048]{1,0:T(8,128)(2,1)S(1)} collective-permute-done((bf16[128,2048]{1,0:T(8,128)(2,1)S(1)}, bf16[128,2048]{1,0:T(8,128)(2,1)S(1)}, u32[]{:S(2)}, u32[]{:S(2)}) %collective-permute-start.28) | collective-permute-done | bytes 524320 | tf_op jit(solution)/shard_map/ppermute | solution.py:591
  546.4 17.9 %collective-permute-done.27 = bf16[128,2048]{1,0:T(8,128)(2,1)S(1)} collective-permute-done((bf16[128,2048]{1,0:T(8,128)(2,1)}, bf16[128,2048]{1,0:T(8,128)(2,1)S(1)}, u32[]{:S(2)}, u32[]{:S(2)}) %collective-permute-start.27) | collective-permute-done | bytes 524320 | tf_op jit(solution)/shard_map/ppermute | solution.py:591
  564.2 4.2 collective-permute-done.29
  568.5 7.2 %attention_grads.3 = bf16[1024,1792]{1,0:T(8,128)(2,1)} custom-call(s32[1]{0:T(128)} %bitcast.33.par_ref, bf16[512,2048]{1,0:T(8,128)(2,1)} %get-tuple-element.159.refs_0_, bf16[512,1024]{1,0:T(8,128)(2,1)} %get-tuple-element.160.refs_1_, bf16[128,2048]{1,0:T(8,128)(2,1)} %copy-done.14, bf16[128,2048]{1,0:T(8,128)(2,1)} %collective-permute-done.22.rest_1_.refs_3_, ...), custom_call_target="tpu_custom_call" | custom-call | flops 1024 | bytes 1024 | tf_op jit(solution)/shard_map/attention_grads/pallas_call | solution.py:574
  581.5 3.9 all-to-all-start.3
  587.1 8.1 %collective-permute-done.31 = bf16[256,512]{1,0:T(8,128)(2,1)S(1)} collective-permute-done((bf16[256,512]{1,0:T(8,128)(2,1)S(1)}, bf16[256,512]{1,0:T(8,128)(2,1)S(1)}, u32[]{:S(2)}, u32[]{:S(2)}) %collective-permute-start.31) | collective-permute-done | bytes 262176 | tf_op jit(solution)/shard_map/ppermute | solution.py:591
  598.4 12.3 %collective-permute-done.32 = bf16[256,512]{1,0:T(8,128)(2,1)S(1)} collective-permute-done((bf16[256,512]{1,0:T(8,128)(2,1)S(1)}, bf16[256,512]{1,0:T(8,128)(2,1)S(1)}, u32[]{:S(2)}, u32[]{:S(2)}) %collective-permute-start.32) | collective-permute-done | bytes 262176 | tf_op jit(solution)/shard_map/ppermute | solution.py:591
  611.6 6.2 all-to-all-done.3
  619.1 3.4 convolution_convert_fusion
  626.8 4.0 collective-permute-start.33
  630.8 12.9 %collective-permute-done.34 = bf16[136,2048]{1,0:T(8,128)(2,1)} collective-permute-done((bf16[136,2048]{1,0:T(8,128)(2,1)}, bf16[136,2048]{1,0:T(8,128)(2,1)}, u32[]{:S(2)}, u32[]{:S(2)}) %collective-permute-start.34) | collective-permute-done | bytes 557088 | tf_op jit(solution)/shard_map/ppermute | solution.py:591
  656.3 15.3 %collective-permute-done.36 = bf16[256,768]{1,0:T(8,128)(2,1)} collective-permute-done((bf16[256,768]{1,0:T(8,128)(2,1)}, bf16[256,768]{1,0:T(8,128)(2,1)}, u32[]{:S(2)}, u32[]{:S(2)}) %collective-permute-start.36) | collective-permute-done | bytes 393248 | tf_op jit(solution)/shard_map/ppermute | solution.py:591
  674.9 4.7 convolution_convert_fusion.5
  679.6 11.9 %collective-permute-done.37 = bf16[256,768]{1,0:T(8,128)(2,1)S(1)} collective-permute-done((bf16[256,768]{1,0:T(8,128)(2,1)S(1)}, bf16[256,768]{1,0:T(8,128)(2,1)S(1)}, u32[]{:S(2)}, u32[]{:S(2)}) %collective-permute-start.37) | collective-permute-done | bytes 393248 | tf_op jit(solution)/shard_map/ppermute | solution.py:591
  (373 shorter events, 154.4 us)
Async XLA Ops:
  7.2 71.2 %all-gather.4.cloned.1.call-start = ((), (), s32[]{:S(2)}) async-start(), calls=%async_computation.6 | async-start | bytes 8257536 | tf_op jit(solution)/shard_map/all_gather | solution.py:749
  14.1 197.3 %all-gather.6.cloned.1.call-start = ((), (), s32[]{:S(2)}) async-start(), calls=%async_computation.7 | async-start | bytes 28311552 | tf_op jit(solution)/shard_map/all_gather | solution.py:749
  24.7 27.4 %all-to-all-start = ((bf16[8,40,2048]{2,1,0:T(8,128)(2,1)}), bf16[8,40,2048]{2,1,0:T(8,128)(2,1)S(1)}, u32[]{:S(2)}, u32[]{:S(2)}) async-start(bf16[8,40,2048]{2,1,0:T(8,128)(2,1)} %bitcast.5), calls=%async_computation | async-start | bytes 2621440 | tf_op jit(solution)/shard_map/all_to_all | solution.py:756
  30.8 258.1 %copy-start.51 = (s32[128]{0:T(128)}, s32[128]{0:T(128)S(1)}, u32[]{:S(2)}) copy-start(s32[128]{0:T(128)S(1)} %multiply_add_fusion.9) | copy-start | bytes 1540
  52.7 23.4 %collective-permute-start.1 = (bf16[128,2048]{1,0:T(8,128)(2,1)S(1)}, bf16[128,2048]{1,0:T(8,128)(2,1)}, u32[]{:S(2)}, u32[]{:S(2)}) collective-permute-start(bf16[128,2048]{1,0:T(8,128)(2,1)S(1)} %get-tuple-element.324.refs_0_), channel_id=1, source_target_pairs={{0,2},{1,3},{2,0},{3,1},{4,6},{5,7},{6,4},{7,5},{8,10},{9,11},{10,... | collective-permute-start | bytes 1572872 | tf_op jit(solution)/shard_map/ppermute | solution.py:591
  57.0 26.7 %collective-permute-start = (bf16[128,2048]{1,0:T(8,128)(2,1)S(1)}, bf16[128,2048]{1,0:T(8,128)(2,1)}, u32[]{:S(2)}, u32[]{:S(2)}) collective-permute-start(bf16[128,2048]{1,0:T(8,128)(2,1)S(1)} %get-tuple-element.324.refs_0_), channel_id=1, source_target_pairs={{0,1},{1,0},{2,3},{3,2},{4,5},{5,4},{6,7},{7,6},{8,9},{9,8},{10,11... | collective-permute-start | bytes 1572872 | tf_op jit(solution)/shard_map/ppermute | solution.py:591
  76.0 13.2 %collective-permute-start.2 = (bf16[128,2048]{1,0:T(8,128)(2,1)}, bf16[128,2048]{1,0:T(8,128)(2,1)}, u32[]{:S(2)}, u32[]{:S(2)}) collective-permute-start(bf16[128,2048]{1,0:T(8,128)(2,1)} %collective-permute-done.1.refs_2_), channel_id=1, source_target_pairs={{0,1},{1,0},{2,3},{3,2},{4,5},{5,4},{6,7},{7,6},{8,9},{9,8},{10,11... | collective-permute-start | bytes 1572872 | tf_op jit(solution)/shard_map/ppermute | solution.py:591
  98.0 4.0 collective-permute-start.3
  112.9 9.5 %collective-permute-start.5 = (bf16[128,2048]{1,0:T(8,128)(2,1)}, bf16[128,2048]{1,0:T(8,128)(2,1)S(1)}, u32[]{:S(2)}, u32[]{:S(2)}) collective-permute-start(bf16[128,2048]{1,0:T(8,128)(2,1)} %get-tuple-element.103), channel_id=1, source_target_pairs={{0,1},{1,0},{2,3},{3,2},{4,5},{5,4},{6,7},{7,6},{8,9},{9,8},{10,11... | collective-permute-start | bytes 1572872 | tf_op jit(solution)/shard_map/ppermute | solution.py:591
  114.7 15.4 %collective-permute-start.4 = (bf16[128,2048]{1,0:T(8,128)(2,1)}, bf16[128,2048]{1,0:T(8,128)(2,1)S(1)}, u32[]{:S(2)}, u32[]{:S(2)}) collective-permute-start(bf16[128,2048]{1,0:T(8,128)(2,1)} %get-tuple-element.101), channel_id=1, source_target_pairs={{0,1},{1,0},{2,3},{3,2},{4,5},{5,4},{6,7},{7,6},{8,9},{9,8},{10,11... | collective-permute-start | bytes 1572872 | tf_op jit(solution)/shard_map/ppermute | solution.py:591
  123.6 16.4 %collective-permute-start.6 = (bf16[128,2048]{1,0:T(8,128)(2,1)S(1)}, bf16[128,2048]{1,0:T(8,128)(2,1)S(1)}, u32[]{:S(2)}, u32[]{:S(2)}) collective-permute-start(bf16[128,2048]{1,0:T(8,128)(2,1)S(1)} %add_convert_fusion.4), channel_id=1, source_target_pairs={{0,2},{1,3},{2,0},{3,1},{4,6},{5,7},{6,4},{7,5},{8,10},{9,11},{10,... | collective-permute-start | bytes 1572872 | tf_op jit(solution)/shard_map/ppermute | solution.py:591
  142.0 24.9 %collective-permute-start.8 = (bf16[128,2048]{1,0:T(8,128)(2,1)S(1)}, bf16[128,2048]{1,0:T(8,128)(2,1)S(1)}, u32[]{:S(2)}, u32[]{:S(2)}) collective-permute-start(bf16[128,2048]{1,0:T(8,128)(2,1)S(1)} %multiply_convert_fusion.refs_0_.refs_5_), channel_id=1, source_target_pairs={{0,2},{1,3},{2,0},{3,1},{4,6},{5,7},{6,4},{7,5},{8,10},{9,11},{10,... | collective-permute-start | bytes 1572872 | tf_op jit(solution)/shard_map/ppermute | solution.py:591
  142.0 76.0 %collective-permute-start.7 = (bf16[128,2048]{1,0:T(8,128)(2,1)S(1)}, bf16[128,2048]{1,0:T(8,128)(2,1)}, u32[]{:S(2)}, u32[]{:S(2)}) collective-permute-start(bf16[128,2048]{1,0:T(8,128)(2,1)S(1)} %multiply_convert_fusion.refs_0_.refs_5_), channel_id=1, source_target_pairs={{0,1},{1,0},{2,3},{3,2},{4,5},{5,4},{6,7},{7,6},{8,9},{9,8},{10,11... | collective-permute-start | bytes 1572872 | tf_op jit(solution)/shard_map/ppermute | solution.py:591
  166.8 51.3 %collective-permute-start.9 = (bf16[128,2048]{1,0:T(8,128)(2,1)S(1)}, bf16[128,2048]{1,0:T(8,128)(2,1)}, u32[]{:S(2)}, u32[]{:S(2)}) collective-permute-start(bf16[128,2048]{1,0:T(8,128)(2,1)S(1)} %collective-permute-done.8.refs_2_.refs_7_), channel_id=1, source_target_pairs={{0,1},{1,0},{2,3},{3,2},{4,5},{5,4},{6,7},{7,6},{8,9},{9,8},{10,11... | collective-permute-start | bytes 1572872 | tf_op jit(solution)/shard_map/ppermute | solution.py:591
  211.4 28.4 %all-to-all-start.1 = ((bf16[8,40,2304]{2,1,0:T(8,128)(2,1)}), bf16[8,40,2304]{2,1,0:T(8,128)(2,1)}, u32[]{:S(2)}, u32[]{:S(2)}) async-start(bf16[8,40,2304]{2,1,0:T(8,128)(2,1)} %bitcast.114), calls=%async_computation.1 | async-start | bytes 2949120 | tf_op jit(solution)/shard_map/all_to_all | solution.py:818
  215.7 66.5 %all-gather.8.cloned.1.call-start = ((), (), s32[]{:S(2)}) async-start(), calls=%async_computation.8 | async-start | bytes 2359296 | tf_op jit(solution)/shard_map/all_gather | solution.py:749
  239.8 15.0 %collective-permute-start.11 = (bf16[128,2048]{1,0:T(8,128)(2,1)}, bf16[128,2048]{1,0:T(8,128)(2,1)S(1)}, u32[]{:S(2)}, u32[]{:S(2)}) collective-permute-start(bf16[128,2048]{1,0:T(8,128)(2,1)} %get-tuple-element.114), channel_id=1, source_target_pairs={{0,1},{1,0},{2,3},{3,2},{4,5},{5,4},{6,7},{7,6},{8,9},{9,8},{10,11... | collective-permute-start | bytes 1572872 | tf_op jit(solution)/shard_map/ppermute | solution.py:591
  241.4 33.0 %collective-permute-start.10 = (bf16[128,2048]{1,0:T(8,128)(2,1)}, bf16[128,2048]{1,0:T(8,128)(2,1)S(1)}, u32[]{:S(2)}, u32[]{:S(2)}) collective-permute-start(bf16[128,2048]{1,0:T(8,128)(2,1)} %get-tuple-element.112), channel_id=1, source_target_pairs={{0,1},{1,0},{2,3},{3,2},{4,5},{5,4},{6,7},{7,6},{8,9},{9,8},{10,11... | collective-permute-start | bytes 1572872 | tf_op jit(solution)/shard_map/ppermute | solution.py:591
  256.0 25.0 %collective-permute-start.12 = (bf16[128,2048]{1,0:T(8,128)(2,1)S(1)}, bf16[128,2048]{1,0:T(8,128)(2,1)S(1)}, u32[]{:S(2)}, u32[]{:S(2)}) collective-permute-start(bf16[128,2048]{1,0:T(8,128)(2,1)S(1)} %add_convert_fusion.3), channel_id=1, source_target_pairs={{0,2},{1,3},{2,0},{3,1},{4,6},{5,7},{6,4},{7,5},{8,10},{9,11},{10,... | collective-permute-start | bytes 1572872 | tf_op jit(solution)/shard_map/ppermute | solution.py:591
  290.7 49.4 %all-to-all-start.2 = ((bf16[8,40,2304]{2,1,0:T(8,128)(2,1)}), bf16[8,40,2304]{2,1,0:T(8,128)(2,1)}, u32[]{:S(2)}, u32[]{:S(2)}) async-start(bf16[8,40,2304]{2,1,0:T(8,128)(2,1)} %bitcast.107), calls=%async_computation.2 | async-start | bytes 2949120 | tf_op jit(solution)/shard_map/all_to_all | solution.py:766
  295.0 280.7 %reduce-scatter.3.cloned.1.call-start = ((), (), s32[]{:S(2)}) async-start(), calls=%async_computation.9 | async-start | bytes 17039360 | tf_op jit(solution)/shard_map/reduce_scatter | solution.py:774
  299.8 26.7 %collective-permute-start.14 = (bf16[128,2048]{1,0:T(8,128)(2,1)}, bf16[128,2048]{1,0:T(8,128)(2,1)}, u32[]{:S(2)}, u32[]{:S(2)}) collective-permute-start(bf16[128,2048]{1,0:T(8,128)(2,1)} %fusion.23.refs_0_.refs_10_), channel_id=1, source_target_pairs={{0,2},{1,3},{2,0},{3,1},{4,6},{5,7},{6,4},{7,5},{8,10},{9,11},{10,... | collective-permute-start | bytes 1572872 | tf_op jit(solution)/shard_map/ppermute | solution.py:591
  300.1 30.4 %collective-permute-start.13 = (bf16[128,2048]{1,0:T(8,128)(2,1)}, bf16[128,2048]{1,0:T(8,128)(2,1)}, u32[]{:S(2)}, u32[]{:S(2)}) collective-permute-start(bf16[128,2048]{1,0:T(8,128)(2,1)} %fusion.23.refs_0_.refs_10_), channel_id=1, source_target_pairs={{0,1},{1,0},{2,3},{3,2},{4,5},{5,4},{6,7},{7,6},{8,9},{9,8},{10,11... | collective-permute-start | bytes 1572872 | tf_op jit(solution)/shard_map/ppermute | solution.py:591
  326.5 13.6 %collective-permute-start.15 = (bf16[128,2048]{1,0:T(8,128)(2,1)}, bf16[128,2048]{1,0:T(8,128)(2,1)}, u32[]{:S(2)}, u32[]{:S(2)}) collective-permute-start(bf16[128,2048]{1,0:T(8,128)(2,1)} %collective-permute-done.14.refs_2_.refs_12_), channel_id=1, source_target_pairs={{0,1},{1,0},{2,3},{3,2},{4,5},{5,4},{6,7},{7,6},{8,9},{9,8},{10,11... | collective-permute-start | bytes 1572872 | tf_op jit(solution)/shard_map/ppermute | solution.py:591
  342.0 40.7 %collective-permute-start.16 = (bf16[136,2304]{1,0:T(8,128)(2,1)S(1)}, bf16[136,2304]{1,0:T(8,128)(2,1)S(1)}, u32[]{:S(2)}, u32[]{:S(2)}) collective-permute-start(bf16[136,2304]{1,0:T(8,128)(2,1)S(1)} %convolution_convert_fusion.3), channel_id=1, source_target_pairs={{0,1},{1,0},{2,3},{3,2},{4,5},{5,4},{6,7},{7,6},{8,9},{9,8},{10,11... | collective-permute-start | bytes 1880072 | tf_op jit(solution)/shard_map/ppermute | solution.py:591
  342.3 40.4 %collective-permute-start.17 = (bf16[136,2304]{1,0:T(8,128)(2,1)S(1)}, bf16[136,2304]{1,0:T(8,128)(2,1)S(1)}, u32[]{:S(2)}, u32[]{:S(2)}) collective-permute-start(bf16[136,2304]{1,0:T(8,128)(2,1)S(1)} %convolution_convert_fusion.3), channel_id=1, source_target_pairs={{0,2},{1,3},{2,0},{3,1},{4,6},{5,7},{6,4},{7,5},{8,10},{9,11},{10,... | collective-permute-start | bytes 1880072 | tf_op jit(solution)/shard_map/ppermute | solution.py:591
  382.7 21.1 %collective-permute-start.21 = (bf16[1024,6656]{1,0:T(8,128)(2,1)}, bf16[1024,6656]{1,0:T(8,128)(2,1)}, u32[]{:S(2)}, u32[]{:S(2)}) collective-permute-start(bf16[1024,6656]{1,0:T(8,128)(2,1)} %feed_grads.2), channel_id=1, source_target_pairs={{0,4},{4,0},{8,12},{12,8},{16,20},{20,16},{24,28},{28,24},{1,5},{5... | collective-permute-start | bytes 40894472 | tf_op jit(solution)/shard_map/ppermute | solution.py:591
  383.7 15.1 %collective-permute-start.19 = (bf16[128,2048]{1,0:T(8,128)(2,1)}, bf16[128,2048]{1,0:T(8,128)(2,1)S(1)}, u32[]{:S(2)}, u32[]{:S(2)}) collective-permute-start(bf16[128,2048]{1,0:T(8,128)(2,1)} %get-tuple-element.142), channel_id=1, source_target_pairs={{0,1},{1,0},{2,3},{3,2},{4,5},{5,4},{6,7},{7,6},{8,9},{9,8},{10,11... | collective-permute-start | bytes 1572872 | tf_op jit(solution)/shard_map/ppermute | solution.py:591
  384.0 36.8 %collective-permute-start.18 = (bf16[128,2048]{1,0:T(8,128)(2,1)}, bf16[128,2048]{1,0:T(8,128)(2,1)S(1)}, u32[]{:S(2)}, u32[]{:S(2)}) collective-permute-start(bf16[128,2048]{1,0:T(8,128)(2,1)} %get-tuple-element.134), channel_id=1, source_target_pairs={{0,1},{1,0},{2,3},{3,2},{4,5},{5,4},{6,7},{7,6},{8,9},{9,8},{10,11... | collective-permute-start | bytes 1572872 | tf_op jit(solution)/shard_map/ppermute | solution.py:591
  400.7 23.5 %collective-permute-start.20 = (bf16[128,2048]{1,0:T(8,128)(2,1)}, bf16[128,2048]{1,0:T(8,128)(2,1)}, u32[]{:S(2)}, u32[]{:S(2)}) collective-permute-start(bf16[128,2048]{1,0:T(8,128)(2,1)} %add_convert_fusion.1), channel_id=1, source_target_pairs={{0,2},{1,3},{2,0},{3,1},{4,6},{5,7},{6,4},{7,5},{8,10},{9,11},{10,... | collective-permute-start | bytes 1572872 | tf_op jit(solution)/shard_map/ppermute | solution.py:591
  424.3 219.3 %reduce-scatter.5.cloned.1.call-start = ((), (), s32[]{:S(2)}) async-start(), calls=%async_computation.10 | async-start | bytes 4587520 | tf_op jit(solution)/shard_map/reduce_scatter | solution.py:774
  431.0 23.2 %collective-permute-start.23 = (bf16[128,2048]{1,0:T(8,128)(2,1)S(1)}, bf16[128,2048]{1,0:T(8,128)(2,1)S(1)}, u32[]{:S(2)}, u32[]{:S(2)}) collective-permute-start(bf16[128,2048]{1,0:T(8,128)(2,1)S(1)} %get-tuple-element.292.rest_0_.refs_2_), channel_id=1, source_target_pairs={{0,2},{1,3},{2,0},{3,1},{4,6},{5,7},{6,4},{7,5},{8,10},{9,11},{10,... | collective-permute-start | bytes 1572872 | tf_op jit(solution)/shard_map/ppermute | solution.py:591
  434.0 62.1 %collective-permute-start.25 = (bf16[136,2304]{1,0:T(8,128)(2,1)}, bf16[136,2304]{1,0:T(8,128)(2,1)}, u32[]{:S(2)}, u32[]{:S(2)}) collective-permute-start(bf16[136,2304]{1,0:T(8,128)(2,1)} %copy-done.74), channel_id=1, source_target_pairs={{0,1},{1,0},{2,3},{3,2},{4,5},{5,4},{6,7},{7,6},{8,9},{9,8},{10,11... | collective-permute-start | bytes 1880072 | tf_op jit(solution)/shard_map/ppermute | solution.py:591
  436.6 37.7 %collective-permute-start.22 = (bf16[128,2048]{1,0:T(8,128)(2,1)S(1)}, bf16[128,2048]{1,0:T(8,128)(2,1)}, u32[]{:S(2)}, u32[]{:S(2)}) collective-permute-start(bf16[128,2048]{1,0:T(8,128)(2,1)S(1)} %get-tuple-element.292.rest_0_.refs_2_), channel_id=1, source_target_pairs={{0,1},{1,0},{2,3},{3,2},{4,5},{5,4},{6,7},{7,6},{8,9},{9,8},{10,11... | collective-permute-start | bytes 1572872 | tf_op jit(solution)/shard_map/ppermute | solution.py:591
  454.2 27.8 %collective-permute-start.24 = (bf16[128,2048]{1,0:T(8,128)(2,1)S(1)}, bf16[128,2048]{1,0:T(8,128)(2,1)}, u32[]{:S(2)}, u32[]{:S(2)}) collective-permute-start(bf16[128,2048]{1,0:T(8,128)(2,1)S(1)} %collective-permute-done.23.rest_2_.refs_4_), channel_id=1, source_target_pairs={{0,1},{1,0},{2,3},{3,2},{4,5},{5,4},{6,7},{7,6},{8,9},{9,8},{10,11... | collective-permute-start | bytes 1572872 | tf_op jit(solution)/shard_map/ppermute | solution.py:591
  494.5 4.0 collective-permute-start.26
  516.4 52.1 %collective-permute-start.30 = (bf16[1024,1792]{1,0:T(8,128)(2,1)}, bf16[1024,1792]{1,0:T(8,128)(2,1)}, u32[]{:S(2)}, u32[]{:S(2)}) collective-permute-start(bf16[1024,1792]{1,0:T(8,128)(2,1)} %attention_grads.2), channel_id=1, source_target_pairs={{0,4},{4,0},{8,12},{12,8},{16,20},{20,16},{24,28},{28,24},{1,5},{5... | collective-permute-start | bytes 11010056 | tf_op jit(solution)/shard_map/ppermute | solution.py:591
  529.0 14.8 %collective-permute-start.28 = (bf16[128,2048]{1,0:T(8,128)(2,1)S(1)}, bf16[128,2048]{1,0:T(8,128)(2,1)S(1)}, u32[]{:S(2)}, u32[]{:S(2)}) collective-permute-start(bf16[128,2048]{1,0:T(8,128)(2,1)S(1)} %copy-done.75), channel_id=1, source_target_pairs={{0,1},{1,0},{2,3},{3,2},{4,5},{5,4},{6,7},{7,6},{8,9},{9,8},{10,11... | collective-permute-start | bytes 1572872 | tf_op jit(solution)/shard_map/ppermute | solution.py:591
  530.5 33.8 %collective-permute-start.27 = (bf16[128,2048]{1,0:T(8,128)(2,1)}, bf16[128,2048]{1,0:T(8,128)(2,1)S(1)}, u32[]{:S(2)}, u32[]{:S(2)}) collective-permute-start(bf16[128,2048]{1,0:T(8,128)(2,1)} %get-tuple-element.157), channel_id=1, source_target_pairs={{0,1},{1,0},{2,3},{3,2},{4,5},{5,4},{6,7},{7,6},{8,9},{9,8},{10,11... | collective-permute-start | bytes 1572872 | tf_op jit(solution)/shard_map/ppermute | solution.py:591
  543.9 24.5 %collective-permute-start.29 = (bf16[128,2048]{1,0:T(8,128)(2,1)S(1)}, bf16[128,2048]{1,0:T(8,128)(2,1)S(1)}, u32[]{:S(2)}, u32[]{:S(2)}) collective-permute-start(bf16[128,2048]{1,0:T(8,128)(2,1)S(1)} %add_convert_fusion), channel_id=1, source_target_pairs={{0,2},{1,3},{2,0},{3,1},{4,6},{5,7},{6,4},{7,5},{8,10},{9,11},{10,... | collective-permute-start | bytes 1572872 | tf_op jit(solution)/shard_map/ppermute | solution.py:591
  581.5 36.3 %all-to-all-start.3 = ((bf16[8,40,2048]{2,1,0:T(8,128)(2,1)}), bf16[8,40,2048]{2,1,0:T(8,128)(2,1)S(1)}, u32[]{:S(2)}, u32[]{:S(2)}) async-start(bf16[8,40,2048]{2,1,0:T(8,128)(2,1)} %bitcast.110), calls=%async_computation.3 | async-start | bytes 2621440 | tf_op jit(solution)/shard_map/all_to_all | solution.py:931
  586.4 8.7 %collective-permute-start.31 = (bf16[256,512]{1,0:T(8,128)(2,1)S(1)}, bf16[256,512]{1,0:T(8,128)(2,1)S(1)}, u32[]{:S(2)}, u32[]{:S(2)}) collective-permute-start(bf16[256,512]{1,0:T(8,128)(2,1)S(1)} %slice.198), channel_id=1, source_target_pairs={{0,1},{1,0},{2,3},{3,2},{4,5},{5,4},{6,7},{7,6},{8,9},{9,8},{10,11... | collective-permute-start | bytes 786440 | tf_op jit(solution)/shard_map/ppermute | solution.py:591
  596.2 14.5 %collective-permute-start.32 = (bf16[256,512]{1,0:T(8,128)(2,1)S(1)}, bf16[256,512]{1,0:T(8,128)(2,1)S(1)}, u32[]{:S(2)}, u32[]{:S(2)}) collective-permute-start(bf16[256,512]{1,0:T(8,128)(2,1)S(1)} %add_convert_fusion.6), channel_id=1, source_target_pairs={{0,2},{1,3},{2,0},{3,1},{4,6},{5,7},{6,4},{7,5},{8,10},{9,11},{10,... | collective-permute-start | bytes 786440 | tf_op jit(solution)/shard_map/ppermute | solution.py:591
  619.1 24.5 %collective-permute-start.34 = (bf16[136,2048]{1,0:T(8,128)(2,1)}, bf16[136,2048]{1,0:T(8,128)(2,1)}, u32[]{:S(2)}, u32[]{:S(2)}) collective-permute-start(bf16[136,2048]{1,0:T(8,128)(2,1)} %fusion.8), channel_id=1, source_target_pairs={{0,2},{1,3},{2,0},{3,1},{4,6},{5,7},{6,4},{7,5},{8,10},{9,11},{10,... | collective-permute-start | bytes 1671176 | tf_op jit(solution)/shard_map/ppermute | solution.py:591
  626.8 46.0 %collective-permute-start.33 = (bf16[136,2048]{1,0:T(8,128)(2,1)}, bf16[136,2048]{1,0:T(8,128)(2,1)}, u32[]{:S(2)}, u32[]{:S(2)}) collective-permute-start(bf16[136,2048]{1,0:T(8,128)(2,1)} %fusion.8), channel_id=1, source_target_pairs={{0,1},{1,0},{2,3},{3,2},{4,5},{5,4},{6,7},{7,6},{8,9},{9,8},{10,11... | collective-permute-start | bytes 1671176 | tf_op jit(solution)/shard_map/ppermute | solution.py:591
  643.6 29.1 %collective-permute-start.35 = (bf16[136,2048]{1,0:T(8,128)(2,1)}, bf16[136,2048]{1,0:T(8,128)(2,1)}, u32[]{:S(2)}, u32[]{:S(2)}) collective-permute-start(bf16[136,2048]{1,0:T(8,128)(2,1)} %collective-permute-done.34), channel_id=1, source_target_pairs={{0,1},{1,0},{2,3},{3,2},{4,5},{5,4},{6,7},{7,6},{8,9},{9,8},{10,11... | collective-permute-start | bytes 1671176 | tf_op jit(solution)/shard_map/ppermute | solution.py:591
  647.6 24.0 %collective-permute-start.36 = (bf16[256,768]{1,0:T(8,128)(2,1)}, bf16[256,768]{1,0:T(8,128)(2,1)}, u32[]{:S(2)}, u32[]{:S(2)}) collective-permute-start(bf16[256,768]{1,0:T(8,128)(2,1)} %pad_maximum_fusion.4), channel_id=1, source_target_pairs={{0,1},{1,0},{2,3},{3,2},{4,5},{5,4},{6,7},{7,6},{8,9},{9,8},{10,11... | collective-permute-start | bytes 1179656 | tf_op jit(solution)/shard_map/ppermute | solution.py:591
  674.5 17.0 %collective-permute-start.37 = (bf16[256,768]{1,0:T(8,128)(2,1)S(1)}, bf16[256,768]{1,0:T(8,128)(2,1)S(1)}, u32[]{:S(2)}, u32[]{:S(2)}) collective-permute-start(bf16[256,768]{1,0:T(8,128)(2,1)S(1)} %add_convert_fusion.5), channel_id=1, source_target_pairs={{0,2},{1,3},{2,0},{3,1},{4,6},{5,7},{6,4},{7,5},{8,10},{9,11},{10,... | collective-permute-start | bytes 1179656 | tf_op jit(solution)/shard_map/ppermute | solution.py:591
  (76 other events, 1227.3 us)
Sparse Core Ops, SparseCore 0:
  14.2 64.1 all-gather.3
  80.9 130.5 all-gather.5
  219.0 32.7 all-gather.7
  424.4 132.9 reduce-scatter.2
  575.8 62.7 reduce-scatter.4

commit v5 on v4

--- a/solution.py
+++ b/solution.py
@@ -915,9 +915,9 @@
             *where,
         )
 
-    in_parts, at_leaving = beside_first(in_parts, grads_leaving(at_grads_of))
     in_pieces = fold_start(in_parts, "tensor")
-    in_pieces, at_come = with_work(in_pieces, grads_come(at_leaving))
+    at_leaving = grads_leaving(at_grads_of)
+    in_pieces, at_leaving = with_work(in_pieces, at_leaving)
     in_attn = summed(in_pieces)
     normal_grad = in_attn + against(low_rank_grad, wl) + shared
     _, back_in = jax.vjp(normed, inputs, gains_f[0])
@@ -929,15 +929,15 @@
     )
     sent_two = across(receiver, input_grad.astype(bf16)) + extra.reshape(-1, width)
     come_two = lax.all_to_all(sent_two.astype(bf16), "dp", 0, 0, tiled=True)
-    at_grads = grads_staying(at_grads_of, at_come)
-    at_grads, s_ff = with_work(at_grads, s_ff)
-    s_at = scattered(at_grads)
     early = s_ff[:, 3 * units :]
     bit = 1
     while bit < parts:
         early = summed([early, crossed(early, "tensor", bit)])
         early = early.astype(bf16) if 2 * bit < parts else early
         bit *= 2
+    at_grads = grads_staying(at_grads_of, grads_come(at_leaving))
+    at_grads, (s_ff, come_two) = with_work(at_grads, (s_ff, come_two))
+    s_at = scattered(at_grads)
     come_two, early = with_work(come_two, early)
     g0_part = jnp.sum(come_two.reshape(devices, -1, width)[:, -1, :block].astype(f32), axis=0)
     home_two = product(compact, come_two) + jnp.pad(

time: 711 us -> 710 us (level)
  waiting for transfers between devices: 351 us -> 332 us
  starting transfers between devices: 80.2 us -> 91.4 us
    ppermute x36, waiting for transfers between devices: 278 us -> 252 us  [crossed(): return lax.ppermute(piece, axis, [(i, i ^ bit) for i in range(length)])]
    all_to_all x1, starting transfers between devices: 3.86 us -> 14.6 us  [body(): come_two = lax.all_to_all(sent_two.astype(bf16), 'dp', 0, 0, tiled=True)]
    unnamed x166 -> x162, local copies, waits for them, and re-layouts: 15.7 us -> 15.8 us
where the time goes in v5:
time: 710 us; the launch traced here: 697 us
  waiting for transfers between devices  332 us (47%)
  Pallas kernels  131 us (18%)
  starting transfers between devices  91.4 us (13%)
  other arithmetic  47.4 us (7%)
  matrix products  40.6 us (6%)
  local copies, waits for them, and re-layouts  38.9 us (5%)
  between operations  15.6 us (2%)
    ppermute x36, waiting for transfers between devices, crossed(): return lax.ppermute(piece, axis, [(i, i ^ bit) for i in range(length)])  252 us
    ppermute x36, starting transfers between devices, crossed(): return lax.ppermute(piece, axis, [(i, i ^ bit) for i in range(length)])  59.2 us
    pallas_call x4, Pallas kernels, column_grads(): pl.pallas_call(kernel, out_shape=jax.ShapeDtypeStruct((width // every, to...  44 us
    all_gather x3, waiting for transfers between devices, gather_columns(): lax.all_gather(jnp.concatenate(pieces, axis=1), 'dp', axis=0, tiled=True)  43.7 us
    pallas_call x1, Pallas kernels, feed_back(): pl.pallas_call(kernel, out_shape=[jax.ShapeDtypeStruct((tok, units), bf16...  25 us
    dot_general x12, matrix products, product(): return jnp.dot(left_mat, right_mat, preferred_element_type=f32).astype(kind)  23.6 us
    pallas_call x1, Pallas kernels, feed_forward(): pl.pallas_call(kernel, out_shape=[jax.ShapeDtypeStruct((tok, units), bf16...  21.7 us
    all_to_all x1, waiting for transfers between devices, body(): come_in = lax.all_to_all(packed_in, 'dp', 0, 0, tiled=True)  21.2 us
  transfers between devices with their start and end apart: 47, of which 29 were waited for; matrix products, arithmetic and copies ran while one was open for 14% of the time, Pallas kernels for 19%

profile of v5, /device:TPU:0, one launch (start us, length us, event | category | flops | bytes accessed | tf_op | source)
XLA Modules:
  0.0 696.5 jit_solution(15204400147360157906)
XLA Ops:
  24.7 5.2 all-to-all-start
  30.8 21.2 %all-to-all-done = bf16[8,40,2048]{2,1,0:T(8,128)(2,1)S(1)} async-done(((bf16[8,40,2048]{2,1,0:T(8,128)(2,1)}), bf16[8,40,2048]{2,1,0:T(8,128)(2,1)S(1)}, u32[]{:S(2)}, u32[]{:S(2)}) %all-to-all-start) | async-done | bytes 1310752 | tf_op jit(solution)/shard_map/all_to_all | solution.py:756
  58.5 17.6 %collective-permute-done.1.refs_2_ = bf16[128,2048]{1,0:T(8,128)(2,1)} collective-permute-done((bf16[128,2048]{1,0:T(8,128)(2,1)S(1)}, bf16[128,2048]{1,0:T(8,128)(2,1)}, u32[]{:S(2)}, u32[]{:S(2)}) %collective-permute-start.1) | collective-permute-done | bytes 524320 | tf_op jit(solution)/shard_map/ppermute | solution.py:591
  83.7 5.5 collective-permute-done.2.refs_3_
  89.2 8.8 %project.1 = (bf16[512,2048]{1,0:T(8,128)(2,1)}, f32[512,1024]{1,0:T(8,128)}, bf16[512,512]{1,0:T(8,128)(2,1)}, bf16[512,512]{1,0:T(8,128)(2,1)}) custom-call(bf16[128,2048]{1,0:T(8,128)(2,1)} %copy-done.5, bf16[128,2048]{1,0:T(8,128)(2,1)} %collective-permute-done.refs_1_, bf16[128,2048]{1,0:T(8,128)(2,1)} %collective-permute-done.1.refs_2_, ...), custom_call_target="tpu_custom_call" | custom-call | flops 2147483648 | bytes 1024 | tf_op jit(solution)/shard_map/project/pallas_call | solution.py:153
  102.8 10.1 %attend.1 = (bf16[512,512]{1,0:T(8,128)(2,1)}, bf16[128,2048]{1,0:T(8,128)(2,1)}, bf16[128,2048]{1,0:T(8,128)(2,1)}, bf16[128,2048]{1,0:T(8,128)(2,1)}, bf16[128,2048]{1,0:T(8,128)(2,1)}) custom-call(bf16[512,512]{1,0:T(8,128)(2,1)} %get-tuple-element.97.q_ref, bf16[512,512]{1,0:T(8,128)(2,1)} %copy-done.34, bf16[512,512]{1,0:T(8,128)(2,1)} %get-tuple-element.98.o_ref, ...), custom_call_target="tpu_custom_call" | custom-call | flops 1073741824 | bytes 1024 | tf_op jit(solution)/shard_map/attend/pallas_call | solution.py:217
  115.1 7.3 %collective-permute-done.5 = bf16[128,2048]{1,0:T(8,128)(2,1)S(1)} collective-permute-done((bf16[128,2048]{1,0:T(8,128)(2,1)}, bf16[128,2048]{1,0:T(8,128)(2,1)S(1)}, u32[]{:S(2)}, u32[]{:S(2)}) %collective-permute-start.5) | collective-permute-done | bytes 524320 | tf_op jit(solution)/shard_map/ppermute | solution.py:591
  123.6 3.5 collective-permute-start.6
  130.1 9.8 %collective-permute-done.6 = bf16[128,2048]{1,0:T(8,128)(2,1)S(1)} collective-permute-done((bf16[128,2048]{1,0:T(8,128)(2,1)S(1)}, bf16[128,2048]{1,0:T(8,128)(2,1)S(1)}, u32[]{:S(2)}, u32[]{:S(2)}) %collective-permute-start.6) | collective-permute-done | bytes 524320 | tf_op jit(solution)/shard_map/ppermute | solution.py:591
  142.0 4.4 collective-permute-start.7
  146.4 20.4 %collective-permute-done.8.refs_2_.refs_7_ = bf16[128,2048]{1,0:T(8,128)(2,1)S(1)} collective-permute-done((bf16[128,2048]{1,0:T(8,128)(2,1)S(1)}, bf16[128,2048]{1,0:T(8,128)(2,1)S(1)}, u32[]{:S(2)}, u32[]{:S(2)}) %collective-permute-start.8) | collective-permute-done | bytes 524320 | tf_op jit(solution)/shard_map/ppermute | solution.py:591
  169.5 41.9 %all-gather.6.cloned.1.call-done.refs_4_.refs_5_.refs_6_ = bf16[2048,6144]{1,0:T(8,128)(2,1)} async-done(((bf16[256,6144]{1,0:T(8,128)(2,1)}), bf16[2048,6144]{1,0:T(8,128)(2,1)}) %all-gather.6.cloned.1.call-update) | async-done | bytes 25165840 | tf_op jit(solution)/shard_map/all_gather | solution.py:749
  211.4 4.3 all-to-all-start.1
  218.1 21.7 %feed_forward.1 = (bf16[512,2048]{1,0:T(8,128)(2,1)}, bf16[512,2048]{1,0:T(8,128)(2,1)}, bf16[512,2048]{1,0:T(8,128)(2,1)}, bf16[128,2048]{1,0:T(8,128)(2,1)}, b...) custom-call(bf16[128,2048]{1,0:T(8,128)(2,1)} %copy-done.3, ...), custom_call_target="tpu_custom_call" | custom-call | flops 12884901888 | bytes 1024 | tf_op jit(solution)/shard_map/feed_forward/pallas_call | solution.py:460
  241.9 12.9 %collective-permute-done.11 = bf16[128,2048]{1,0:T(8,128)(2,1)S(1)} collective-permute-done((bf16[128,2048]{1,0:T(8,128)(2,1)}, bf16[128,2048]{1,0:T(8,128)(2,1)S(1)}, u32[]{:S(2)}, u32[]{:S(2)}) %collective-permute-start.11) | collective-permute-done | bytes 524320 | tf_op jit(solution)/shard_map/ppermute | solution.py:591
  261.2 13.2 %collective-permute-done.10 = bf16[128,2048]{1,0:T(8,128)(2,1)S(1)} collective-permute-done((bf16[128,2048]{1,0:T(8,128)(2,1)}, bf16[128,2048]{1,0:T(8,128)(2,1)S(1)}, u32[]{:S(2)}, u32[]{:S(2)}) %collective-permute-start.10) | collective-permute-done | bytes 524320 | tf_op jit(solution)/shard_map/ppermute | solution.py:591
  274.3 6.7 collective-permute-done.12
  290.6 4.3 all-to-all-start.2
  295.2 3.3 multiply_reduce_fusion
  300.0 3.9 collective-permute-start.13
  304.0 22.5 %collective-permute-done.14.refs_2_.refs_12_ = bf16[128,2048]{1,0:T(8,128)(2,1)} collective-permute-done((bf16[128,2048]{1,0:T(8,128)(2,1)}, bf16[128,2048]{1,0:T(8,128)(2,1)}, u32[]{:S(2)}, u32[]{:S(2)}) %collective-permute-start.14) | collective-permute-done | bytes 524320 | tf_op jit(solution)/shard_map/ppermute | solution.py:591
  330.4 9.6 %collective-permute-done.15.refs_3_.refs_13_ = bf16[128,2048]{1,0:T(8,128)(2,1)} collective-permute-done((bf16[128,2048]{1,0:T(8,128)(2,1)}, bf16[128,2048]{1,0:T(8,128)(2,1)}, u32[]{:S(2)}, u32[]{:S(2)}) %collective-permute-start.15) | collective-permute-done | bytes 524320 | tf_op jit(solution)/shard_map/ppermute | solution.py:591
  344.2 25.0 %feed_back.1 = (bf16[512,2048]{1,0:T(8,128)(2,1)}, bf16[512,2048]{1,0:T(8,128)(2,1)}, bf16[128,2048]{1,0:T(8,128)(2,1)}, bf16[128,2048]{1,0:T(8,128)(2,1)}, bf16...) custom-call(bf16[128,2048]{1,0:T(8,128)(2,1)} %fusion.23.refs_0_.refs_10_, ...), custom_call_target="tpu_custom_call" | custom-call | flops 12884901888 | bytes 1024 | tf_op jit(solution)/shard_map/feed_back/pallas_call | solution.py:516
  369.2 13.4 %feed_grads.2 = bf16[1024,6656]{1,0:T(8,128)(2,1)} custom-call(s32[1]{0:T(128)} %bitcast.32.par_ref, bf16[128,2048]{1,0:T(8,128)(2,1)} %copy-done.3, bf16[128,2048]{1,0:T(8,128)(2,1)} %collective-permute-done.7.refs_1_.refs_6_, bf16[128,2048]{1,0:T(8,128)(2,1)} %copy-done.4, bf16[128,2048]{1,0:T(8,128)(2,1)} %collective-permute-done.9.refs_3_.refs_8_, ...), custom_call_target="tpu_custom_call" | custom-call | flops 1024 | bytes 1024 | tf_op jit(solution)/shard_map/feed_grads/pallas_call | solution.py:574
  385.7 13.0 %collective-permute-done.19 = bf16[128,2048]{1,0:T(8,128)(2,1)S(1)} collective-permute-done((bf16[128,2048]{1,0:T(8,128)(2,1)}, bf16[128,2048]{1,0:T(8,128)(2,1)S(1)}, u32[]{:S(2)}, u32[]{:S(2)}) %collective-permute-start.19) | collective-permute-done | bytes 524320 | tf_op jit(solution)/shard_map/ppermute | solution.py:591
  403.7 17.1 %feed_grads.3 = bf16[1024,6656]{1,0:T(8,128)(2,1)} custom-call(s32[1]{0:T(128)} %bitcast.33.par_ref, bf16[128,2048]{1,0:T(8,128)(2,1)} %copy-done.3, bf16[128,2048]{1,0:T(8,128)(2,1)} %collective-permute-done.7.refs_1_.refs_6_, bf16[128,2048]{1,0:T(8,128)(2,1)} %copy-done.4, bf16[128,2048]{1,0:T(8,128)(2,1)} %collective-permute-done.9.refs_3_.refs_8_, ...), custom_call_target="tpu_custom_call" | custom-call | flops 1024 | bytes 1024 | tf_op jit(solution)/shard_map/feed_grads/pallas_call | solution.py:574
  420.9 3.3 collective-permute-done.20
  426.7 3.3 multiply_reduce_fusion.2
  438.0 16.3 %collective-permute-done.23.rest_2_.refs_4_ = bf16[128,2048]{1,0:T(8,128)(2,1)S(1)} collective-permute-done((bf16[128,2048]{1,0:T(8,128)(2,1)S(1)}, bf16[128,2048]{1,0:T(8,128)(2,1)S(1)}, u32[]{:S(2)}, u32[]{:S(2)}) %collective-permute-start.23) | collective-permute-done | bytes 524320 | tf_op jit(solution)/shard_map/ppermute | solution.py:591
  459.9 14.2 %collective-permute-done.22.rest_1_.refs_3_ = bf16[128,2048]{1,0:T(8,128)(2,1)} collective-permute-done((bf16[128,2048]{1,0:T(8,128)(2,1)S(1)}, bf16[128,2048]{1,0:T(8,128)(2,1)}, u32[]{:S(2)}, u32[]{:S(2)}) %collective-permute-start.22) | collective-permute-done | bytes 524320 | tf_op jit(solution)/shard_map/ppermute | solution.py:591
  474.1 8.1 %collective-permute-done.24.rest_3_.refs_5_ = bf16[128,2048]{1,0:T(8,128)(2,1)} collective-permute-done((bf16[128,2048]{1,0:T(8,128)(2,1)S(1)}, bf16[128,2048]{1,0:T(8,128)(2,1)}, u32[]{:S(2)}, u32[]{:S(2)}) %collective-permute-start.24) | collective-permute-done | bytes 524320 | tf_op jit(solution)/shard_map/ppermute | solution.py:591
  482.2 12.5 %attend_back.1 = (f32[512,512]{1,0:T(8,128)}, f32[512,512]{1,0:T(8,128)}, bf16[512,512]{1,0:T(8,128)(2,1)}) custom-call(bf16[512,512]{1,0:T(8,128)(2,1)} %get-tuple-element.97.q_ref, bf16[512,512]{1,0:T(8,128)(2,1)} %copy-done.34, bf16[512,512]{1,0:T(8,128)(2,1)} %get-tuple-element.98.o_ref, s32[1,512]{1,0:T(1,128)} %bitcast.131, s32[1,512]{1,0:T(1,128)} %bitcast.133, ...), custom_call_target="tpu_custom_call" | custom-call | flops 2684354560 | bytes 1024 | tf_op jit(solution)/shard_map/attend_back/pallas_call | solution.py:301
  499.5 9.0 %project_back.1 = (bf16[512,1024]{1,0:T(8,128)(2,1)}, f32[2,256]{1,0:T(2,128)}, bf16[128,2048]{1,0:T(8,128)(2,1)}, bf16[128,2048]{1,0:T(8,128)(2,1)}, bf16[128,2...) custom-call(f32[512,512]{1,0:T(8,128)} %get-tuple-element.152.dq_ref, f32[512,512]{1,0:T(8,128)} %get-tuple-element.153.o_ref, ...), custom_call_target="tpu_custom_call" | custom-call | flops 2147483648 | bytes 1024 | tf_op jit(solution)/shard_map/project_back/pallas_call | solution.py:393
  511.3 6.7 collective-permute-done.28
  521.5 6.2 attention_grads.2
  527.7 8.0 %collective-permute-done.29 = bf16[128,2048]{1,0:T(8,128)(2,1)} collective-permute-done((bf16[128,2048]{1,0:T(8,128)(2,1)}, bf16[128,2048]{1,0:T(8,128)(2,1)}, u32[]{:S(2)}, u32[]{:S(2)}) %collective-permute-start.29) | collective-permute-done | bytes 524320 | tf_op jit(solution)/shard_map/ppermute | solution.py:591
  535.7 15.5 %collective-permute-start.30 = (bf16[1024,1792]{1,0:T(8,128)(2,1)}, bf16[1024,1792]{1,0:T(8,128)(2,1)}, u32[]{:S(2)}, u32[]{:S(2)}) collective-permute-start(bf16[1024,1792]{1,0:T(8,128)(2,1)} %attention_grads.2), channel_id=1, source_target_pairs={{0,4},{4,0},{8,12},{12,8},{16,20},{20,16},{24,28},{28,24},{1,5},{5... | collective-permute-start | bytes 11010056 | tf_op jit(solution)/shard_map/ppermute | solution.py:591
  556.9 14.6 %all-to-all-start.3 = ((bf16[8,40,2048]{2,1,0:T(8,128)(2,1)}), bf16[8,40,2048]{2,1,0:T(8,128)(2,1)S(1)}, u32[]{:S(2)}, u32[]{:S(2)}) async-start(bf16[8,40,2048]{2,1,0:T(8,128)(2,1)} %bitcast.110), calls=%async_computation.4 | async-start | bytes 2621440 | tf_op jit(solution)/shard_map/all_to_all | solution.py:931
  571.6 7.3 %attention_grads.3 = bf16[1024,1792]{1,0:T(8,128)(2,1)} custom-call(s32[1]{0:T(128)} %bitcast.33.par_ref, bf16[512,2048]{1,0:T(8,128)(2,1)} %get-tuple-element.151.refs_0_, bf16[512,1024]{1,0:T(8,128)(2,1)} %get-tuple-element.156.refs_1_, bf16[128,2048]{1,0:T(8,128)(2,1)} %copy-done.14, bf16[128,2048]{1,0:T(8,128)(2,1)} %collective-permute-done.22.rest_1_.refs_3_, ...), custom_call_target="tpu_custom_call" | custom-call | flops 1024 | bytes 1024 | tf_op jit(solution)/shard_map/attention_grads/pallas_call | solution.py:574
  578.9 10.9 %all-to-all-done.3 = bf16[8,40,2048]{2,1,0:T(8,128)(2,1)S(1)} async-done(((bf16[8,40,2048]{2,1,0:T(8,128)(2,1)}), bf16[8,40,2048]{2,1,0:T(8,128)(2,1)S(1)}, u32[]{:S(2)}, u32[]{:S(2)}) %all-to-all-start.3) | async-done | bytes 1310752 | tf_op jit(solution)/shard_map/all_to_all | solution.py:931
  591.9 5.4 collective-permute-done.31
  600.8 8.3 %collective-permute-done.32 = bf16[256,512]{1,0:T(8,128)(2,1)S(1)} collective-permute-done((bf16[256,512]{1,0:T(8,128)(2,1)S(1)}, bf16[256,512]{1,0:T(8,128)(2,1)S(1)}, u32[]{:S(2)}, u32[]{:S(2)}) %collective-permute-start.32) | collective-permute-done | bytes 262176 | tf_op jit(solution)/shard_map/ppermute | solution.py:591
  611.2 3.1 convolution_convert_fusion
  618.6 4.0 collective-permute-start.33
  622.7 14.1 %collective-permute-done.34 = bf16[136,2048]{1,0:T(8,128)(2,1)} collective-permute-done((bf16[136,2048]{1,0:T(8,128)(2,1)}, bf16[136,2048]{1,0:T(8,128)(2,1)}, u32[]{:S(2)}, u32[]{:S(2)}) %collective-permute-start.34) | collective-permute-done | bytes 557088 | tf_op jit(solution)/shard_map/ppermute | solution.py:591
  650.3 14.3 %collective-permute-done.36 = bf16[256,768]{1,0:T(8,128)(2,1)} collective-permute-done((bf16[256,768]{1,0:T(8,128)(2,1)}, bf16[256,768]{1,0:T(8,128)(2,1)}, u32[]{:S(2)}, u32[]{:S(2)}) %collective-permute-start.36) | collective-permute-done | bytes 393248 | tf_op jit(solution)/shard_map/ppermute | solution.py:591
  668.1 4.7 convolution_convert_fusion.5
  672.8 12.3 %collective-permute-done.37 = bf16[256,768]{1,0:T(8,128)(2,1)S(1)} collective-permute-done((bf16[256,768]{1,0:T(8,128)(2,1)S(1)}, bf16[256,768]{1,0:T(8,128)(2,1)S(1)}, u32[]{:S(2)}, u32[]{:S(2)}) %collective-permute-start.37) | collective-permute-done | bytes 393248 | tf_op jit(solution)/shard_map/ppermute | solution.py:591
  (369 shorter events, 152.3 us)
Async XLA Ops:
  7.2 71.2 %all-gather.4.cloned.1.call-start = ((), (), s32[]{:S(2)}) async-start(), calls=%async_computation.6 | async-start | bytes 8257536 | tf_op jit(solution)/shard_map/all_gather | solution.py:749
  14.1 197.3 %all-gather.6.cloned.1.call-start = ((), (), s32[]{:S(2)}) async-start(), calls=%async_computation.7 | async-start | bytes 28311552 | tf_op jit(solution)/shard_map/all_gather | solution.py:749
  24.7 27.4 %all-to-all-start = ((bf16[8,40,2048]{2,1,0:T(8,128)(2,1)}), bf16[8,40,2048]{2,1,0:T(8,128)(2,1)S(1)}, u32[]{:S(2)}, u32[]{:S(2)}) async-start(bf16[8,40,2048]{2,1,0:T(8,128)(2,1)} %bitcast.5), calls=%async_computation | async-start | bytes 2621440 | tf_op jit(solution)/shard_map/all_to_all | solution.py:756
  30.8 258.0 %copy-start.49 = (s32[128]{0:T(128)}, s32[128]{0:T(128)S(1)}, u32[]{:S(2)}) copy-start(s32[128]{0:T(128)S(1)} %multiply_add_fusion.9) | copy-start | bytes 1540
  52.7 23.4 %collective-permute-start.1 = (bf16[128,2048]{1,0:T(8,128)(2,1)S(1)}, bf16[128,2048]{1,0:T(8,128)(2,1)}, u32[]{:S(2)}, u32[]{:S(2)}) collective-permute-start(bf16[128,2048]{1,0:T(8,128)(2,1)S(1)} %get-tuple-element.322.refs_0_), channel_id=1, source_target_pairs={{0,2},{1,3},{2,0},{3,1},{4,6},{5,7},{6,4},{7,5},{8,10},{9,11},{10,... | collective-permute-start | bytes 1572872 | tf_op jit(solution)/shard_map/ppermute | solution.py:591
  57.0 26.7 %collective-permute-start = (bf16[128,2048]{1,0:T(8,128)(2,1)S(1)}, bf16[128,2048]{1,0:T(8,128)(2,1)}, u32[]{:S(2)}, u32[]{:S(2)}) collective-permute-start(bf16[128,2048]{1,0:T(8,128)(2,1)S(1)} %get-tuple-element.322.refs_0_), channel_id=1, source_target_pairs={{0,1},{1,0},{2,3},{3,2},{4,5},{5,4},{6,7},{7,6},{8,9},{9,8},{10,11... | collective-permute-start | bytes 1572872 | tf_op jit(solution)/shard_map/ppermute | solution.py:591
  76.0 13.2 %collective-permute-start.2 = (bf16[128,2048]{1,0:T(8,128)(2,1)}, bf16[128,2048]{1,0:T(8,128)(2,1)}, u32[]{:S(2)}, u32[]{:S(2)}) collective-permute-start(bf16[128,2048]{1,0:T(8,128)(2,1)} %collective-permute-done.1.refs_2_), channel_id=1, source_target_pairs={{0,1},{1,0},{2,3},{3,2},{4,5},{5,4},{6,7},{7,6},{8,9},{9,8},{10,11... | collective-permute-start | bytes 1572872 | tf_op jit(solution)/shard_map/ppermute | solution.py:591
  98.0 4.0 collective-permute-start.3
  112.9 9.5 %collective-permute-start.5 = (bf16[128,2048]{1,0:T(8,128)(2,1)}, bf16[128,2048]{1,0:T(8,128)(2,1)S(1)}, u32[]{:S(2)}, u32[]{:S(2)}) collective-permute-start(bf16[128,2048]{1,0:T(8,128)(2,1)} %get-tuple-element.102), channel_id=1, source_target_pairs={{0,1},{1,0},{2,3},{3,2},{4,5},{5,4},{6,7},{7,6},{8,9},{9,8},{10,11... | collective-permute-start | bytes 1572872 | tf_op jit(solution)/shard_map/ppermute | solution.py:591
  114.7 15.4 %collective-permute-start.4 = (bf16[128,2048]{1,0:T(8,128)(2,1)}, bf16[128,2048]{1,0:T(8,128)(2,1)S(1)}, u32[]{:S(2)}, u32[]{:S(2)}) collective-permute-start(bf16[128,2048]{1,0:T(8,128)(2,1)} %get-tuple-element.100), channel_id=1, source_target_pairs={{0,1},{1,0},{2,3},{3,2},{4,5},{5,4},{6,7},{7,6},{8,9},{9,8},{10,11... | collective-permute-start | bytes 1572872 | tf_op jit(solution)/shard_map/ppermute | solution.py:591
  123.6 16.4 %collective-permute-start.6 = (bf16[128,2048]{1,0:T(8,128)(2,1)S(1)}, bf16[128,2048]{1,0:T(8,128)(2,1)S(1)}, u32[]{:S(2)}, u32[]{:S(2)}) collective-permute-start(bf16[128,2048]{1,0:T(8,128)(2,1)S(1)} %add_convert_fusion.4), channel_id=1, source_target_pairs={{0,2},{1,3},{2,0},{3,1},{4,6},{5,7},{6,4},{7,5},{8,10},{9,11},{10,... | collective-permute-start | bytes 1572872 | tf_op jit(solution)/shard_map/ppermute | solution.py:591
  141.9 24.9 %collective-permute-start.8 = (bf16[128,2048]{1,0:T(8,128)(2,1)S(1)}, bf16[128,2048]{1,0:T(8,128)(2,1)S(1)}, u32[]{:S(2)}, u32[]{:S(2)}) collective-permute-start(bf16[128,2048]{1,0:T(8,128)(2,1)S(1)} %multiply_convert_fusion.refs_0_.refs_5_), channel_id=1, source_target_pairs={{0,2},{1,3},{2,0},{3,1},{4,6},{5,7},{6,4},{7,5},{8,10},{9,11},{10,... | collective-permute-start | bytes 1572872 | tf_op jit(solution)/shard_map/ppermute | solution.py:591
  142.0 76.0 %collective-permute-start.7 = (bf16[128,2048]{1,0:T(8,128)(2,1)S(1)}, bf16[128,2048]{1,0:T(8,128)(2,1)}, u32[]{:S(2)}, u32[]{:S(2)}) collective-permute-start(bf16[128,2048]{1,0:T(8,128)(2,1)S(1)} %multiply_convert_fusion.refs_0_.refs_5_), channel_id=1, source_target_pairs={{0,1},{1,0},{2,3},{3,2},{4,5},{5,4},{6,7},{7,6},{8,9},{9,8},{10,11... | collective-permute-start | bytes 1572872 | tf_op jit(solution)/shard_map/ppermute | solution.py:591
  166.8 51.3 %collective-permute-start.9 = (bf16[128,2048]{1,0:T(8,128)(2,1)S(1)}, bf16[128,2048]{1,0:T(8,128)(2,1)}, u32[]{:S(2)}, u32[]{:S(2)}) collective-permute-start(bf16[128,2048]{1,0:T(8,128)(2,1)S(1)} %collective-permute-done.8.refs_2_.refs_7_), channel_id=1, source_target_pairs={{0,1},{1,0},{2,3},{3,2},{4,5},{5,4},{6,7},{7,6},{8,9},{9,8},{10,11... | collective-permute-start | bytes 1572872 | tf_op jit(solution)/shard_map/ppermute | solution.py:591
  211.4 28.4 %all-to-all-start.1 = ((bf16[8,40,2304]{2,1,0:T(8,128)(2,1)}), bf16[8,40,2304]{2,1,0:T(8,128)(2,1)}, u32[]{:S(2)}, u32[]{:S(2)}) async-start(bf16[8,40,2304]{2,1,0:T(8,128)(2,1)} %bitcast.114), calls=%async_computation.1 | async-start | bytes 2949120 | tf_op jit(solution)/shard_map/all_to_all | solution.py:818
  215.7 66.5 %all-gather.8.cloned.1.call-start = ((), (), s32[]{:S(2)}) async-start(), calls=%async_computation.8 | async-start | bytes 2359296 | tf_op jit(solution)/shard_map/all_gather | solution.py:749
  239.8 15.0 %collective-permute-start.11 = (bf16[128,2048]{1,0:T(8,128)(2,1)}, bf16[128,2048]{1,0:T(8,128)(2,1)S(1)}, u32[]{:S(2)}, u32[]{:S(2)}) collective-permute-start(bf16[128,2048]{1,0:T(8,128)(2,1)} %get-tuple-element.113), channel_id=1, source_target_pairs={{0,1},{1,0},{2,3},{3,2},{4,5},{5,4},{6,7},{7,6},{8,9},{9,8},{10,11... | collective-permute-start | bytes 1572872 | tf_op jit(solution)/shard_map/ppermute | solution.py:591
  241.4 33.0 %collective-permute-start.10 = (bf16[128,2048]{1,0:T(8,128)(2,1)}, bf16[128,2048]{1,0:T(8,128)(2,1)S(1)}, u32[]{:S(2)}, u32[]{:S(2)}) collective-permute-start(bf16[128,2048]{1,0:T(8,128)(2,1)} %get-tuple-element.111), channel_id=1, source_target_pairs={{0,1},{1,0},{2,3},{3,2},{4,5},{5,4},{6,7},{7,6},{8,9},{9,8},{10,11... | collective-permute-start | bytes 1572872 | tf_op jit(solution)/shard_map/ppermute | solution.py:591
  256.0 25.0 %collective-permute-start.12 = (bf16[128,2048]{1,0:T(8,128)(2,1)S(1)}, bf16[128,2048]{1,0:T(8,128)(2,1)S(1)}, u32[]{:S(2)}, u32[]{:S(2)}) collective-permute-start(bf16[128,2048]{1,0:T(8,128)(2,1)S(1)} %add_convert_fusion.3), channel_id=1, source_target_pairs={{0,2},{1,3},{2,0},{3,1},{4,6},{5,7},{6,4},{7,5},{8,10},{9,11},{10,... | collective-permute-start | bytes 1572872 | tf_op jit(solution)/shard_map/ppermute | solution.py:591
  290.6 49.4 %all-to-all-start.2 = ((bf16[8,40,2304]{2,1,0:T(8,128)(2,1)}), bf16[8,40,2304]{2,1,0:T(8,128)(2,1)}, u32[]{:S(2)}, u32[]{:S(2)}) async-start(bf16[8,40,2304]{2,1,0:T(8,128)(2,1)} %bitcast.107), calls=%async_computation.2 | async-start | bytes 2949120 | tf_op jit(solution)/shard_map/all_to_all | solution.py:766
  294.9 294.8 %reduce-scatter.3.cloned.1.call-start = ((), (), s32[]{:S(2)}) async-start(), calls=%async_computation.9 | async-start | bytes 17039360 | tf_op jit(solution)/shard_map/reduce_scatter | solution.py:774
  299.7 26.7 %collective-permute-start.14 = (bf16[128,2048]{1,0:T(8,128)(2,1)}, bf16[128,2048]{1,0:T(8,128)(2,1)}, u32[]{:S(2)}, u32[]{:S(2)}) collective-permute-start(bf16[128,2048]{1,0:T(8,128)(2,1)} %fusion.23.refs_0_.refs_10_), channel_id=1, source_target_pairs={{0,2},{1,3},{2,0},{3,1},{4,6},{5,7},{6,4},{7,5},{8,10},{9,11},{10,... | collective-permute-start | bytes 1572872 | tf_op jit(solution)/shard_map/ppermute | solution.py:591
  300.0 30.4 %collective-permute-start.13 = (bf16[128,2048]{1,0:T(8,128)(2,1)}, bf16[128,2048]{1,0:T(8,128)(2,1)}, u32[]{:S(2)}, u32[]{:S(2)}) collective-permute-start(bf16[128,2048]{1,0:T(8,128)(2,1)} %fusion.23.refs_0_.refs_10_), channel_id=1, source_target_pairs={{0,1},{1,0},{2,3},{3,2},{4,5},{5,4},{6,7},{7,6},{8,9},{9,8},{10,11... | collective-permute-start | bytes 1572872 | tf_op jit(solution)/shard_map/ppermute | solution.py:591
  326.4 13.6 %collective-permute-start.15 = (bf16[128,2048]{1,0:T(8,128)(2,1)}, bf16[128,2048]{1,0:T(8,128)(2,1)}, u32[]{:S(2)}, u32[]{:S(2)}) collective-permute-start(bf16[128,2048]{1,0:T(8,128)(2,1)} %collective-permute-done.14.refs_2_.refs_12_), channel_id=1, source_target_pairs={{0,1},{1,0},{2,3},{3,2},{4,5},{5,4},{6,7},{7,6},{8,9},{9,8},{10,11... | collective-permute-start | bytes 1572872 | tf_op jit(solution)/shard_map/ppermute | solution.py:591
  341.9 40.7 %collective-permute-start.16 = (bf16[136,2304]{1,0:T(8,128)(2,1)S(1)}, bf16[136,2304]{1,0:T(8,128)(2,1)S(1)}, u32[]{:S(2)}, u32[]{:S(2)}) collective-permute-start(bf16[136,2304]{1,0:T(8,128)(2,1)S(1)} %convolution_convert_fusion.3), channel_id=1, source_target_pairs={{0,1},{1,0},{2,3},{3,2},{4,5},{5,4},{6,7},{7,6},{8,9},{9,8},{10,11... | collective-permute-start | bytes 1880072 | tf_op jit(solution)/shard_map/ppermute | solution.py:591
  342.3 40.4 %collective-permute-start.17 = (bf16[136,2304]{1,0:T(8,128)(2,1)S(1)}, bf16[136,2304]{1,0:T(8,128)(2,1)S(1)}, u32[]{:S(2)}, u32[]{:S(2)}) collective-permute-start(bf16[136,2304]{1,0:T(8,128)(2,1)S(1)} %convolution_convert_fusion.3), channel_id=1, source_target_pairs={{0,2},{1,3},{2,0},{3,1},{4,6},{5,7},{6,4},{7,5},{8,10},{9,11},{10,... | collective-permute-start | bytes 1880072 | tf_op jit(solution)/shard_map/ppermute | solution.py:591
  382.7 21.1 %collective-permute-start.21 = (bf16[1024,6656]{1,0:T(8,128)(2,1)}, bf16[1024,6656]{1,0:T(8,128)(2,1)}, u32[]{:S(2)}, u32[]{:S(2)}) collective-permute-start(bf16[1024,6656]{1,0:T(8,128)(2,1)} %feed_grads.2), channel_id=1, source_target_pairs={{0,4},{4,0},{8,12},{12,8},{16,20},{20,16},{24,28},{28,24},{1,5},{5... | collective-permute-start | bytes 40894472 | tf_op jit(solution)/shard_map/ppermute | solution.py:591
  383.7 15.1 %collective-permute-start.19 = (bf16[128,2048]{1,0:T(8,128)(2,1)}, bf16[128,2048]{1,0:T(8,128)(2,1)S(1)}, u32[]{:S(2)}, u32[]{:S(2)}) collective-permute-start(bf16[128,2048]{1,0:T(8,128)(2,1)} %get-tuple-element.141), channel_id=1, source_target_pairs={{0,1},{1,0},{2,3},{3,2},{4,5},{5,4},{6,7},{7,6},{8,9},{9,8},{10,11... | collective-permute-start | bytes 1572872 | tf_op jit(solution)/shard_map/ppermute | solution.py:591
  384.0 36.9 %collective-permute-start.18 = (bf16[128,2048]{1,0:T(8,128)(2,1)}, bf16[128,2048]{1,0:T(8,128)(2,1)S(1)}, u32[]{:S(2)}, u32[]{:S(2)}) collective-permute-start(bf16[128,2048]{1,0:T(8,128)(2,1)} %get-tuple-element.133), channel_id=1, source_target_pairs={{0,1},{1,0},{2,3},{3,2},{4,5},{5,4},{6,7},{7,6},{8,9},{9,8},{10,11... | collective-permute-start | bytes 1572872 | tf_op jit(solution)/shard_map/ppermute | solution.py:591
  400.7 23.5 %collective-permute-start.20 = (bf16[128,2048]{1,0:T(8,128)(2,1)}, bf16[128,2048]{1,0:T(8,128)(2,1)}, u32[]{:S(2)}, u32[]{:S(2)}) collective-permute-start(bf16[128,2048]{1,0:T(8,128)(2,1)} %add_convert_fusion.1), channel_id=1, source_target_pairs={{0,2},{1,3},{2,0},{3,1},{4,6},{5,7},{6,4},{7,5},{8,10},{9,11},{10,... | collective-permute-start | bytes 1572872 | tf_op jit(solution)/shard_map/ppermute | solution.py:591
  430.7 23.6 %collective-permute-start.23 = (bf16[128,2048]{1,0:T(8,128)(2,1)S(1)}, bf16[128,2048]{1,0:T(8,128)(2,1)S(1)}, u32[]{:S(2)}, u32[]{:S(2)}) collective-permute-start(bf16[128,2048]{1,0:T(8,128)(2,1)S(1)} %get-tuple-element.290.rest_0_.refs_2_), channel_id=1, source_target_pairs={{0,2},{1,3},{2,0},{3,1},{4,6},{5,7},{6,4},{7,5},{8,10},{9,11},{10,... | collective-permute-start | bytes 1572872 | tf_op jit(solution)/shard_map/ppermute | solution.py:591
  433.7 62.3 %collective-permute-start.25 = (bf16[136,2304]{1,0:T(8,128)(2,1)}, bf16[136,2304]{1,0:T(8,128)(2,1)}, u32[]{:S(2)}, u32[]{:S(2)}) collective-permute-start(bf16[136,2304]{1,0:T(8,128)(2,1)} %copy-done.72), channel_id=1, source_target_pairs={{0,1},{1,0},{2,3},{3,2},{4,5},{5,4},{6,7},{7,6},{8,9},{9,8},{10,11... | collective-permute-start | bytes 1880072 | tf_op jit(solution)/shard_map/ppermute | solution.py:591
  436.3 37.7 %collective-permute-start.22 = (bf16[128,2048]{1,0:T(8,128)(2,1)S(1)}, bf16[128,2048]{1,0:T(8,128)(2,1)}, u32[]{:S(2)}, u32[]{:S(2)}) collective-permute-start(bf16[128,2048]{1,0:T(8,128)(2,1)S(1)} %get-tuple-element.290.rest_0_.refs_2_), channel_id=1, source_target_pairs={{0,1},{1,0},{2,3},{3,2},{4,5},{5,4},{6,7},{7,6},{8,9},{9,8},{10,11... | collective-permute-start | bytes 1572872 | tf_op jit(solution)/shard_map/ppermute | solution.py:591
  454.3 27.9 %collective-permute-start.24 = (bf16[128,2048]{1,0:T(8,128)(2,1)S(1)}, bf16[128,2048]{1,0:T(8,128)(2,1)}, u32[]{:S(2)}, u32[]{:S(2)}) collective-permute-start(bf16[128,2048]{1,0:T(8,128)(2,1)S(1)} %collective-permute-done.23.rest_2_.refs_4_), channel_id=1, source_target_pairs={{0,1},{1,0},{2,3},{3,2},{4,5},{5,4},{6,7},{7,6},{8,9},{9,8},{10,11... | collective-permute-start | bytes 1572872 | tf_op jit(solution)/shard_map/ppermute | solution.py:591
  494.7 4.0 collective-permute-start.26
  508.5 9.5 %collective-permute-start.28 = (bf16[128,2048]{1,0:T(8,128)(2,1)}, bf16[128,2048]{1,0:T(8,128)(2,1)S(1)}, u32[]{:S(2)}, u32[]{:S(2)}) collective-permute-start(bf16[128,2048]{1,0:T(8,128)(2,1)} %get-tuple-element.164), channel_id=1, source_target_pairs={{0,1},{1,0},{2,3},{3,2},{4,5},{5,4},{6,7},{7,6},{8,9},{9,8},{10,11... | collective-permute-start | bytes 1572872 | tf_op jit(solution)/shard_map/ppermute | solution.py:591
  509.3 18.4 %collective-permute-start.27 = (bf16[128,2048]{1,0:T(8,128)(2,1)}, bf16[128,2048]{1,0:T(8,128)(2,1)S(1)}, u32[]{:S(2)}, u32[]{:S(2)}) collective-permute-start(bf16[128,2048]{1,0:T(8,128)(2,1)} %get-tuple-element.162), channel_id=1, source_target_pairs={{0,1},{1,0},{2,3},{3,2},{4,5},{5,4},{6,7},{7,6},{8,9},{9,8},{10,11... | collective-permute-start | bytes 1572872 | tf_op jit(solution)/shard_map/ppermute | solution.py:591
  520.0 15.7 %collective-permute-start.29 = (bf16[128,2048]{1,0:T(8,128)(2,1)}, bf16[128,2048]{1,0:T(8,128)(2,1)}, u32[]{:S(2)}, u32[]{:S(2)}) collective-permute-start(bf16[128,2048]{1,0:T(8,128)(2,1)} %add_convert_fusion), channel_id=1, source_target_pairs={{0,2},{1,3},{2,0},{3,1},{4,6},{5,7},{6,4},{7,5},{8,10},{9,11},{10,... | collective-permute-start | bytes 1572872 | tf_op jit(solution)/shard_map/ppermute | solution.py:591
  535.7 35.9 %collective-permute-start.30 = (bf16[1024,1792]{1,0:T(8,128)(2,1)}, bf16[1024,1792]{1,0:T(8,128)(2,1)}, u32[]{:S(2)}, u32[]{:S(2)}) collective-permute-start(bf16[1024,1792]{1,0:T(8,128)(2,1)} %attention_grads.2), channel_id=1, source_target_pairs={{0,4},{4,0},{8,12},{12,8},{16,20},{20,16},{24,28},{28,24},{1,5},{5... | collective-permute-start | bytes 11010056 | tf_op jit(solution)/shard_map/ppermute | solution.py:591
  556.9 32.8 %all-to-all-start.3 = ((bf16[8,40,2048]{2,1,0:T(8,128)(2,1)}), bf16[8,40,2048]{2,1,0:T(8,128)(2,1)S(1)}, u32[]{:S(2)}, u32[]{:S(2)}) async-start(bf16[8,40,2048]{2,1,0:T(8,128)(2,1)} %bitcast.110), calls=%async_computation.4 | async-start | bytes 2621440 | tf_op jit(solution)/shard_map/all_to_all | solution.py:931
  571.5 66.7 %reduce-scatter.5.cloned.1.call-start = ((), (), s32[]{:S(2)}) async-start(), calls=%async_computation.10 | async-start | bytes 4587520 | tf_op jit(solution)/shard_map/reduce_scatter | solution.py:774
  590.9 6.4 collective-permute-start.31
  598.3 10.7 %collective-permute-start.32 = (bf16[256,512]{1,0:T(8,128)(2,1)S(1)}, bf16[256,512]{1,0:T(8,128)(2,1)S(1)}, u32[]{:S(2)}, u32[]{:S(2)}) collective-permute-start(bf16[256,512]{1,0:T(8,128)(2,1)S(1)} %add_convert_fusion.6), channel_id=1, source_target_pairs={{0,2},{1,3},{2,0},{3,1},{4,6},{5,7},{6,4},{7,5},{8,10},{9,11},{10,... | collective-permute-start | bytes 786440 | tf_op jit(solution)/shard_map/ppermute | solution.py:591
  611.2 25.6 %collective-permute-start.34 = (bf16[136,2048]{1,0:T(8,128)(2,1)}, bf16[136,2048]{1,0:T(8,128)(2,1)}, u32[]{:S(2)}, u32[]{:S(2)}) collective-permute-start(bf16[136,2048]{1,0:T(8,128)(2,1)} %fusion.8), channel_id=1, source_target_pairs={{0,2},{1,3},{2,0},{3,1},{4,6},{5,7},{6,4},{7,5},{8,10},{9,11},{10,... | collective-permute-start | bytes 1671176 | tf_op jit(solution)/shard_map/ppermute | solution.py:591
  618.6 47.1 %collective-permute-start.33 = (bf16[136,2048]{1,0:T(8,128)(2,1)}, bf16[136,2048]{1,0:T(8,128)(2,1)}, u32[]{:S(2)}, u32[]{:S(2)}) collective-permute-start(bf16[136,2048]{1,0:T(8,128)(2,1)} %fusion.8), channel_id=1, source_target_pairs={{0,1},{1,0},{2,3},{3,2},{4,5},{5,4},{6,7},{7,6},{8,9},{9,8},{10,11... | collective-permute-start | bytes 1671176 | tf_op jit(solution)/shard_map/ppermute | solution.py:591
  636.8 29.0 %collective-permute-start.35 = (bf16[136,2048]{1,0:T(8,128)(2,1)}, bf16[136,2048]{1,0:T(8,128)(2,1)}, u32[]{:S(2)}, u32[]{:S(2)}) collective-permute-start(bf16[136,2048]{1,0:T(8,128)(2,1)} %collective-permute-done.34), channel_id=1, source_target_pairs={{0,1},{1,0},{2,3},{3,2},{4,5},{5,4},{6,7},{7,6},{8,9},{9,8},{10,11... | collective-permute-start | bytes 1671176 | tf_op jit(solution)/shard_map/ppermute | solution.py:591
  642.2 22.5 %collective-permute-start.36 = (bf16[256,768]{1,0:T(8,128)(2,1)}, bf16[256,768]{1,0:T(8,128)(2,1)}, u32[]{:S(2)}, u32[]{:S(2)}) collective-permute-start(bf16[256,768]{1,0:T(8,128)(2,1)} %pad_maximum_fusion.4), channel_id=1, source_target_pairs={{0,1},{1,0},{2,3},{3,2},{4,5},{5,4},{6,7},{7,6},{8,9},{9,8},{10,11... | collective-permute-start | bytes 1179656 | tf_op jit(solution)/shard_map/ppermute | solution.py:591
  667.5 17.7 %collective-permute-start.37 = (bf16[256,768]{1,0:T(8,128)(2,1)S(1)}, bf16[256,768]{1,0:T(8,128)(2,1)S(1)}, u32[]{:S(2)}, u32[]{:S(2)}) collective-permute-start(bf16[256,768]{1,0:T(8,128)(2,1)S(1)} %add_convert_fusion.5), channel_id=1, source_target_pairs={{0,2},{1,3},{2,0},{3,1},{4,6},{5,7},{6,4},{7,5},{8,10},{9,11},{10,... | collective-permute-start | bytes 1179656 | tf_op jit(solution)/shard_map/ppermute | solution.py:591
  (74 other events, 1196.0 us)
Sparse Core Ops, SparseCore 0:
  14.2 64.1 all-gather.3
  80.9 130.5 all-gather.5
  219.0 32.7 all-gather.7
  424.4 132.8 reduce-scatter.2
  589.9 48.2 reduce-scatter.4
